TPU v7x, 32 devices: a whole 2x2x4 slice. The times are simulated.
32 devices in a mesh: blk: 8 (over z, y), grp: 4 (over x, core).
Axes of the slice: x: 2, y: 2, z: 4, core: 2. Of those that a mesh axis runs over, the one named last changes fastest.
Arguments:
- embeddings: bfloat16 [4, 4096, 1024], P('grp', 'blk'), may hold values from -12 to 12
- strata: int32 [4, 4096], P('grp', 'blk'), may hold values from 0 to 127, as said below
- centroids: bfloat16 [4, 128, 1024], P('grp', 'blk'), may hold values from -12 to 12
Outputs:
- probs: float32 [4, 4096], P('grp', 'blk')
Inputs may be any that keep to these rules, and one draw needn't show every extreme that they name: `strata`: within each aligned run of 512 rows of a collection the stratum ids never fall; within each range of 16 consecutive ids the smallest are about four times as common as the largest. `strata`: in each aligned run of 512 rows, at most 128 rows have ids in one range k * 16 to (k + 1) * 16 - 1, and exactly 128 in some range.
All inputs are finite; a program needn't handle non-finite values.
Results may differ from a plain program's by a relative error of at most 0.0014.
Values may be sent and summed in bfloat16 or wider, within the bound.
No kernel may reach another device: no remote copies, remote signals or barrier semaphores. Data moves between devices by JAX's collectives and lax.ppermute only.
A program may use at most 64 MiB of HBM per device.

v0:
```python
import math

import jax
import jax.numpy as jnp
from jax import lax
from jax.sharding import PartitionSpec as P

sharpness_divisor = 0.25
base_term = 0.05
epsilon = 1e-06


def unit_rows(matrix):
    values = matrix.astype(jnp.float32)
    scaling = lax.rsqrt(jnp.mean(values * values, axis=-1, keepdims=True) + epsilon) / math.sqrt(
        matrix.shape[-1]
    )
    return (values * scaling).astype(jnp.bfloat16)


def dense_sums(query_rows, query_ids, key_rows, key_ids):
    logit_entries = lax.dot_general(
        query_rows, key_rows, (((1,), (1,)), ((), ())), preferred_element_type=jnp.float32
    )
    similarity_grid = jnp.where(
        query_ids[:, None] == key_ids[None, :],
        jnp.exp((logit_entries - 1.0) / sharpness_divisor),
        jnp.zeros_like(logit_entries),
    )
    return (jnp.sum(similarity_grid, axis=1), jnp.sum(similarity_grid, axis=0))


def pair_sums(query_rows, query_ids, key_rows, key_ids):
    return dense_sums(query_rows, query_ids, key_rows, key_ids)


def body(embeddings, strata, centroids):
    own_units = unit_rows(embeddings[0])
    own_ids = strata[0]
    row_count = own_units.shape[0]
    cent_local = unit_rows(centroids[0])
    cent_units = lax.all_gather(cent_local, "blk", axis=0, tiled=True)
    strata_count = cent_units.shape[0]
    selector = (own_ids[:, None] == lax.broadcasted_iota(jnp.int32, (1, strata_count), 1)).astype(
        jnp.bfloat16
    )
    picked = jnp.dot(selector, cent_units, preferred_element_type=jnp.float32)
    distance = 1.0 - jnp.sum(own_units.astype(jnp.float32) * picked, axis=-1)
    guest_rows = lax.all_gather(own_units, "blk", axis=0, tiled=True)
    guest_ids = lax.all_gather(own_ids, "blk", axis=0, tiled=True)
    row_sums, column_sums = pair_sums(own_units, own_ids, guest_rows, guest_ids)
    weights = (distance + base_term) / row_sums
    total = lax.psum(jnp.sum(weights), ("blk", "grp"))
    row_total = float(row_count * lax.axis_size("blk") * lax.axis_size("grp"))
    return (weights * (row_total / total))[None, :]


def solution(mesh):
    placed = (P("grp", "blk", None), P("grp", "blk"), P("grp", "blk", None))
    return jax.shard_map(
        body, mesh=mesh, in_specs=placed, out_specs=P("grp", "blk"), check_vma=False
    )
```

profile of v0, /device:TPU:0, one launch (start us, length us, event | category | flops | bytes accessed | tf_op | source)
XLA Modules:
  0.0 197.1 jit_solution(4007569216989032687)
XLA Ops:
  6.5 0.0 all-gather.3.cloned.1.call-start
  6.5 1.5 fusion
  8.1 2.5 %fusion.1 = bf16[512,1024]{1,0:T(8,128)(2,1)} fusion(bf16[1,512,1024]{2,1,0:T(8,128)(2,1)} %param.3, f32[512]{0:T(512)S(1)} %rsqrt_multiply_fusion), kind=kLoop, calls=%fused_computation.4 | loop fusion | flops 1572864 | bytes 2099200 | tf_op jit(solution)/shard_map/convert_element_type | solution.py:18
  10.6 0.0 all-gather.3.cloned.1.call-update
  10.6 28.4 %all-gather = s32[1,4096]{1,0:T(1,128)S(1)} all-gather(s32[1,512]{1,0:T(1,128)} %param.4), channel_id=2, replica_groups=mesh['blk'=8,'grp'=4] {'blk'}, dimensions={1}, use_global_device_ids=true | all-gather | bytes 18432 | tf_op jit(solution)/shard_map/all_gather | solution.py:50
  39.0 0.9 fusion.3
  39.9 0.8 fusion.4
  40.7 31.6 %all_gather.9 = bf16[128,1024]{1,0:T(8,128)(2,1)S(1)} all-gather(bf16[16,1024]{1,0:T(8,128)(2,1)S(1)} %fusion.4), channel_id=1, replica_groups=mesh['blk'=8,'grp'=4] {'blk'}, dimensions={0}, use_global_device_ids=true | all-gather | bytes 294912 | tf_op jit(solution)/shard_map/all_gather | solution.py:42
  72.3 1.8 multiply_reduce_fusion
  74.1 66.4 %all-gather.3.cloned.1.call-done = bf16[4096,1024]{1,0:T(8,128)(2,1)} async-done(((bf16[512,1024]{1,0:T(8,128)(2,1)}), bf16[4096,1024]{1,0:T(8,128)(2,1)}) %all-gather.3.cloned.1.call-update) | async-done | bytes 8388624 | tf_op jit(solution)/shard_map/all_gather | solution.py:49
  140.5 9.1 %select_reduce_fusion = f32[512]{0:T(512)S(1)} fusion(bf16[512,1024]{1,0:T(8,128)(2,1)} %fusion.1, bf16[4096,1024]{1,0:T(8,128)(2,1)} %all-gather.3.cloned.1.call-done, s32[4096]{0:T(1024)S(1)} %bitcast.14, s32[512]{0:T(512)} %bitcast.16), kind=kOutput, calls=%fused_computation | convolution fusion | flops 4305452544 | bytes 9457664 | tf_op jit(solution)/shard_map/dot_general | solution.py:22
  149.6 0.6 fusion.5
  150.2 38.8 %psum.7 = f32[]{:T(128)} all-reduce(f32[]{:T(128)} %get-tuple-element.5), channel_id=1, replica_groups=mesh['blk'=8,'grp'=4] {'blk','grp'}, use_global_device_ids=true, to_apply=%region_5.6 | all-reduce | flops 1 | bytes 8 | tf_op jit(solution)/shard_map/psum | solution.py:53
  189.7 0.6 broadcast_multiply_fusion
  (2 shorter events, 0.0 us)
Async XLA Ops:
  6.5 134.0 %all-gather.3.cloned.1.call-start = ((), (), s32[]{:S(2)}) async-start(), calls=%async_computation | async-start | bytes 9437184 | tf_op jit(solution)/shard_map/all_gather | solution.py:49
Sparse Core Ops, SparseCore 0:
  10.7 129.7 all-gather.2
where the time goes:
time: 198 us; the launch traced here: 197 us
  blocking collectives  98.8 us (50%)
  waiting for transfers between devices  66.4 us (34%)
  between operations  14.1 us (7%)
  matrix products  10.9 us (6%)
  other arithmetic  6.97 us (4%)
    all_gather x1, waiting for transfers between devices, body(): guest_rows = lax.all_gather(own_units, 'blk', axis=0, tiled=True)  66.4 us
    psum x1, blocking collectives, body(): total = lax.psum(jnp.sum(weights), ('blk', 'grp'))  38.8 us
    all_gather x1, blocking collectives, body(): cent_units = lax.all_gather(cent_local, 'blk', axis=0, tiled=True)  31.6 us
    all_gather x1, blocking collectives, body(): guest_ids = lax.all_gather(own_ids, 'blk', axis=0, tiled=True)  28.4 us
    dot_general x1, matrix products, dense_sums(): lax.dot_general(query_rows, key_rows, (((1,), (1,)), ((), ())), preferred...  9.08 us
  transfers between devices with their start and end apart: 1, of which 1 were waited for; matrix products, arithmetic and copies ran while one was open for 2% of the time, Pallas kernels for 0%

commit v1 on v0

v1 whole, which is shorter than its diff:
```python
import functools
import math

import jax
import jax.numpy as jnp
from jax import lax
from jax.experimental import pallas as pl
from jax.experimental.pallas import tpu as pltpu
from jax.sharding import PartitionSpec as P

base_term = 0.05
epsilon = 1e-06
LANES = 128
TAIL = 16

VMEM = pl.BlockSpec(memory_space=pltpu.VMEM)
SMEM = pl.BlockSpec(memory_space=pltpu.SMEM)


def unit_values(rows):
    values = rows.astype(jnp.float32)
    mean = jnp.mean(values * values, axis=-1, keepdims=True)
    scaling = lax.rsqrt(mean + epsilon) / math.sqrt(rows.shape[-1])
    return (values * scaling).astype(jnp.bfloat16)


def first_row(ids, owner, strata_dev, last):
    return jnp.minimum(jnp.sum((ids < owner * strata_dev).astype(jnp.int32)), last)


def pack_kernel(peers, cap, strata_dev, place_ref, ids_ref, rows_ref, *rest):
    outs, held = rest[:peers], rest[peers]
    rows, width = rows_ref.shape
    step, window = 32, 2 * LANES

    def normalize(i, carry):
        at = pl.ds(pl.multiple_of(i * step, step), step)
        held[at, :] = unit_values(rows_ref[at, :])
        return carry

    lax.fori_loop(0, rows // step, normalize, 0, unroll=2)
    ids = ids_ref[...]
    ids_wide = jnp.broadcast_to(ids.astype(jnp.float32), (8, rows))
    for k, out in enumerate(outs):
        start = first_row(ids, place_ref[0] ^ k, strata_dev, rows - cap)
        base = jnp.minimum(start // LANES * LANES, rows - window)
        pick = lax.broadcasted_iota(jnp.int32, (cap, window), 1) == lax.broadcasted_iota(
            jnp.int32, (cap, window), 0
        ) + (start - base)
        run = jnp.dot(
            pick.astype(jnp.bfloat16),
            held[pl.ds(pl.multiple_of(base, LANES), window), :],
            preferred_element_type=jnp.float32,
        ).astype(jnp.bfloat16)
        for c in range(width // LANES):
            out[c * cap : (c + 1) * cap, :] = run[:, c * LANES : (c + 1) * LANES]
        turned = pltpu.roll(ids_wide, rows - start, axis=1)[:, :LANES]
        out[width // LANES * cap :, :] = jnp.concatenate([turned, turned], axis=0).astype(
            jnp.bfloat16
        )


def own_kernel(peers, cap, groups, place_ref, cent_ref, *rest):
    blocks, (out_ref, units, id_col) = rest[:peers], rest[peers:]
    slots, width = units.shape
    strata_dev = cent_ref.shape[0]
    me, group = place_ref[0], place_ref[1]
    low = (me * strata_dev).astype(jnp.float32)

    id_rows = []
    for k, block in enumerate(blocks):
        for c in range(width // LANES):
            units[k * cap : (k + 1) * cap, c * LANES : (c + 1) * LANES] = block[
                c * cap : (c + 1) * cap, :
            ]
        ids = block[width // LANES * cap :, :].astype(jnp.float32)[:1, :]
        ids = ids - low
        ids = jnp.where((ids >= 0) & (ids < strata_dev), ids, -1.0)
        id_rows.append(ids[:, :cap])
        wide = jnp.broadcast_to(ids, (LANES, LANES)).T
        id_col[k * cap : (k + 1) * cap, :] = wide[:cap, :]
    id_row = jnp.concatenate(id_rows, axis=1)
    real = id_row >= 0.0
    id_key = jnp.where(real, id_row, -2.0)

    tile = 256
    sums = jnp.zeros((8, slots), jnp.float32)
    everything = units[...]
    for t in range(slots // tile):
        scores = lax.dot_general(
            units[t * tile : (t + 1) * tile, :],
            everything,
            (((1,), (1,)), ((), ())),
            preferred_element_type=jnp.float32,
        )
        kernel = jnp.exp((scores - 1.0) * 4.0)
        same = jnp.concatenate([id_col[t * tile : (t + 1) * tile, :]] * (slots // LANES), axis=1) == id_key
        kernel = jnp.where(same, kernel, 0.0)
        sums = sums + jnp.sum(kernel.reshape(tile // 8, 8, slots), axis=0)
    density = jnp.sum(sums, axis=0, keepdims=True)

    cent_units = unit_values(cent_ref[...])
    near = lax.dot_general(
        cent_units, everything, (((1,), (1,)), ((), ())), preferred_element_type=jnp.float32
    )
    which = lax.broadcasted_iota(jnp.int32, near.shape, 0).astype(jnp.float32)
    picked = jnp.sum(jnp.where(which == id_row, near, 0.0), axis=0, keepdims=True)
    weight = jnp.where(
        real, ((1.0 - picked) + base_term) / jnp.where(real, density, 1.0), 0.0
    )
    out_ref[...] = jnp.broadcast_to(jnp.sum(weight, axis=1, keepdims=True), out_ref.shape)
    for k in range(peers):
        row = 2 * ((me ^ k) * groups + group)
        out_ref[pl.ds(row, 1), :cap] = weight[:, k * cap : (k + 1) * cap]


def finish_kernel(peers, cap, groups, strata_dev, place_ref, ids_ref, got_ref, out_ref):
    rows = ids_ref.shape[1]
    group = place_ref[1]
    got = got_ref[...]
    odd = lax.broadcasted_iota(jnp.int32, got.shape, 0) % 2
    total = jnp.sum(jnp.where(odd == 1, got, 0.0), axis=0, keepdims=True)[:, :1]
    ids = ids_ref[...]
    weight = jnp.zeros((1, rows), jnp.float32)
    for owner in range(peers):
        start = first_row(ids, owner, strata_dev, rows - cap)
        part = got_ref[pl.ds(2 * (owner * groups + group), 1), :]
        part = jnp.broadcast_to(jnp.concatenate([part] * (rows // LANES), axis=1), (8, rows))
        part = pltpu.roll(part, start, axis=1)[:1, :]
        mine = (ids >= owner * strata_dev) & (ids < (owner + 1) * strata_dev)
        weight = jnp.where(mine, part, weight)
    out_ref[...] = weight * (float(rows * peers * groups) / total)


def body(embeddings, strata, centroids):
    peers, groups = lax.axis_size("blk"), lax.axis_size("grp")
    rows, width = embeddings.shape[1:]
    strata_dev = centroids.shape[1]
    cap = 2 * rows // peers
    depth = width // LANES * cap + TAIL
    place = jnp.stack([lax.axis_index("blk"), lax.axis_index("grp")]).astype(jnp.int32)

    message = jax.ShapeDtypeStruct((depth, LANES), jnp.bfloat16)
    blocks = pl.pallas_call(
        functools.partial(pack_kernel, peers, cap, strata_dev),
        out_shape=[message] * peers,
        in_specs=[SMEM, VMEM, VMEM],
        out_specs=[VMEM] * peers,
        scratch_shapes=[pltpu.VMEM((rows, width), jnp.bfloat16)],
        name="pack",
    )(place, strata, embeddings[0])
    blocks = [blocks[0]] + [
        lax.ppermute(blocks[k], "blk", [(i, i ^ k) for i in range(peers)])
        for k in range(1, peers)
    ]
    sent = pl.pallas_call(
        functools.partial(own_kernel, peers, cap, groups),
        out_shape=jax.ShapeDtypeStruct((peers * groups * 2, LANES), jnp.float32),
        in_specs=[SMEM] + [VMEM] * (peers + 1),
        out_specs=VMEM,
        scratch_shapes=[
            pltpu.VMEM((peers * cap, width), jnp.bfloat16),
            pltpu.VMEM((peers * cap, LANES), jnp.float32),
        ],
        name="own",
    )(place, centroids[0], *blocks)
    got = lax.all_to_all(
        sent.reshape(peers * groups, 2, LANES), ("blk", "grp"), 0, 0, tiled=True
    ).reshape(peers * groups * 2, LANES)
    return pl.pallas_call(
        functools.partial(finish_kernel, peers, cap, groups, strata_dev),
        out_shape=jax.ShapeDtypeStruct((1, rows), jnp.float32),
        in_specs=[SMEM, VMEM, VMEM],
        out_specs=VMEM,
        name="finish",
    )(place, strata, got)


def solution(mesh):
    placed = (P("grp", "blk", None), P("grp", "blk"), P("grp", "blk", None))
    return jax.shard_map(
        body, mesh=mesh, in_specs=placed, out_specs=P("grp", "blk"), check_vma=False
    )
```

time: 198 us -> 78.4 us (0.40)
  blocking collectives: 98.8 us -> 20.6 us
  waiting for transfers between devices: 66.4 us -> 31.2 us
  between operations: 14.1 us -> 0.06 us
  starting transfers between devices: 0.01 us -> 13.6 us
  Pallas kernels: 0 us -> 11.1 us
  matrix products: 10.9 us -> 0 us
  other arithmetic: 6.97 us -> 0.67 us
    all_gather x1 -> x0, waiting for transfers between devices: 66.4 us -> none  [body(): guest_rows = lax.all_gather(own_units, 'blk', axis=0, tiled=True)]
    all_gather x2 -> x0, blocking collectives: 60 us -> none  [the longest x1 31.6 us: body(): cent_units = lax.all_gather(cent_local, 'blk', axis=0, tiled=True)]
    psum x1 -> x0, blocking collectives: 38.8 us -> none  [body(): total = lax.psum(jnp.sum(weights), ('blk', 'grp'))]
    ppermute x0 -> x7, waiting for transfers between devices: none -> 31.2 us  [body(): lax.ppermute(blocks[k], 'blk', [(i, i ^ k) for i in range(peers)])]
    all_to_all x0 -> x1, blocking collectives: none -> 20.6 us  [body(): lax.all_to_all(sent.reshape(peers * groups, 2, LANES), ('blk', 'grp'), 0,...]
    ppermute x0 -> x7, starting transfers between devices: none -> 13.6 us  [body(): lax.ppermute(blocks[k], 'blk', [(i, i ^ k) for i in range(peers)])]
    pallas_call x0 -> x3, Pallas kernels: none -> 11.1 us  [the longest x1 5.45 us: body(): pl.pallas_call(functools.partial(own_kernel, peers, cap, groups), out_sha...]
    dot_general x2 -> x0, matrix products: 10.9 us -> none  [the longest x1 9.08 us: dense_sums(): lax.dot_general(query_rows, key_rows, (((1,), (1,)), ((), ())), preferred...]
  transfers between devices with their start and end apart: 1 -> 7, of which waited for: 1 -> 4; matrix products, arithmetic and copies ran while one was open for 2% -> 0% of each run, Pallas kernels for 0% -> 0%
where the time goes in v1:
time: 78.4 us; the launch traced here: 78.2 us
  waiting for transfers between devices  31.2 us (40%)
  blocking collectives  20.6 us (26%)
  starting transfers between devices  13.6 us (17%)
  Pallas kernels  11.1 us (14%)
  local copies, waits for them, and re-layouts  0.89 us (1%)
    ppermute x7, waiting for transfers between devices, body(): lax.ppermute(blocks[k], 'blk', [(i, i ^ k) for i in range(peers)])  31.2 us
    all_to_all x1, blocking collectives, body(): lax.all_to_all(sent.reshape(peers * groups, 2, LANES), ('blk', 'grp'), 0,...  20.6 us
    ppermute x7, starting transfers between devices, body(): lax.ppermute(blocks[k], 'blk', [(i, i ^ k) for i in range(peers)])  13.6 us
    pallas_call x1, Pallas kernels, body(): pl.pallas_call(functools.partial(own_kernel, peers, cap, groups), out_sha...  5.45 us
    pallas_call x1, Pallas kernels, body(): pl.pallas_call(functools.partial(pack_kernel, peers, cap, strata_dev), ou...  4.1 us
    pallas_call x1, Pallas kernels, body(): pl.pallas_call(functools.partial(finish_kernel, peers, cap, groups, strat...  1.59 us
  transfers between devices with their start and end apart: 7, of which 4 were waited for; matrix products, arithmetic and copies ran while one was open for 0% of the time, Pallas kernels for 0%

profile of v1, /device:TPU:0, one launch (start us, length us, event | category | flops | bytes accessed | tf_op | source)
XLA Modules:
  0.0 78.2 jit_solution(18407615663690645443)
XLA Ops:
  0.0 0.7 pad_add_fusion.place_ref
  0.7 4.1 %pack.1 = (bf16[1040,128]{1,0:T(8,128)(2,1)}, bf16[1040,128]{1,0:T(8,128)(2,1)}, bf16[1040,128]{1,0:T(8,128)(2,1)}, bf16[1040,128]{1,0:T(8,128)(2,1)}, bf16[1040...) custom-call(s32[2]{0:T(128)} %pad_add_fusion.place_ref, ...), custom_call_target="tpu_custom_call" | custom-call | tf_op jit(solution)/shard_map/pack/pallas_call | solution.py:144
  4.8 3.0 %collective-permute-start = (bf16[1040,128]{1,0:T(8,128)(2,1)}, bf16[1040,128]{1,0:T(8,128)(2,1)S(1)}, u32[]{:S(2)}, u32[]{:S(2)}) collective-permute-start(bf16[1040,128]{1,0:T(8,128)(2,1)} %get-tuple-element.14), channel_id=1, source_target_pairs={{0,4},{4,0},{8,12},{12,8},{16,20},{20,16},{24,28},{28,24},{1,5},{5... | collective-permute-start | bytes 798728 | tf_op jit(solution)/shard_map/ppermute | solution.py:153
  7.7 1.6 %collective-permute-start.1 = (bf16[1040,128]{1,0:T(8,128)(2,1)}, bf16[1040,128]{1,0:T(8,128)(2,1)S(1)}, u32[]{:S(2)}, u32[]{:S(2)}) collective-permute-start(bf16[1040,128]{1,0:T(8,128)(2,1)} %get-tuple-element.15), channel_id=1, source_target_pairs={{0,8},{4,12},{8,0},{12,4},{16,24},{20,28},{24,16},{28,20},{1,9},{5... | collective-permute-start | bytes 798728 | tf_op jit(solution)/shard_map/ppermute | solution.py:153
  9.3 0.0 collective-permute-start.2
  9.3 3.0 %collective-permute-start.3 = (bf16[1040,128]{1,0:T(8,128)(2,1)}, bf16[1040,128]{1,0:T(8,128)(2,1)S(1)}, u32[]{:S(2)}, u32[]{:S(2)}) collective-permute-start(bf16[1040,128]{1,0:T(8,128)(2,1)} %get-tuple-element.17), channel_id=1, source_target_pairs={{0,16},{4,20},{8,24},{12,28},{16,0},{20,4},{24,8},{28,12},{1,17},{... | collective-permute-start | bytes 798728 | tf_op jit(solution)/shard_map/ppermute | solution.py:153
  12.3 1.3 %collective-permute-start.4 = (bf16[1040,128]{1,0:T(8,128)(2,1)}, bf16[1040,128]{1,0:T(8,128)(2,1)S(1)}, u32[]{:S(2)}, u32[]{:S(2)}) collective-permute-start(bf16[1040,128]{1,0:T(8,128)(2,1)} %get-tuple-element.18), channel_id=1, source_target_pairs={{0,20},{4,16},{8,28},{12,24},{16,4},{20,0},{24,12},{28,8},{1,21},{... | collective-permute-start | bytes 798728 | tf_op jit(solution)/shard_map/ppermute | solution.py:153
  13.6 0.7 collective-permute-done.rest_1_
  14.3 0.0 copy-start
  14.3 3.8 %collective-permute-start.5 = (bf16[1040,128]{1,0:T(8,128)(2,1)}, bf16[1040,128]{1,0:T(8,128)(2,1)S(1)}, u32[]{:S(2)}, u32[]{:S(2)}) collective-permute-start(bf16[1040,128]{1,0:T(8,128)(2,1)} %get-tuple-element.19), channel_id=1, source_target_pairs={{0,24},{4,28},{8,16},{12,20},{16,8},{20,12},{24,0},{28,4},{1,25},{... | collective-permute-start | bytes 798728 | tf_op jit(solution)/shard_map/ppermute | solution.py:153
  18.2 9.6 %collective-permute-done.1.rest_2_ = bf16[1040,128]{1,0:T(8,128)(2,1)S(1)} collective-permute-done((bf16[1040,128]{1,0:T(8,128)(2,1)}, bf16[1040,128]{1,0:T(8,128)(2,1)S(1)}, u32[]{:S(2)}, u32[]{:S(2)}) %collective-permute-start.1) | collective-permute-done | bytes 266272 | tf_op jit(solution)/shard_map/ppermute | solution.py:153
  27.7 0.0 copy-start.1
  27.7 1.0 %collective-permute-start.6 = (bf16[1040,128]{1,0:T(8,128)(2,1)}, bf16[1040,128]{1,0:T(8,128)(2,1)S(1)}, u32[]{:S(2)}, u32[]{:S(2)}) collective-permute-start(bf16[1040,128]{1,0:T(8,128)(2,1)} %get-tuple-element.20), channel_id=1, source_target_pairs={{0,28},{4,24},{8,20},{12,16},{16,12},{20,8},{24,4},{28,0},{1,29},{... | collective-permute-start | bytes 798728 | tf_op jit(solution)/shard_map/ppermute | solution.py:153
  28.7 2.3 %collective-permute-done.2.rest_3_ = bf16[1040,128]{1,0:T(8,128)(2,1)S(1)} collective-permute-done((bf16[1040,128]{1,0:T(8,128)(2,1)}, bf16[1040,128]{1,0:T(8,128)(2,1)S(1)}, u32[]{:S(2)}, u32[]{:S(2)}) %collective-permute-start.2) | collective-permute-done | bytes 266272 | tf_op jit(solution)/shard_map/ppermute | solution.py:153
  31.1 0.0 copy-start.2
  31.1 0.0 collective-permute-done.3.rest_4_
  31.1 0.0 copy-start.3
  31.1 18.5 %collective-permute-done.4.rest_5_ = bf16[1040,128]{1,0:T(8,128)(2,1)S(1)} collective-permute-done((bf16[1040,128]{1,0:T(8,128)(2,1)}, bf16[1040,128]{1,0:T(8,128)(2,1)S(1)}, u32[]{:S(2)}, u32[]{:S(2)}) %collective-permute-start.4) | collective-permute-done | bytes 266272 | tf_op jit(solution)/shard_map/ppermute | solution.py:153
  49.6 0.0 copy-start.4
  49.6 0.0 collective-permute-done.5.rest_6_
  49.6 0.0 collective-permute-done.6.rest_7_
  49.6 0.0 copy-start.6
  49.7 0.0 copy-done
  49.7 0.0 copy-done.1
  49.7 0.0 copy-done.2
  49.7 0.0 copy-done.3
  49.7 0.6 copy-done.4
  50.3 0.1 copy-done.5
  50.5 0.1 copy-done.6
  50.6 5.4 %own.1 = f32[64,128]{1,0:T(8,128)} custom-call(s32[2]{0:T(128)} %pad_add_fusion.place_ref, bf16[16,1024]{1,0:T(8,128)(2,1)} %bitcast.9, bf16[1040,128]{1,0:T(8,128)(2,1)} %get-tuple-element.13.rest_0_, bf16[1040,128]{1,0:T(8,128)(2,1)} %copy-done, bf16[1040,128]{1,0:T(8,128)(2,1)} %copy-done.1, bf16[1040,128]{1,0:T(8,128)(2,1)} %copy-done.2, ...), custom_call_target="tpu_custom_call" | custom-call | tf_op jit(solution)/shard_map/own/pallas_call | solution.py:156
  56.0 20.6 %all_to_all.5 = f32[32,2,128]{2,1,0:T(2,128)} all-to-all(f32[32,2,128]{2,1,0:T(2,128)} %bitcast.7), channel_id=1, replica_groups=mesh['blk'=8,'grp'=4] {'blk','grp'}, dimensions={0} | all-to-all | bytes 65536 | tf_op jit(solution)/shard_map/all_to_all | solution.py:167
  76.6 1.6 %finish.1 = f32[1,512]{1,0:T(1,128)} custom-call(s32[2]{0:T(128)} %pad_add_fusion.place_ref, s32[1,512]{1,0:T(1,128)} %ids_ref.3, f32[64,128]{1,0:T(8,128)} %bitcast.8), custom_call_target="tpu_custom_call" | custom-call | tf_op jit(solution)/shard_map/finish/pallas_call | solution.py:170
  (1 shorter events, 0.0 us)
Async XLA Ops:
  4.8 9.6 %collective-permute-start = (bf16[1040,128]{1,0:T(8,128)(2,1)}, bf16[1040,128]{1,0:T(8,128)(2,1)S(1)}, u32[]{:S(2)}, u32[]{:S(2)}) collective-permute-start(bf16[1040,128]{1,0:T(8,128)(2,1)} %get-tuple-element.14), channel_id=1, source_target_pairs={{0,4},{4,0},{8,12},{12,8},{16,20},{20,16},{24,28},{28,24},{1,5},{5... | collective-permute-start | bytes 798728 | tf_op jit(solution)/shard_map/ppermute | solution.py:153
  7.7 20.0 %collective-permute-start.1 = (bf16[1040,128]{1,0:T(8,128)(2,1)}, bf16[1040,128]{1,0:T(8,128)(2,1)S(1)}, u32[]{:S(2)}, u32[]{:S(2)}) collective-permute-start(bf16[1040,128]{1,0:T(8,128)(2,1)} %get-tuple-element.15), channel_id=1, source_target_pairs={{0,8},{4,12},{8,0},{12,4},{16,24},{20,28},{24,16},{28,20},{1,9},{5... | collective-permute-start | bytes 798728 | tf_op jit(solution)/shard_map/ppermute | solution.py:153
  9.3 21.8 %collective-permute-start.2 = (bf16[1040,128]{1,0:T(8,128)(2,1)}, bf16[1040,128]{1,0:T(8,128)(2,1)S(1)}, u32[]{:S(2)}, u32[]{:S(2)}) collective-permute-start(bf16[1040,128]{1,0:T(8,128)(2,1)} %get-tuple-element.16), channel_id=1, source_target_pairs={{0,12},{4,8},{8,4},{12,0},{16,28},{20,24},{24,20},{28,16},{1,13},{... | collective-permute-start | bytes 798728 | tf_op jit(solution)/shard_map/ppermute | solution.py:153
  9.3 21.8 %collective-permute-start.3 = (bf16[1040,128]{1,0:T(8,128)(2,1)}, bf16[1040,128]{1,0:T(8,128)(2,1)S(1)}, u32[]{:S(2)}, u32[]{:S(2)}) collective-permute-start(bf16[1040,128]{1,0:T(8,128)(2,1)} %get-tuple-element.17), channel_id=1, source_target_pairs={{0,16},{4,20},{8,24},{12,28},{16,0},{20,4},{24,8},{28,12},{1,17},{... | collective-permute-start | bytes 798728 | tf_op jit(solution)/shard_map/ppermute | solution.py:153
  12.3 37.3 %collective-permute-start.4 = (bf16[1040,128]{1,0:T(8,128)(2,1)}, bf16[1040,128]{1,0:T(8,128)(2,1)S(1)}, u32[]{:S(2)}, u32[]{:S(2)}) collective-permute-start(bf16[1040,128]{1,0:T(8,128)(2,1)} %get-tuple-element.18), channel_id=1, source_target_pairs={{0,20},{4,16},{8,28},{12,24},{16,4},{20,0},{24,12},{28,8},{1,21},{... | collective-permute-start | bytes 798728 | tf_op jit(solution)/shard_map/ppermute | solution.py:153
  14.3 35.3 %copy-start = (bf16[1040,128]{1,0:T(8,128)(2,1)}, bf16[1040,128]{1,0:T(8,128)(2,1)S(1)}, u32[]{:S(2)}) copy-start(bf16[1040,128]{1,0:T(8,128)(2,1)S(1)} %collective-permute-done.rest_1_) | copy-start | bytes 798724
  14.3 35.3 %collective-permute-start.5 = (bf16[1040,128]{1,0:T(8,128)(2,1)}, bf16[1040,128]{1,0:T(8,128)(2,1)S(1)}, u32[]{:S(2)}, u32[]{:S(2)}) collective-permute-start(bf16[1040,128]{1,0:T(8,128)(2,1)} %get-tuple-element.19), channel_id=1, source_target_pairs={{0,24},{4,28},{8,16},{12,20},{16,8},{20,12},{24,0},{28,4},{1,25},{... | collective-permute-start | bytes 798728 | tf_op jit(solution)/shard_map/ppermute | solution.py:153
  27.7 21.9 %copy-start.1 = (bf16[1040,128]{1,0:T(8,128)(2,1)}, bf16[1040,128]{1,0:T(8,128)(2,1)S(1)}, u32[]{:S(2)}) copy-start(bf16[1040,128]{1,0:T(8,128)(2,1)S(1)} %collective-permute-done.1.rest_2_) | copy-start | bytes 798724
  27.7 21.9 %collective-permute-start.6 = (bf16[1040,128]{1,0:T(8,128)(2,1)}, bf16[1040,128]{1,0:T(8,128)(2,1)S(1)}, u32[]{:S(2)}, u32[]{:S(2)}) collective-permute-start(bf16[1040,128]{1,0:T(8,128)(2,1)} %get-tuple-element.20), channel_id=1, source_target_pairs={{0,28},{4,24},{8,20},{12,16},{16,12},{20,8},{24,4},{28,0},{1,29},{... | collective-permute-start | bytes 798728 | tf_op jit(solution)/shard_map/ppermute | solution.py:153
  31.1 18.6 %copy-start.2 = (bf16[1040,128]{1,0:T(8,128)(2,1)}, bf16[1040,128]{1,0:T(8,128)(2,1)S(1)}, u32[]{:S(2)}) copy-start(bf16[1040,128]{1,0:T(8,128)(2,1)S(1)} %collective-permute-done.2.rest_3_) | copy-start | bytes 798724
  31.1 18.6 %copy-start.3 = (bf16[1040,128]{1,0:T(8,128)(2,1)}, bf16[1040,128]{1,0:T(8,128)(2,1)S(1)}, u32[]{:S(2)}) copy-start(bf16[1040,128]{1,0:T(8,128)(2,1)S(1)} %collective-permute-done.3.rest_4_) | copy-start | bytes 798724
  49.6 0.7 copy-start.4
  49.6 0.8 %copy-start.5 = (bf16[1040,128]{1,0:T(8,128)(2,1)}, bf16[1040,128]{1,0:T(8,128)(2,1)S(1)}, u32[]{:S(2)}) copy-start(bf16[1040,128]{1,0:T(8,128)(2,1)S(1)} %collective-permute-done.5.rest_6_) | copy-start | bytes 798724
  49.6 0.9 %copy-start.6 = (bf16[1040,128]{1,0:T(8,128)(2,1)}, bf16[1040,128]{1,0:T(8,128)(2,1)S(1)}, u32[]{:S(2)}) copy-start(bf16[1040,128]{1,0:T(8,128)(2,1)S(1)} %collective-permute-done.6.rest_7_) | copy-start | bytes 798724

commit v2 on v0

v2 whole, which is shorter than its diff:
```python
import functools
import math

import jax
import jax.numpy as jnp
from jax import lax
from jax.experimental import pallas as pl
from jax.experimental.pallas import tpu as pltpu
from jax.sharding import PartitionSpec as P


base_term = 0.05
epsilon = 1e-06
LANES = 128
TAIL = 16
AXES = ("blk", "grp")

VMEM = pl.BlockSpec(memory_space=pltpu.VMEM)
SMEM = pl.BlockSpec(memory_space=pltpu.SMEM)


def unit_values(rows):
    values = rows.astype(jnp.float32)
    mean = jnp.mean(values * values, axis=-1, keepdims=True)
    scaling = lax.rsqrt(mean + epsilon) / math.sqrt(rows.shape[-1])
    return (values * scaling).astype(jnp.bfloat16)


def across(left, right):
    return lax.dot_general(
        left, right, (((1,), (1,)), ((), ())), preferred_element_type=jnp.float32
    )


def first_row(ids, shard, strata_dev, last):
    return jnp.minimum(jnp.sum((ids < shard * strata_dev).astype(jnp.int32)), last)


def pack_kernel(chips, cap, strata_dev, ids_ref, rows_ref, *rest):
    outs, held = rest[:chips], rest[chips]
    rows, width = rows_ref.shape
    step, window = 32, 2 * LANES
    chip = lax.axis_index("blk") % chips

    def normalize(i, carry):
        at = pl.ds(pl.multiple_of(i * step, step), step)
        held[at, :] = unit_values(rows_ref[at, :])
        return carry

    lax.fori_loop(0, rows // step, normalize, 0, unroll=2)
    ids = ids_ref[...]
    ids_wide = jnp.broadcast_to(ids.astype(jnp.float32), (8, rows))
    for d, out in enumerate(outs):
        tails = []
        for r in range(2):
            start = first_row(ids, (chip ^ d) * 2 + r, strata_dev, rows - cap)
            base = jnp.minimum(start // LANES * LANES, rows - window)
            pick = lax.broadcasted_iota(jnp.int32, (cap, window), 1) == lax.broadcasted_iota(
                jnp.int32, (cap, window), 0
            ) + (start - base)
            run = jnp.dot(
                pick.astype(jnp.bfloat16),
                held[pl.ds(pl.multiple_of(base, LANES), window), :],
                preferred_element_type=jnp.float32,
            ).astype(jnp.bfloat16)
            for c in range(width // LANES):
                at = (2 * c + r) * cap
                out[at : at + cap, :] = run[:, c * LANES : (c + 1) * LANES]
            tails.append(pltpu.roll(ids_wide, rows - start, axis=1)[:, :LANES])
        out[width // LANES * 2 * cap :, :] = jnp.concatenate(tails, axis=0).astype(jnp.bfloat16)


def unpack(blocks, cap, strata_dev, units, id_col):
    chip = lax.axis_index("blk") % len(blocks)
    each = len(blocks) * cap
    width = units.shape[1]
    id_rows = [[], []]
    for d, block in enumerate(blocks):
        tail = block[width // LANES * 2 * cap :, :].astype(jnp.float32)
        for r in range(2):
            at = r * each + d * cap
            for c in range(width // LANES):
                units[at : at + cap, c * LANES : (c + 1) * LANES] = block[
                    (2 * c + r) * cap : (2 * c + r + 1) * cap, :
                ]
            ids = tail[8 * r : 8 * r + 1, :] - ((2 * chip + r) * strata_dev).astype(jnp.float32)
            ids = jnp.where((ids >= 0) & (ids < strata_dev), ids, -1.0)
            id_rows[r].append(ids[:, :cap])
            id_col[at : at + cap, :] = jnp.broadcast_to(ids, (LANES, LANES)).T[:cap, :]
    return [jnp.concatenate(rows, axis=1) for rows in id_rows]


def masked_exp(scores, id_col, id_key):
    same = jnp.concatenate([id_col] * (scores.shape[1] // LANES), axis=1) == id_key
    return jnp.where(same, jnp.exp((scores - 1.0) * 4.0), 0.0)


def fold(kernel):
    rows, lanes = kernel.shape
    return jnp.sum(kernel.reshape(rows // 8, 8, lanes), axis=0)


def key_of(id_row):
    return jnp.where(id_row >= 0.0, id_row, -2.0)


def picked_by(cent_units, units, id_row):
    near = across(cent_units, units)
    which = lax.broadcasted_iota(jnp.int32, near.shape, 0).astype(jnp.float32)
    return jnp.sum(jnp.where(which == id_row, near, 0.0), axis=0, keepdims=True)


def early_kernel(chips, cap, cent0_ref, cent1_ref, *rest):
    blocks = rest[:chips]
    units, id_col, cents, facts = rest[chips:]
    strata_dev = cent0_ref.shape[0]
    each = chips * cap
    id_rows = unpack(blocks, cap, strata_dev, units, id_col)
    cents[:strata_dev, :] = unit_values(cent0_ref[...])
    cents[strata_dev:, :] = unit_values(cent1_ref[...])
    for r in range(2):
        mine = units[r * each : (r + 1) * each, :]
        sums = jnp.zeros((8, each), jnp.float32)
        for t in range(each // LANES):
            at = r * each + t * LANES
            kernel = masked_exp(
                across(units[at : at + LANES, :], mine), id_col[at : at + LANES, :], key_of(id_rows[r])
            )
            sums = sums + fold(kernel)
        picked = picked_by(cents[r * strata_dev : (r + 1) * strata_dev, :], mine, id_rows[r])
        facts[r : r + 1, :] = jnp.sum(sums, axis=0, keepdims=True)
        facts[2 + r : 3 + r, :] = picked
        facts[4 + r : 5 + r, :] = id_rows[r]


def late_kernel(chips, cap, groups, units_a, col_a, cents, facts, *rest):
    blocks, (out_ref, units_b, col_b) = rest[:chips], rest[chips:]
    strata_dev = cents.shape[0] // 2
    each = chips * cap
    me, group = lax.axis_index("blk"), lax.axis_index("grp")
    at_work = (me // chips) != (group % 2)
    rows_b = unpack(blocks, cap, strata_dev, units_b, col_b)
    total = jnp.zeros((1, 1), jnp.float32)
    weights = []
    for r in range(2):
        row_a, row_b = facts[4 + r : 5 + r, :], rows_b[r]
        key_b = key_of(row_b)
        mine = units_b[r * each : (r + 1) * each, :]
        sums = jnp.zeros((8, each), jnp.float32)
        more_a = []
        for t in range(each // LANES):
            at = r * each + t * LANES
            kernel = masked_exp(
                across(units_a[at : at + LANES, :], mine), col_a[at : at + LANES, :], key_b
            )
            sums = sums + fold(kernel)
            part = sum(
                kernel[:, c * LANES : (c + 1) * LANES] for c in range(1, each // LANES)
            ) + kernel[:, :LANES]
            more_a.append(jnp.sum(part.T, axis=0, keepdims=True))
            kernel = masked_exp(
                across(units_b[at : at + LANES, :], mine), col_b[at : at + LANES, :], key_b
            )
            sums = sums + fold(kernel)
        density_a = facts[r : r + 1, :] + jnp.concatenate(more_a, axis=1)
        density_b = jnp.sum(sums, axis=0, keepdims=True)
        picked_a = facts[2 + r : 3 + r, :]
        picked_b = picked_by(cents[r * strata_dev : (r + 1) * strata_dev, :], mine, row_b)
        both = []
        for row, picked, density in ((row_a, picked_a, density_a), (row_b, picked_b, density_b)):
            real = row >= 0.0
            weight = jnp.where(
                real, ((1.0 - picked) + base_term) / jnp.where(real, density, 1.0), 0.0
            )
            total = total + jnp.sum(weight, axis=1, keepdims=True)
            both.append(weight)
        weights.append(both)
    out_ref[...] = jnp.broadcast_to(jnp.where(at_work, total, 0.0), out_ref.shape)
    for r in range(2):
        for side in range(2):
            for d in range(chips):
                source = me ^ (d + side * chips)
                row = 4 * (source * groups + (group ^ 1)) + r
                out_ref[pl.ds(row, 1), :cap] = weights[r][side][:, d * cap : (d + 1) * cap]


def finish_kernel(chips, cap, groups, strata_dev, ids_ref, got_ref, out_ref):
    rows = ids_ref.shape[1]
    group = lax.axis_index("grp")
    got = got_ref[...]
    row_of = lax.broadcasted_iota(jnp.int32, got.shape, 0) % 4
    total = jnp.sum(jnp.where(row_of == 2, got, 0.0), axis=0, keepdims=True)[:, :1]
    ids = ids_ref[...]
    weight = jnp.zeros((1, rows), jnp.float32)
    for i in range(chips):
        owner = ((group % 2) * chips + i) * groups + (group ^ 1)
        for r in range(2):
            shard = 2 * i + r
            start = first_row(ids, shard, strata_dev, rows - cap)
            part = got_ref[pl.ds(4 * owner + r, 1), :]
            part = jnp.broadcast_to(jnp.concatenate([part] * (rows // LANES), axis=1), (8, rows))
            part = pltpu.roll(part, start, axis=1)[:1, :]
            mine = (ids >= shard * strata_dev) & (ids < (shard + 1) * strata_dev)
            weight = jnp.where(mine, part, weight)
    out_ref[...] = weight * (float(rows * 2 * chips * groups) / total)


def body(embeddings, strata, centroids):
    shards, groups = lax.axis_size("blk"), lax.axis_size("grp")
    chips = shards // 2
    rows, width = embeddings.shape[1:]
    strata_dev = centroids.shape[1]
    cap = 2 * rows // shards
    depth = width // LANES * 2 * cap + TAIL
    each = chips * cap
    every = [(b, g) for b in range(shards) for g in range(groups)]
    kind_a = [(b, g) for b, g in every if b // chips == g % 2]
    kind_b = [(b, g) for b, g in every if b // chips != g % 2]

    def send(array, pairs):
        return lax.ppermute(
            array, AXES, [(b * groups + g, to_b * groups + to_g) for (b, g), (to_b, to_g) in pairs]
        )

    def pack(ids, rows_in):
        return pl.pallas_call(
            functools.partial(pack_kernel, chips, cap, strata_dev),
            out_shape=[jax.ShapeDtypeStruct((depth, LANES), jnp.bfloat16)] * chips,
            in_specs=[VMEM, VMEM],
            out_specs=[VMEM] * chips,
            scratch_shapes=[pltpu.VMEM((rows, width), jnp.bfloat16)],
            name="pack",
        )(ids, rows_in)

    own_rows = embeddings[0]
    swap = [((b, g), (b ^ chips, g ^ 1)) for b, g in kind_b]
    far_rows, far_ids = send(own_rows, swap), send(strata, swap)
    cents = [
        send(
            centroids[0],
            [((b, g), ((g % 2) * chips + b // 2, g ^ 1)) for b, g in every if b % 2 == parity],
        )
        for parity in range(2)
    ]
    blocks_a = [
        send(block, [((b, g), (b ^ d, g ^ 1)) for b, g in kind_a])
        for d, block in enumerate(pack(strata, own_rows))
    ]
    held = pl.pallas_call(
        functools.partial(early_kernel, chips, cap),
        out_shape=[
            jax.ShapeDtypeStruct((2 * each, width), jnp.bfloat16),
            jax.ShapeDtypeStruct((2 * each, LANES), jnp.float32),
            jax.ShapeDtypeStruct((2 * strata_dev, width), jnp.bfloat16),
            jax.ShapeDtypeStruct((8, each), jnp.float32),
        ],
        in_specs=[VMEM] * (chips + 2),
        out_specs=[VMEM] * 4,
        name="early",
    )(*cents, *blocks_a)
    blocks_b = [
        block if d == 0 else send(block, [((b, g), (b ^ d, g)) for b, g in kind_b])
        for d, block in enumerate(pack(far_ids, far_rows))
    ]
    sent = pl.pallas_call(
        functools.partial(late_kernel, chips, cap, groups),
        out_shape=jax.ShapeDtypeStruct((shards * groups * 4, LANES), jnp.float32),
        in_specs=[VMEM] * (chips + 4),
        out_specs=VMEM,
        scratch_shapes=[
            pltpu.VMEM((2 * each, width), jnp.bfloat16),
            pltpu.VMEM((2 * each, LANES), jnp.float32),
        ],
        name="late",
    )(*held, *blocks_b)
    got = lax.all_to_all(
        sent.reshape(shards * groups, 4, LANES), AXES, 0, 0, tiled=True
    ).reshape(shards * groups * 4, LANES)
    return pl.pallas_call(
        functools.partial(finish_kernel, chips, cap, groups, strata_dev),
        out_shape=jax.ShapeDtypeStruct((1, rows), jnp.float32),
        in_specs=[VMEM, VMEM],
        out_specs=VMEM,
        name="finish",
    )(strata, got)


def solution(mesh):
    placed = (P("grp", "blk", None), P("grp", "blk"), P("grp", "blk", None))
    return jax.shard_map(
        body, mesh=mesh, in_specs=placed, out_specs=P("grp", "blk"), check_vma=False
    )
```

time: 198 us -> 86 us (0.43)
  blocking collectives: 98.8 us -> 15 us
  waiting for transfers between devices: 66.4 us -> 9.1 us
  starting transfers between devices: 0.01 us -> 35.2 us
  Pallas kernels: 0 us -> 24.7 us
  between operations: 14.1 us -> 0.23 us
  matrix products: 10.9 us -> 0 us
  other arithmetic: 6.97 us -> 0 us
    all_gather x1 -> x0, waiting for transfers between devices: 66.4 us -> none  [body(): guest_rows = lax.all_gather(own_units, 'blk', axis=0, tiled=True)]
    all_gather x2 -> x0, blocking collectives: 60 us -> none  [the longest x1 31.6 us: body(): cent_units = lax.all_gather(cent_local, 'blk', axis=0, tiled=True)]
    psum x1 -> x0, blocking collectives: 38.8 us -> none  [body(): total = lax.psum(jnp.sum(weights), ('blk', 'grp'))]
    ppermute x0 -> x11, starting transfers between devices: none -> 35.2 us  [send(): lax.ppermute(array, AXES, [(b * groups + g, to_b * groups + to_g) for (b,...]
    pallas_call x0 -> x5, Pallas kernels: none -> 24.7 us  [the longest x1 9.29 us: body(): pl.pallas_call(functools.partial(late_kernel, chips, cap, groups), out_sh...]
    all_to_all x0 -> x1, blocking collectives: none -> 15 us  [body(): lax.all_to_all(sent.reshape(shards * groups, 4, LANES), AXES, 0, 0, tiled...]
    dot_general x2 -> x0, matrix products: 10.9 us -> none  [the longest x1 9.08 us: dense_sums(): lax.dot_general(query_rows, key_rows, (((1,), (1,)), ((), ())), preferred...]
    ppermute x0 -> x11, waiting for transfers between devices: none -> 9.1 us  [send(): lax.ppermute(array, AXES, [(b * groups + g, to_b * groups + to_g) for (b,...]
  transfers between devices with their start and end apart: 1 -> 11, of which waited for: 1 -> 1; matrix products, arithmetic and copies ran while one was open for 2% -> 0% of each run, Pallas kernels for 0% -> 16%
where the time goes in v2:
time: 86 us; the launch traced here: 85.5 us
  starting transfers between devices  35.2 us (41%)
  Pallas kernels  24.7 us (29%)
  blocking collectives  15 us (17%)
  waiting for transfers between devices  9.1 us (11%)
  local copies, waits for them, and re-layouts  1.14 us (1%)
    ppermute x11, starting transfers between devices, send(): lax.ppermute(array, AXES, [(b * groups + g, to_b * groups + to_g) for (b,...  35.2 us
    all_to_all x1, blocking collectives, body(): lax.all_to_all(sent.reshape(shards * groups, 4, LANES), AXES, 0, 0, tiled...  15 us
    pallas_call x1, Pallas kernels, body(): pl.pallas_call(functools.partial(late_kernel, chips, cap, groups), out_sh...  9.29 us
    ppermute x11, waiting for transfers between devices, send(): lax.ppermute(array, AXES, [(b * groups + g, to_b * groups + to_g) for (b,...  9.1 us
    pallas_call x2, Pallas kernels, pack(): pl.pallas_call(functools.partial(pack_kernel, chips, cap, strata_dev), ou...  8.19 us
    pallas_call x1, Pallas kernels, body(): pl.pallas_call(functools.partial(early_kernel, chips, cap), out_shape=[ja...  5.6 us
  transfers between devices with their start and end apart: 11, of which 1 were waited for; matrix products, arithmetic and copies ran while one was open for 0% of the time, Pallas kernels for 16%

profile of v2, /device:TPU:0, one launch (start us, length us, event | category | flops | bytes accessed | tf_op | source)
XLA Modules:
  0.0 85.5 jit_solution(14209259921241510310)
XLA Ops:
  0.0 0.7 collective-permute-start.7
  0.7 4.1 %pack.2 = (bf16[2064,128]{1,0:T(8,128)(2,1)}, bf16[2064,128]{1,0:T(8,128)(2,1)}, bf16[2064,128]{1,0:T(8,128)(2,1)}, bf16[2064,128]{1,0:T(8,128)(2,1)}) custom-call(s32[1,512]{1,0:T(1,128)} %ids_ref.3, bf16[512,1024]{1,0:T(8,128)(2,1)} %bitcast.5), custom_call_target="tpu_custom_call" | custom-call | tf_op jit(solution)/shard_map/pack/pallas_call | solution.py:226
  4.8 7.3 %collective-permute-start.2 = (bf16[2064,128]{1,0:T(8,128)(2,1)}, bf16[2064,128]{1,0:T(8,128)(2,1)S(1)}, u32[]{:S(2)}, u32[]{:S(2)}) collective-permute-start(bf16[2064,128]{1,0:T(8,128)(2,1)} %get-tuple-element.17), channel_id=1, source_target_pairs={{0,1},{2,3},{4,5},{6,7},{8,9},{10,11},{12,13},{14,15},{17,16},{19,... | collective-permute-start | bytes 1585160 | tf_op jit(solution)/shard_map/ppermute | solution.py:221
  12.1 2.4 %collective-permute-start.3 = (bf16[2064,128]{1,0:T(8,128)(2,1)}, bf16[2064,128]{1,0:T(8,128)(2,1)S(1)}, u32[]{:S(2)}, u32[]{:S(2)}) collective-permute-start(bf16[2064,128]{1,0:T(8,128)(2,1)} %get-tuple-element.18), channel_id=1, source_target_pairs={{0,5},{2,7},{4,1},{6,3},{8,13},{10,15},{12,9},{14,11},{17,20},{19,... | collective-permute-start | bytes 1585160 | tf_op jit(solution)/shard_map/ppermute | solution.py:221
  14.5 0.7 collective-permute-start.6
  15.2 1.4 %collective-permute-start = (bf16[16,1024]{1,0:T(8,128)(2,1)}, bf16[16,1024]{1,0:T(8,128)(2,1)S(1)}, u32[]{:S(2)}, u32[]{:S(2)}) collective-permute-start(bf16[16,1024]{1,0:T(8,128)(2,1)} %bitcast.8), channel_id=1, source_target_pairs={{0,1},{1,16},{2,3},{3,18},{8,5},{9,20},{10,7},{11,22},{16,9},{17,2... | collective-permute-start | bytes 98312 | tf_op jit(solution)/shard_map/ppermute | solution.py:221
  16.6 0.0 collective-permute-done.6.ids_ref
  16.6 0.0 copy-start.9
  16.6 0.7 collective-permute-start.1
  17.3 0.0 collective-permute-done.7.rows_ref
  17.3 16.7 %collective-permute-start.4 = (bf16[2064,128]{1,0:T(8,128)(2,1)}, bf16[2064,128]{1,0:T(8,128)(2,1)S(1)}, u32[]{:S(2)}, u32[]{:S(2)}) collective-permute-start(bf16[2064,128]{1,0:T(8,128)(2,1)} %get-tuple-element.19), channel_id=1, source_target_pairs={{0,9},{2,11},{4,13},{6,15},{8,1},{10,3},{12,5},{14,7},{17,24},{19,... | collective-permute-start | bytes 1585160 | tf_op jit(solution)/shard_map/ppermute | solution.py:221
  34.0 4.1 %pack.3 = (bf16[2064,128]{1,0:T(8,128)(2,1)}, bf16[2064,128]{1,0:T(8,128)(2,1)}, bf16[2064,128]{1,0:T(8,128)(2,1)}, bf16[2064,128]{1,0:T(8,128)(2,1)}) custom-call(s32[1,512]{1,0:T(1,128)} %copy-done.9, bf16[512,1024]{1,0:T(8,128)(2,1)} %copy-done), custom_call_target="tpu_custom_call" | custom-call | tf_op jit(solution)/shard_map/pack/pallas_call | solution.py:226
  38.2 0.0 collective-permute-done.cent0_ref
  38.2 3.3 %collective-permute-start.5 = (bf16[2064,128]{1,0:T(8,128)(2,1)}, bf16[2064,128]{1,0:T(8,128)(2,1)}, u32[]{:S(2)}, u32[]{:S(2)}) collective-permute-start(bf16[2064,128]{1,0:T(8,128)(2,1)} %get-tuple-element.20), channel_id=1, source_target_pairs={{0,13},{2,15},{4,9},{6,11},{8,5},{10,7},{12,1},{14,3},{17,28},{19,... | collective-permute-start | bytes 1585160 | tf_op jit(solution)/shard_map/ppermute | solution.py:221
  41.5 0.0 collective-permute-done.1.cent1_ref
  41.5 0.7 collective-permute-start.10
  42.2 0.0 collective-permute-done.2.rest_0_
  42.2 0.7 collective-permute-start.8
  42.9 0.0 collective-permute-done.3.rest_1_
  42.9 0.7 collective-permute-start.9
  43.6 0.0 collective-permute-done.4.rest_2_
  43.6 9.1 %collective-permute-done.5.rest_3_ = bf16[2064,128]{1,0:T(8,128)(2,1)} collective-permute-done((bf16[2064,128]{1,0:T(8,128)(2,1)}, bf16[2064,128]{1,0:T(8,128)(2,1)}, u32[]{:S(2)}, u32[]{:S(2)}) %collective-permute-start.5) | collective-permute-done | bytes 528416 | tf_op jit(solution)/shard_map/ppermute | solution.py:221
  52.7 5.6 %early.1 = (bf16[1024,1024]{1,0:T(8,128)(2,1)}, f32[1024,128]{1,0:T(8,128)}, bf16[32,1024]{1,0:T(8,128)(2,1)}, f32[8,512]{1,0:T(8,128)}) custom-call(bf16[16,1024]{1,0:T(8,128)(2,1)} %copy-done.7, bf16[16,1024]{1,0:T(8,128)(2,1)} %copy-done.8, bf16[2064,128]{1,0:T(8,128)(2,1)} %copy-done.4, bf16[2064,128]{1,0:T(8,128)(2,1)} %copy-done.5, ...), custom_call_target="tpu_custom_call" | custom-call | tf_op jit(solution)/shard_map/early/pallas_call | solution.py:249
  58.3 0.0 collective-permute-done.10.rest_3_
  58.3 0.0 collective-permute-done.8.rest_1_
  58.3 0.0 collective-permute-done.9.rest_2_
  58.4 0.7 copy-done.1
  59.1 0.2 copy-done.2
  59.3 0.2 copy-done.3
  59.5 9.3 %late.1 = f32[128,128]{1,0:T(8,128)} custom-call(bf16[1024,1024]{1,0:T(8,128)(2,1)} %get-tuple-element.21.units_a, f32[1024,128]{1,0:T(8,128)} %get-tuple-element.22.col_a, bf16[32,1024]{1,0:T(8,128)(2,1)} %get-tuple-element.23.cents, f32[8,512]{1,0:T(8,128)} %get-tuple-element.24.facts, bf16[2064,128]{1,0:T(8,128)(2,1)} %get-tuple-element.25.rest_0_, ...), custom_call_target="tpu_custom_call" | custom-call | tf_op jit(solution)/shard_map/late/pallas_call | solution.py:265
  68.8 15.0 %all_to_all.5 = f32[32,4,128]{2,1,0:T(4,128)} all-to-all(f32[32,4,128]{2,1,0:T(4,128)} %bitcast.6), channel_id=1, replica_groups=mesh['blk'=8,'grp'=4] {'blk','grp'}, dimensions={0} | all-to-all | bytes 131072 | tf_op jit(solution)/shard_map/all_to_all | solution.py:276
  83.8 1.7 %finish.1 = f32[1,512]{1,0:T(1,128)} custom-call(s32[1,512]{1,0:T(1,128)} %ids_ref.3, f32[128,128]{1,0:T(8,128)} %bitcast.7), custom_call_target="tpu_custom_call" | custom-call | tf_op jit(solution)/shard_map/finish/pallas_call | solution.py:279
  (16 shorter events, 0.0 us)
Async XLA Ops:
  0.0 17.3 %collective-permute-start.7 = (bf16[512,1024]{1,0:T(8,128)(2,1)}, bf16[512,1024]{1,0:T(8,128)(2,1)S(1)}, u32[]{:S(2)}, u32[]{:S(2)}) collective-permute-start(bf16[512,1024]{1,0:T(8,128)(2,1)} %bitcast.4), channel_id=1, source_target_pairs={{1,16},{3,18},{5,20},{7,22},{9,24},{11,26},{13,28},{15,30},{16,1},... | collective-permute-start | bytes 3145736 | tf_op jit(solution)/shard_map/ppermute | solution.py:221
  4.8 37.3 %collective-permute-start.2 = (bf16[2064,128]{1,0:T(8,128)(2,1)}, bf16[2064,128]{1,0:T(8,128)(2,1)S(1)}, u32[]{:S(2)}, u32[]{:S(2)}) collective-permute-start(bf16[2064,128]{1,0:T(8,128)(2,1)} %get-tuple-element.17), channel_id=1, source_target_pairs={{0,1},{2,3},{4,5},{6,7},{8,9},{10,11},{12,13},{14,15},{17,16},{19,... | collective-permute-start | bytes 1585160 | tf_op jit(solution)/shard_map/ppermute | solution.py:221
  12.1 30.8 %collective-permute-start.3 = (bf16[2064,128]{1,0:T(8,128)(2,1)}, bf16[2064,128]{1,0:T(8,128)(2,1)S(1)}, u32[]{:S(2)}, u32[]{:S(2)}) collective-permute-start(bf16[2064,128]{1,0:T(8,128)(2,1)} %get-tuple-element.18), channel_id=1, source_target_pairs={{0,5},{2,7},{4,1},{6,3},{8,13},{10,15},{12,9},{14,11},{17,20},{19,... | collective-permute-start | bytes 1585160 | tf_op jit(solution)/shard_map/ppermute | solution.py:221
  14.5 2.1 %collective-permute-start.6 = (s32[1,512]{1,0:T(1,128)}, s32[1,512]{1,0:T(1,128)S(1)}, u32[]{:S(2)}, u32[]{:S(2)}) collective-permute-start(s32[1,512]{1,0:T(1,128)} %ids_ref.3), channel_id=1, source_target_pairs={{1,16},{3,18},{5,20},{7,22},{9,24},{11,26},{13,28},{15,30},{16,1},... | collective-permute-start | bytes 6152 | tf_op jit(solution)/shard_map/ppermute | solution.py:221
  15.2 23.0 %collective-permute-start = (bf16[16,1024]{1,0:T(8,128)(2,1)}, bf16[16,1024]{1,0:T(8,128)(2,1)S(1)}, u32[]{:S(2)}, u32[]{:S(2)}) collective-permute-start(bf16[16,1024]{1,0:T(8,128)(2,1)} %bitcast.8), channel_id=1, source_target_pairs={{0,1},{1,16},{2,3},{3,18},{8,5},{9,20},{10,7},{11,22},{16,9},{17,2... | collective-permute-start | bytes 98312 | tf_op jit(solution)/shard_map/ppermute | solution.py:221
  16.6 17.4 %copy-start.9 = (s32[1,512]{1,0:T(1,128)}, s32[1,512]{1,0:T(1,128)S(1)}, u32[]{:S(2)}) copy-start(s32[1,512]{1,0:T(1,128)S(1)} %collective-permute-done.6.ids_ref) | copy-start | bytes 6148
  16.6 24.8 %collective-permute-start.1 = (bf16[16,1024]{1,0:T(8,128)(2,1)}, bf16[16,1024]{1,0:T(8,128)(2,1)S(1)}, u32[]{:S(2)}, u32[]{:S(2)}) collective-permute-start(bf16[16,1024]{1,0:T(8,128)(2,1)} %bitcast.9), channel_id=1, source_target_pairs={{4,1},{5,16},{6,3},{7,18},{12,5},{13,20},{14,7},{15,22},{20,9},{21... | collective-permute-start | bytes 98312 | tf_op jit(solution)/shard_map/ppermute | solution.py:221
  17.3 16.7 %copy-start = (bf16[512,1024]{1,0:T(8,128)(2,1)}, bf16[512,1024]{1,0:T(8,128)(2,1)S(1)}, u32[]{:S(2)}) copy-start(bf16[512,1024]{1,0:T(8,128)(2,1)S(1)} %collective-permute-done.7.rows_ref) | copy-start | bytes 3145732
  17.3 26.3 %collective-permute-start.4 = (bf16[2064,128]{1,0:T(8,128)(2,1)}, bf16[2064,128]{1,0:T(8,128)(2,1)S(1)}, u32[]{:S(2)}, u32[]{:S(2)}) collective-permute-start(bf16[2064,128]{1,0:T(8,128)(2,1)} %get-tuple-element.19), channel_id=1, source_target_pairs={{0,9},{2,11},{4,13},{6,15},{8,1},{10,3},{12,5},{14,7},{17,24},{19,... | collective-permute-start | bytes 1585160 | tf_op jit(solution)/shard_map/ppermute | solution.py:221
  38.2 14.5 %copy-start.7 = (bf16[16,1024]{1,0:T(8,128)(2,1)}, bf16[16,1024]{1,0:T(8,128)(2,1)S(1)}, u32[]{:S(2)}) copy-start(bf16[16,1024]{1,0:T(8,128)(2,1)S(1)} %collective-permute-done.cent0_ref) | copy-start | bytes 98308
  38.2 14.5 %collective-permute-start.5 = (bf16[2064,128]{1,0:T(8,128)(2,1)}, bf16[2064,128]{1,0:T(8,128)(2,1)}, u32[]{:S(2)}, u32[]{:S(2)}) collective-permute-start(bf16[2064,128]{1,0:T(8,128)(2,1)} %get-tuple-element.20), channel_id=1, source_target_pairs={{0,13},{2,15},{4,9},{6,11},{8,5},{10,7},{12,1},{14,3},{17,28},{19,... | collective-permute-start | bytes 1585160 | tf_op jit(solution)/shard_map/ppermute | solution.py:221
  41.5 11.2 %copy-start.8 = (bf16[16,1024]{1,0:T(8,128)(2,1)}, bf16[16,1024]{1,0:T(8,128)(2,1)S(1)}, u32[]{:S(2)}) copy-start(bf16[16,1024]{1,0:T(8,128)(2,1)S(1)} %collective-permute-done.1.cent1_ref) | copy-start | bytes 98308
  41.5 16.9 %collective-permute-start.10 = (bf16[2064,128]{1,0:T(8,128)(2,1)}, bf16[2064,128]{1,0:T(8,128)(2,1)S(1)}, u32[]{:S(2)}, u32[]{:S(2)}) collective-permute-start(bf16[2064,128]{1,0:T(8,128)(2,1)} %get-tuple-element.28), channel_id=1, source_target_pairs={{1,13},{3,15},{5,9},{7,11},{9,5},{11,7},{13,1},{15,3},{16,28},{18,... | collective-permute-start | bytes 1585160 | tf_op jit(solution)/shard_map/ppermute | solution.py:221
  42.2 10.5 %copy-start.4 = (bf16[2064,128]{1,0:T(8,128)(2,1)}, bf16[2064,128]{1,0:T(8,128)(2,1)S(1)}, u32[]{:S(2)}) copy-start(bf16[2064,128]{1,0:T(8,128)(2,1)S(1)} %collective-permute-done.2.rest_0_) | copy-start | bytes 1585156
  42.2 16.2 %collective-permute-start.8 = (bf16[2064,128]{1,0:T(8,128)(2,1)}, bf16[2064,128]{1,0:T(8,128)(2,1)S(1)}, u32[]{:S(2)}, u32[]{:S(2)}) collective-permute-start(bf16[2064,128]{1,0:T(8,128)(2,1)} %get-tuple-element.26), channel_id=1, source_target_pairs={{1,5},{3,7},{5,1},{7,3},{9,13},{11,15},{13,9},{15,11},{16,20},{18,... | collective-permute-start | bytes 1585160 | tf_op jit(solution)/shard_map/ppermute | solution.py:221
  42.9 9.8 %copy-start.5 = (bf16[2064,128]{1,0:T(8,128)(2,1)}, bf16[2064,128]{1,0:T(8,128)(2,1)S(1)}, u32[]{:S(2)}) copy-start(bf16[2064,128]{1,0:T(8,128)(2,1)S(1)} %collective-permute-done.3.rest_1_) | copy-start | bytes 1585156
  42.9 15.5 %collective-permute-start.9 = (bf16[2064,128]{1,0:T(8,128)(2,1)}, bf16[2064,128]{1,0:T(8,128)(2,1)S(1)}, u32[]{:S(2)}, u32[]{:S(2)}) collective-permute-start(bf16[2064,128]{1,0:T(8,128)(2,1)} %get-tuple-element.27), channel_id=1, source_target_pairs={{1,9},{3,11},{5,13},{7,15},{9,1},{11,3},{13,5},{15,7},{16,24},{18,... | collective-permute-start | bytes 1585160 | tf_op jit(solution)/shard_map/ppermute | solution.py:221
  43.6 9.1 %copy-start.6 = (bf16[2064,128]{1,0:T(8,128)(2,1)}, bf16[2064,128]{1,0:T(8,128)(2,1)S(1)}, u32[]{:S(2)}) copy-start(bf16[2064,128]{1,0:T(8,128)(2,1)S(1)} %collective-permute-done.4.rest_2_) | copy-start | bytes 1585156
  58.3 0.8 copy-start.1
  58.3 1.0 %copy-start.2 = (bf16[2064,128]{1,0:T(8,128)(2,1)}, bf16[2064,128]{1,0:T(8,128)(2,1)S(1)}, u32[]{:S(2)}) copy-start(bf16[2064,128]{1,0:T(8,128)(2,1)S(1)} %collective-permute-done.8.rest_1_) | copy-start | bytes 1585156
  58.4 1.1 %copy-start.3 = (bf16[2064,128]{1,0:T(8,128)(2,1)}, bf16[2064,128]{1,0:T(8,128)(2,1)S(1)}, u32[]{:S(2)}) copy-start(bf16[2064,128]{1,0:T(8,128)(2,1)S(1)} %collective-permute-done.9.rest_2_) | copy-start | bytes 1585156

commit v3 on v1

v3 whole, which is shorter than its diff:
```python
import functools
import math

import jax
import jax.numpy as jnp
from jax import lax
from jax.experimental import pallas as pl
from jax.experimental.pallas import tpu as pltpu
from jax.sharding import PartitionSpec as P


base_term = 0.05
epsilon = 1e-06
LANES = 128
TAIL = 16
AXES = ("blk", "grp")

VMEM = pl.BlockSpec(memory_space=pltpu.VMEM)
ANY = pl.BlockSpec(memory_space=pl.ANY)


def params(mib):
    return pltpu.CompilerParams(vmem_limit_bytes=mib << 20)


def unit_values(rows):
    values = rows.astype(jnp.float32)
    mean = jnp.mean(values * values, axis=-1, keepdims=True)
    scaling = lax.rsqrt(mean + epsilon) / math.sqrt(rows.shape[-1])
    return (values * scaling).astype(jnp.bfloat16)


def across(left, right):
    return lax.dot_general(
        left, right, (((1,), (1,)), ((), ())), preferred_element_type=jnp.float32
    )


def pack_kernel(peers, cap, strata_dev, ids_any, rows_any, *rest):
    outs, (rows_ref, ids_ref, held, pick, sems) = rest[:peers], rest[peers:]
    rows, width = rows_ref.shape
    me = lax.axis_index("blk")
    pieces = 4
    step = rows // pieces
    loads = [pltpu.make_async_copy(ids_any, ids_ref, sems.at[pieces])]
    for i in range(pieces):
        at = pl.ds(i * step, step)
        loads.append(pltpu.make_async_copy(rows_any.at[at, :], rows_ref.at[at, :], sems.at[i]))
    for load in loads:
        load.start()
    loads[0].wait()
    ids = ids_ref[...].astype(jnp.float32)
    number = lax.broadcasted_iota(jnp.int32, (peers, 1), 0)
    lowest = ((me ^ number) * strata_dev).astype(jnp.float32)
    begin = jnp.sum((ids < lowest).astype(jnp.float32), axis=1, keepdims=True)
    start = jnp.minimum(begin, float(rows - cap))
    number = lax.broadcasted_iota(jnp.int32, (peers * strata_dev, 1), 0)
    stratum = (me ^ (number // strata_dev)) * strata_dev + number % strata_dev
    ends = jnp.sum((ids <= stratum.astype(jnp.float32)).astype(jnp.float32), axis=1, keepdims=True)
    slot = lax.broadcasted_iota(jnp.int32, (cap, rows), 0).astype(jnp.float32)
    row = lax.broadcasted_iota(jnp.int32, (cap, rows), 1).astype(jnp.float32)
    ahead = row - slot
    lane = lax.broadcasted_iota(jnp.int32, (1, LANES), 1).astype(jnp.float32)
    for k, out in enumerate(outs):
        first = start[k : k + 1, :]
        pick[k * cap : (k + 1) * cap, :] = (ahead == first).astype(jnp.bfloat16)
        at = lane + first
        passed = (ends[k * strata_dev : (k + 1) * strata_dev, :] <= at).astype(jnp.float32)
        local = jnp.where(
            at >= begin[k : k + 1, :], jnp.sum(passed, axis=0, keepdims=True), float(strata_dev)
        )
        out[width // LANES * cap :, :] = jnp.broadcast_to(local, (TAIL, LANES)).astype(jnp.bfloat16)
    for i in range(pieces):
        loads[1 + i].wait()
        held[i * step : (i + 1) * step, :] = unit_values(rows_ref[i * step : (i + 1) * step, :])
    wide = 2 * LANES
    for c in range(width // wide):
        runs = jnp.dot(
            pick[...], held[:, c * wide : (c + 1) * wide], preferred_element_type=jnp.float32
        ).astype(jnp.bfloat16)
        for k, out in enumerate(outs):
            for part in range(2):
                at = (2 * c + part) * cap
                out[at : at + cap, :] = runs[
                    k * cap : (k + 1) * cap, part * LANES : (part + 1) * LANES
                ]


def own_kernel(order, cap, groups, cent_ref, *rest):
    peers = len(order)
    blocks, (out_ref, units, id_col) = rest[:peers], rest[peers:]
    slots, width = units.shape
    strata_dev = cent_ref.shape[0]
    me, group = lax.axis_index("blk"), lax.axis_index("grp")

    id_rows = []
    for k, block in enumerate(blocks):
        for c in range(width // LANES):
            units[k * cap : (k + 1) * cap, c * LANES : (c + 1) * LANES] = block[
                c * cap : (c + 1) * cap, :
            ]
        ids = block[width // LANES * cap :, :].astype(jnp.float32)[:1, :]
        ids = jnp.where(ids < float(strata_dev), ids, -1.0)
        id_rows.append(ids[:, :cap])
        wide = jnp.broadcast_to(ids, (LANES, LANES)).T
        id_col[k * cap : (k + 1) * cap, :] = wide[:cap, :]
    id_row = jnp.concatenate(id_rows, axis=1)
    real = id_row >= 0.0
    id_key = jnp.where(real, id_row, -2.0)

    tile = 512
    sums = jnp.zeros((8, slots), jnp.float32)
    everything = units[...]
    for t in range(slots // tile):
        scores = across(units[t * tile : (t + 1) * tile, :], everything)
        kernel = jnp.exp((scores - 1.0) * 4.0)
        same = (
            jnp.concatenate([id_col[t * tile : (t + 1) * tile, :]] * (slots // LANES), axis=1)
            == id_key
        )
        kernel = jnp.where(same, kernel, 0.0)
        sums = sums + jnp.sum(kernel.reshape(tile // 8, 8, slots), axis=0)
    density = jnp.sum(sums, axis=0, keepdims=True)

    near = across(unit_values(cent_ref[...]), everything)
    which = lax.broadcasted_iota(jnp.int32, near.shape, 0).astype(jnp.float32)
    picked = jnp.sum(jnp.where(which == id_row, near, 0.0), axis=0, keepdims=True)
    weight = jnp.where(
        real, ((1.0 - picked) + base_term) / jnp.where(real, density, 1.0), 0.0
    )
    out_ref[...] = jnp.broadcast_to(jnp.sum(weight, axis=1, keepdims=True), out_ref.shape)
    for i, k in enumerate(order):
        row = 2 * ((me ^ k) * groups + group)
        out_ref[pl.ds(row, 1), :cap] = weight[:, i * cap : (i + 1) * cap]


def finish_kernel(peers, cap, groups, strata_dev, ids_ref, got_ref, out_ref):
    rows = ids_ref.shape[1]
    group = lax.axis_index("grp")
    got = got_ref[...]
    odd = lax.broadcasted_iota(jnp.int32, got.shape, 0) % 2
    total = jnp.sum(jnp.where(odd == 1, got, 0.0), axis=0, keepdims=True)[:, :1]
    ids = ids_ref[...]
    weight = jnp.zeros((1, rows), jnp.float32)
    for owner in range(peers):
        begin = jnp.sum((ids < owner * strata_dev).astype(jnp.int32))
        start = jnp.minimum(begin, rows - cap)
        part = got_ref[pl.ds(2 * (owner * groups + group), 1), :]
        part = jnp.broadcast_to(jnp.concatenate([part] * (rows // LANES), axis=1), (8, rows))
        part = pltpu.roll(part, start, axis=1)[:1, :]
        mine = (ids >= owner * strata_dev) & (ids < (owner + 1) * strata_dev)
        weight = jnp.where(mine, part, weight)
    out_ref[...] = weight * (float(rows * peers * groups) / total)


def body(embeddings, strata, centroids):
    peers, groups = lax.axis_size("blk"), lax.axis_size("grp")
    rows, width = embeddings.shape[1:]
    strata_dev = centroids.shape[1]
    cap = 2 * rows // peers
    depth = width // LANES * cap + TAIL

    blocks = [*pl.pallas_call(
        functools.partial(pack_kernel, peers, cap, strata_dev),
        out_shape=[pltpu.VMEM((depth, LANES), jnp.bfloat16)] * peers,
        in_specs=[ANY, ANY],
        out_specs=[VMEM] * peers,
        scratch_shapes=[
            pltpu.VMEM((rows, width), jnp.bfloat16),
            pltpu.VMEM((1, rows), jnp.int32),
            pltpu.VMEM((rows, width), jnp.bfloat16),
            pltpu.VMEM((peers * cap, rows), jnp.bfloat16),
            pltpu.SemaphoreType.DMA((5,)),
        ],
        compiler_params=params(58),
        name="pack",
    )(strata, embeddings[0])]
    far = range(peers // 2, peers)
    order = [0, 1, 2, *far, *range(3, peers // 2)]
    blocks = [
        blocks[k] if k == 0 else lax.ppermute(blocks[k], "blk", [(i, i ^ k) for i in range(peers)])
        for k in order
    ]
    sent = pl.pallas_call(
        functools.partial(own_kernel, order, cap, groups),
        out_shape=jax.ShapeDtypeStruct((peers * groups * 2, LANES), jnp.float32),
        in_specs=[VMEM] * (peers + 1),
        out_specs=VMEM,
        scratch_shapes=[
            pltpu.VMEM((peers * cap, width), jnp.bfloat16),
            pltpu.VMEM((peers * cap, LANES), jnp.float32),
        ],
        compiler_params=params(24),
        name="own",
    )(centroids[0], *blocks)
    got = lax.all_to_all(
        sent.reshape(peers * groups, 2, LANES), AXES, 0, 0, tiled=True
    ).reshape(peers * groups * 2, LANES)
    return pl.pallas_call(
        functools.partial(finish_kernel, peers, cap, groups, strata_dev),
        out_shape=jax.ShapeDtypeStruct((1, rows), jnp.float32),
        in_specs=[VMEM, VMEM],
        out_specs=VMEM,
        compiler_params=params(8),
        name="finish",
    )(strata, got)


def solution(mesh):
    placed = (P("grp", "blk", None), P("grp", "blk"), P("grp", "blk", None))
    return jax.shard_map(
        body, mesh=mesh, in_specs=placed, out_specs=P("grp", "blk"), check_vma=False
    )
```

time: 78.4 us -> 70.9 us (0.904)
  Pallas kernels: 11.1 us -> 6.81 us
  waiting for transfers between devices: 31.2 us -> 29.1 us
  local copies, waits for them, and re-layouts: 0.89 us -> 0.01 us
    pallas_call x1, Pallas kernels: 5.45 us -> 3.29 us  [body(): pl.pallas_call(functools.partial(own_kernel, order, cap, groups), out_sha...]
    ppermute x7, waiting for transfers between devices: 31.2 us -> 29.1 us  [body(): lax.ppermute(blocks[k], 'blk', [(i, i ^ k) for i in range(peers)])]
    pallas_call x1, Pallas kernels: 4.1 us -> 2.71 us  [body(): pl.pallas_call(functools.partial(pack_kernel, peers, cap, strata_dev), ou...]
    unnamed x14 -> x4, local copies, waits for them, and re-layouts: 0.89 us -> 0.01 us
  transfers between devices with their start and end apart: 7 -> 7, of which waited for: 4 -> 3; matrix products, arithmetic and copies ran while one was open for 0% -> 0% of each run, Pallas kernels for 0% -> 0%
where the time goes in v3:
time: 70.9 us; the launch traced here: 70.8 us
  waiting for transfers between devices  29.1 us (41%)
  blocking collectives  20.6 us (29%)
  starting transfers between devices  14.2 us (20%)
  Pallas kernels  6.81 us (10%)
    ppermute x7, waiting for transfers between devices, body(): lax.ppermute(blocks[k], 'blk', [(i, i ^ k) for i in range(peers)])  29.1 us
    all_to_all x1, blocking collectives, body(): lax.all_to_all(sent.reshape(peers * groups, 2, LANES), AXES, 0, 0, tiled=...  20.6 us
    ppermute x7, starting transfers between devices, body(): lax.ppermute(blocks[k], 'blk', [(i, i ^ k) for i in range(peers)])  14.2 us
    pallas_call x1, Pallas kernels, body(): pl.pallas_call(functools.partial(own_kernel, order, cap, groups), out_sha...  3.29 us
    pallas_call x1, Pallas kernels, body(): pl.pallas_call(functools.partial(pack_kernel, peers, cap, strata_dev), ou...  2.71 us
  transfers between devices with their start and end apart: 7, of which 3 were waited for; matrix products, arithmetic and copies ran while one was open for 0% of the time, Pallas kernels for 0%

profile of v3, /device:TPU:0, one launch (start us, length us, event | category | flops | bytes accessed | tf_op | source)
XLA Modules:
  0.0 70.8 jit_solution(11402431138513508263)
XLA Ops:
  0.0 0.0 copy-start
  0.0 2.7 %pack.1 = (bf16[1040,128]{1,0:T(8,128)(2,1)S(1)}, bf16[1040,128]{1,0:T(8,128)(2,1)S(1)}, bf16[1040,128]{1,0:T(8,128)(2,1)S(1)}, bf16[1040,128]{1,0:T(8,128)(2,1)...) custom-call(s32[1,512]{1,0:T(1,128)} %ids_ref.1, ...), custom_call_target="tpu_custom_call" | custom-call | tf_op jit(solution)/shard_map/pack/pallas_call | solution.py:163
  2.7 3.0 %collective-permute-start = (bf16[1040,128]{1,0:T(8,128)(2,1)S(1)}, bf16[1040,128]{1,0:T(8,128)(2,1)S(1)}, u32[]{:S(2)}, u32[]{:S(2)}) collective-permute-start(bf16[1040,128]{1,0:T(8,128)(2,1)S(1)} %get-tuple-element.14), channel_id=1, source_target_pairs={{0,4},{4,0},{8,12},{12,8},{16,20},{20,16},{24,28},{28,24},{1,5},{5... | collective-permute-start | bytes 798728 | tf_op jit(solution)/shard_map/ppermute | solution.py:181
  5.8 1.6 %collective-permute-start.1 = (bf16[1040,128]{1,0:T(8,128)(2,1)S(1)}, bf16[1040,128]{1,0:T(8,128)(2,1)S(1)}, u32[]{:S(2)}, u32[]{:S(2)}) collective-permute-start(bf16[1040,128]{1,0:T(8,128)(2,1)S(1)} %get-tuple-element.15), channel_id=1, source_target_pairs={{0,8},{4,12},{8,0},{12,4},{16,24},{20,28},{24,16},{28,20},{1,9},{5... | collective-permute-start | bytes 798728 | tf_op jit(solution)/shard_map/ppermute | solution.py:181
  7.3 2.6 %collective-permute-start.2 = (bf16[1040,128]{1,0:T(8,128)(2,1)S(1)}, bf16[1040,128]{1,0:T(8,128)(2,1)S(1)}, u32[]{:S(2)}, u32[]{:S(2)}) collective-permute-start(bf16[1040,128]{1,0:T(8,128)(2,1)S(1)} %get-tuple-element.16), channel_id=1, source_target_pairs={{0,16},{4,20},{8,24},{12,28},{16,0},{20,4},{24,8},{28,12},{1,17},{... | collective-permute-start | bytes 798728 | tf_op jit(solution)/shard_map/ppermute | solution.py:181
  9.9 0.3 collective-permute-start.3
  10.2 2.5 %collective-permute-start.4 = (bf16[1040,128]{1,0:T(8,128)(2,1)S(1)}, bf16[1040,128]{1,0:T(8,128)(2,1)S(1)}, u32[]{:S(2)}, u32[]{:S(2)}) collective-permute-start(bf16[1040,128]{1,0:T(8,128)(2,1)S(1)} %get-tuple-element.18), channel_id=1, source_target_pairs={{0,24},{4,28},{8,16},{12,20},{16,8},{20,12},{24,0},{28,4},{1,25},{... | collective-permute-start | bytes 798728 | tf_op jit(solution)/shard_map/ppermute | solution.py:181
  12.7 0.0 collective-permute-done.rest_1_
  12.7 4.2 %collective-permute-start.5 = (bf16[1040,128]{1,0:T(8,128)(2,1)S(1)}, bf16[1040,128]{1,0:T(8,128)(2,1)S(1)}, u32[]{:S(2)}, u32[]{:S(2)}) collective-permute-start(bf16[1040,128]{1,0:T(8,128)(2,1)S(1)} %get-tuple-element.19), channel_id=1, source_target_pairs={{0,28},{4,24},{8,20},{12,16},{16,12},{20,8},{24,4},{28,0},{1,29},{... | collective-permute-start | bytes 798728 | tf_op jit(solution)/shard_map/ppermute | solution.py:181
  16.9 2.3 %collective-permute-done.1.rest_2_ = bf16[1040,128]{1,0:T(8,128)(2,1)S(1)} collective-permute-done((bf16[1040,128]{1,0:T(8,128)(2,1)S(1)}, bf16[1040,128]{1,0:T(8,128)(2,1)S(1)}, u32[]{:S(2)}, u32[]{:S(2)}) %collective-permute-start.1) | collective-permute-done | bytes 266272 | tf_op jit(solution)/shard_map/ppermute | solution.py:181
  19.2 0.0 collective-permute-start.6
  19.2 21.2 %collective-permute-done.2.rest_3_ = bf16[1040,128]{1,0:T(8,128)(2,1)S(1)} collective-permute-done((bf16[1040,128]{1,0:T(8,128)(2,1)S(1)}, bf16[1040,128]{1,0:T(8,128)(2,1)S(1)}, u32[]{:S(2)}, u32[]{:S(2)}) %collective-permute-start.2) | collective-permute-done | bytes 266272 | tf_op jit(solution)/shard_map/ppermute | solution.py:181
  40.4 5.6 %collective-permute-done.3.rest_4_ = bf16[1040,128]{1,0:T(8,128)(2,1)S(1)} collective-permute-done((bf16[1040,128]{1,0:T(8,128)(2,1)S(1)}, bf16[1040,128]{1,0:T(8,128)(2,1)S(1)}, u32[]{:S(2)}, u32[]{:S(2)}) %collective-permute-start.3) | collective-permute-done | bytes 266272 | tf_op jit(solution)/shard_map/ppermute | solution.py:181
  46.0 0.0 collective-permute-done.4.rest_5_
  46.0 0.0 collective-permute-done.5.rest_6_
  46.0 0.0 collective-permute-done.6.rest_7_
  46.0 0.0 copy-done
  46.1 3.3 %own.1 = f32[64,128]{1,0:T(8,128)S(1)} custom-call(bf16[16,1024]{1,0:T(8,128)(2,1)S(1)} %bitcast.6, bf16[1040,128]{1,0:T(8,128)(2,1)S(1)} %get-tuple-element.13.rest_0_, bf16[1040,128]{1,0:T(8,128)(2,1)S(1)} %collective-permute-done.rest_1_, bf16[1040,128]{1,0:T(8,128)(2,1)S(1)} %collective-permute-done.1.rest_2_, ...), custom_call_target="tpu_custom_call" | custom-call | tf_op jit(solution)/shard_map/own/pallas_call | solution.py:184
  49.3 0.0 copy-start.1
  49.3 20.6 %all_to_all.5 = f32[32,2,128]{2,1,0:T(2,128)S(1)} all-to-all(f32[32,2,128]{2,1,0:T(2,128)S(1)} %bitcast.4), channel_id=1, replica_groups=mesh['blk'=8,'grp'=4] {'blk','grp'}, dimensions={0} | all-to-all | bytes 65536 | tf_op jit(solution)/shard_map/all_to_all | solution.py:196
  70.0 0.0 copy-done.1
  70.0 0.8 %finish.1 = f32[1,512]{1,0:T(1,128)} custom-call(s32[1,512]{1,0:T(1,128)S(1)} %copy-done.1, f32[64,128]{1,0:T(8,128)S(1)} %bitcast.5), custom_call_target="tpu_custom_call" | custom-call | tf_op jit(solution)/shard_map/finish/pallas_call | solution.py:199
Async XLA Ops:
  0.0 46.0 %copy-start = (bf16[1,16,1024]{2,1,0:T(8,128)(2,1)S(1)}, bf16[1,16,1024]{2,1,0:T(8,128)(2,1)}, u32[]{:S(2)}) copy-start(bf16[1,16,1024]{2,1,0:T(8,128)(2,1)} %param.5) | copy-start | bytes 98308
  2.7 10.0 %collective-permute-start = (bf16[1040,128]{1,0:T(8,128)(2,1)S(1)}, bf16[1040,128]{1,0:T(8,128)(2,1)S(1)}, u32[]{:S(2)}, u32[]{:S(2)}) collective-permute-start(bf16[1040,128]{1,0:T(8,128)(2,1)S(1)} %get-tuple-element.14), channel_id=1, source_target_pairs={{0,4},{4,0},{8,12},{12,8},{16,20},{20,16},{24,28},{28,24},{1,5},{5... | collective-permute-start | bytes 798728 | tf_op jit(solution)/shard_map/ppermute | solution.py:181
  5.8 13.4 %collective-permute-start.1 = (bf16[1040,128]{1,0:T(8,128)(2,1)S(1)}, bf16[1040,128]{1,0:T(8,128)(2,1)S(1)}, u32[]{:S(2)}, u32[]{:S(2)}) collective-permute-start(bf16[1040,128]{1,0:T(8,128)(2,1)S(1)} %get-tuple-element.15), channel_id=1, source_target_pairs={{0,8},{4,12},{8,0},{12,4},{16,24},{20,28},{24,16},{28,20},{1,9},{5... | collective-permute-start | bytes 798728 | tf_op jit(solution)/shard_map/ppermute | solution.py:181
  7.3 33.1 %collective-permute-start.2 = (bf16[1040,128]{1,0:T(8,128)(2,1)S(1)}, bf16[1040,128]{1,0:T(8,128)(2,1)S(1)}, u32[]{:S(2)}, u32[]{:S(2)}) collective-permute-start(bf16[1040,128]{1,0:T(8,128)(2,1)S(1)} %get-tuple-element.16), channel_id=1, source_target_pairs={{0,16},{4,20},{8,24},{12,28},{16,0},{20,4},{24,8},{28,12},{1,17},{... | collective-permute-start | bytes 798728 | tf_op jit(solution)/shard_map/ppermute | solution.py:181
  9.9 36.1 %collective-permute-start.3 = (bf16[1040,128]{1,0:T(8,128)(2,1)S(1)}, bf16[1040,128]{1,0:T(8,128)(2,1)S(1)}, u32[]{:S(2)}, u32[]{:S(2)}) collective-permute-start(bf16[1040,128]{1,0:T(8,128)(2,1)S(1)} %get-tuple-element.17), channel_id=1, source_target_pairs={{0,20},{4,16},{8,28},{12,24},{16,4},{20,0},{24,12},{28,8},{1,21},{... | collective-permute-start | bytes 798728 | tf_op jit(solution)/shard_map/ppermute | solution.py:181
  10.2 35.8 %collective-permute-start.4 = (bf16[1040,128]{1,0:T(8,128)(2,1)S(1)}, bf16[1040,128]{1,0:T(8,128)(2,1)S(1)}, u32[]{:S(2)}, u32[]{:S(2)}) collective-permute-start(bf16[1040,128]{1,0:T(8,128)(2,1)S(1)} %get-tuple-element.18), channel_id=1, source_target_pairs={{0,24},{4,28},{8,16},{12,20},{16,8},{20,12},{24,0},{28,4},{1,25},{... | collective-permute-start | bytes 798728 | tf_op jit(solution)/shard_map/ppermute | solution.py:181
  12.7 33.4 %collective-permute-start.5 = (bf16[1040,128]{1,0:T(8,128)(2,1)S(1)}, bf16[1040,128]{1,0:T(8,128)(2,1)S(1)}, u32[]{:S(2)}, u32[]{:S(2)}) collective-permute-start(bf16[1040,128]{1,0:T(8,128)(2,1)S(1)} %get-tuple-element.19), channel_id=1, source_target_pairs={{0,28},{4,24},{8,20},{12,16},{16,12},{20,8},{24,4},{28,0},{1,29},{... | collective-permute-start | bytes 798728 | tf_op jit(solution)/shard_map/ppermute | solution.py:181
  19.2 26.8 %collective-permute-start.6 = (bf16[1040,128]{1,0:T(8,128)(2,1)S(1)}, bf16[1040,128]{1,0:T(8,128)(2,1)S(1)}, u32[]{:S(2)}, u32[]{:S(2)}) collective-permute-start(bf16[1040,128]{1,0:T(8,128)(2,1)S(1)} %get-tuple-element.20), channel_id=1, source_target_pairs={{0,12},{4,8},{8,4},{12,0},{16,28},{20,24},{24,20},{28,16},{1,13},{... | collective-permute-start | bytes 798728 | tf_op jit(solution)/shard_map/ppermute | solution.py:181
  49.3 20.6 %copy-start.1 = (s32[1,512]{1,0:T(1,128)S(1)}, s32[1,512]{1,0:T(1,128)}, u32[]{:S(2)}) copy-start(s32[1,512]{1,0:T(1,128)} %ids_ref.1) | copy-start | bytes 6148

commit v4 on v2

v4 whole, which is shorter than its diff:
```python
import functools
import math

import jax
import jax.numpy as jnp
from jax import lax
from jax.experimental import pallas as pl
from jax.experimental.pallas import tpu as pltpu
from jax.sharding import PartitionSpec as P


base_term = 0.05
epsilon = 1e-06
LANES = 128
TAIL = 16
AXES = ("blk", "grp")

VMEM = pl.BlockSpec(memory_space=pltpu.VMEM)
ANY = pl.BlockSpec(memory_space=pl.ANY)


def params(mib):
    return pltpu.CompilerParams(vmem_limit_bytes=mib << 20)


def unit_values(rows):
    values = rows.astype(jnp.float32)
    mean = jnp.mean(values * values, axis=-1, keepdims=True)
    scaling = lax.rsqrt(mean + epsilon) / math.sqrt(rows.shape[-1])
    return (values * scaling).astype(jnp.bfloat16)


def across(left, right):
    return lax.dot_general(
        left, right, (((1,), (1,)), ((), ())), preferred_element_type=jnp.float32
    )


def shard_of(k, chips):
    me = lax.axis_index("blk")
    half, chip = me // chips, me % chips
    return ((half ^ (k % 2)) * chips) + (chip ^ (k // 2))


def pack_into(ids, loads, rows_ref, outs, held, pick, cap, strata_dev):
    rows, width = rows_ref.shape
    chips = len(outs)
    shards = 2 * chips
    number = lax.broadcasted_iota(jnp.int32, (shards, 1), 0)
    lowest = (shard_of(number, chips) * strata_dev).astype(jnp.float32)
    begin = jnp.sum((ids < lowest).astype(jnp.float32), axis=1, keepdims=True)
    start = jnp.minimum(begin, float(rows - cap))
    number = lax.broadcasted_iota(jnp.int32, (shards * strata_dev, 1), 0)
    stratum = shard_of(number // strata_dev, chips) * strata_dev + number % strata_dev
    ends = jnp.sum((ids <= stratum.astype(jnp.float32)).astype(jnp.float32), axis=1, keepdims=True)
    slot = lax.broadcasted_iota(jnp.int32, (cap, rows), 0).astype(jnp.float32)
    row = lax.broadcasted_iota(jnp.int32, (cap, rows), 1).astype(jnp.float32)
    ahead = row - slot
    lane = lax.broadcasted_iota(jnp.int32, (1, LANES), 1).astype(jnp.float32)
    for k in range(shards):
        first = start[k : k + 1, :]
        pick[k * cap : (k + 1) * cap, :] = (ahead == first).astype(jnp.bfloat16)
        at = lane + first
        passed = (ends[k * strata_dev : (k + 1) * strata_dev, :] <= at).astype(jnp.float32)
        local = jnp.where(
            at >= begin[k : k + 1, :], jnp.sum(passed, axis=0, keepdims=True), float(strata_dev)
        )
        tail = width // LANES * 2 * cap + (k % 2) * 8
        outs[k // 2][tail : tail + 8, :] = jnp.broadcast_to(local, (8, LANES)).astype(jnp.bfloat16)
    step = rows // max(len(loads), 1)
    for i, load in enumerate(loads):
        load.wait()
        held[i * step : (i + 1) * step, :] = unit_values(rows_ref[i * step : (i + 1) * step, :])
    if not loads:
        held[...] = unit_values(rows_ref[...])
    wide = 2 * LANES
    for c in range(width // wide):
        runs = jnp.dot(
            pick[...], held[:, c * wide : (c + 1) * wide], preferred_element_type=jnp.float32
        ).astype(jnp.bfloat16)
        for d, out in enumerate(outs):
            for part in range(2):
                at = (2 * c + part) * 2 * cap
                out[at : at + 2 * cap, :] = runs[
                    d * 2 * cap : (d + 1) * 2 * cap, part * LANES : (part + 1) * LANES
                ]


def near_kernel(chips, cap, ids_any, cent_ref, rows_any, *rest):
    outs, (extra, rows_ref, ids_ref, held, pick, sems) = rest[:chips], rest[chips:]
    strata_dev, width = cent_ref.shape
    rows = rows_ref.shape[0]
    pieces = 4
    loads = [pltpu.make_async_copy(ids_any, ids_ref, sems.at[pieces])]
    for i in range(pieces):
        at = pl.ds(i * (rows // pieces), rows // pieces)
        loads.append(pltpu.make_async_copy(rows_any.at[at, :], rows_ref.at[at, :], sems.at[i]))
    for load in loads:
        load.start()
    cent = unit_values(cent_ref[...])
    extra[:strata_dev, :] = cent
    depth = width // LANES * 2 * cap + TAIL
    for c in range(width // LANES):
        at = depth + c * strata_dev
        outs[0][at : at + strata_dev, :] = cent[:, c * LANES : (c + 1) * LANES]
    loads[0].wait()
    ids = ids_ref[...].astype(jnp.float32)
    extra[strata_dev:, :] = jnp.zeros((TAIL, width), jnp.bfloat16)
    extra[strata_dev:, :rows] = jnp.broadcast_to(ids, (TAIL, rows)).astype(jnp.bfloat16)
    pack_into(ids, loads[1:], rows_ref, outs, held, pick, cap, strata_dev)


def far_kernel(chips, cap, strata_dev, extra, rows_ref, *rest):
    outs, (held, pick) = rest[:chips], rest[chips:]
    rows = rows_ref.shape[0]
    ids = extra[strata_dev:, :rows].astype(jnp.float32)[:1, :]
    pack_into(ids, [], rows_ref, outs, held, pick, cap, strata_dev)


def unpack(blocks, cap, strata_dev, units, id_col):
    each = len(blocks) * cap
    width = units.shape[1]
    id_rows = [[], []]
    for i, block in enumerate(blocks):
        depth = width // LANES * 2 * cap
        tail = block[depth : depth + TAIL, :].astype(jnp.float32)
        for r in range(2):
            at = r * each + i * cap
            for c in range(width // LANES):
                units[at : at + cap, c * LANES : (c + 1) * LANES] = block[
                    (2 * c + r) * cap : (2 * c + r + 1) * cap, :
                ]
            ids = tail[8 * r : 8 * r + 1, :]
            ids = jnp.where(ids < float(strata_dev), ids, -1.0)
            id_rows[r].append(ids[:, :cap])
            id_col[at : at + cap, :] = jnp.broadcast_to(ids, (LANES, LANES)).T[:cap, :]
    return [jnp.concatenate(rows, axis=1) for rows in id_rows]


def masked_exp(scores, id_col, id_key):
    same = jnp.concatenate([id_col] * (scores.shape[1] // LANES), axis=1) == id_key
    return jnp.where(same, jnp.exp((scores - 1.0) * 4.0), 0.0)


def fold(kernel):
    rows, lanes = kernel.shape
    return jnp.sum(kernel.reshape(rows // 8, 8, lanes), axis=0)


def key_of(id_row):
    return jnp.where(id_row >= 0.0, id_row, -2.0)


def picked_by(cent_units, units, id_row):
    near = across(cent_units, units)
    which = lax.broadcasted_iota(jnp.int32, near.shape, 0).astype(jnp.float32)
    return jnp.sum(jnp.where(which == id_row, near, 0.0), axis=0, keepdims=True)


def early_kernel(chips, cap, strata_dev, *rest):
    blocks, (units, id_col, facts) = rest[:chips], rest[chips:]
    each = chips * cap
    id_rows = unpack(blocks, cap, strata_dev, units, id_col)
    for r, row in enumerate(id_rows):
        mine = units[r * each : (r + 1) * each, :]
        kernel = masked_exp(across(mine, mine), id_col[r * each : (r + 1) * each, :], key_of(row))
        facts[r : r + 1, :] = jnp.sum(fold(kernel), axis=0, keepdims=True)
        facts[2 + r : 3 + r, :] = row


def late_kernel(order, cap, groups, units_a, col_a, facts, extra, block0, *rest):
    chips = len(order)
    blocks, (out_ref, units_b, col_b, cent0) = rest[:chips], rest[chips:]
    strata_dev, width = cent0.shape
    depth = width // LANES * 2 * cap + TAIL
    for c in range(width // LANES):
        at = depth + c * strata_dev
        cent0[:, c * LANES : (c + 1) * LANES] = block0[at : at + strata_dev, :]
    ids_b = unpack(blocks, cap, strata_dev, units_b, col_b)
    each = chips * cap
    me, group = lax.axis_index("blk"), lax.axis_index("grp")
    at_work = (me // chips) != (group % 2)
    total = jnp.zeros((1, 1), jnp.float32)
    weights = []
    for r in range(2):
        part_of = slice(r * each, (r + 1) * each)
        row_a, row_b = facts[2 + r : 3 + r, :], ids_b[r]
        key_b = key_of(row_b)
        rows_a, rows_b = units_a[part_of, :], units_b[part_of, :]
        kernel = masked_exp(across(rows_a, rows_b), col_a[part_of, :], key_b)
        sums = fold(kernel)
        part = kernel[:, :LANES]
        for c in range(1, each // LANES):
            part = part + kernel[:, c * LANES : (c + 1) * LANES]
        density_a = facts[r : r + 1, :] + jnp.concatenate(
            [
                jnp.sum(part[i * LANES : (i + 1) * LANES, :].T, axis=0, keepdims=True)
                for i in range(each // LANES)
            ],
            axis=1,
        )
        kernel = masked_exp(across(rows_b, rows_b), col_b[part_of, :], key_b)
        density_b = jnp.sum(sums + fold(kernel), axis=0, keepdims=True)
        cents = cent0[...] if r == 0 else extra[:strata_dev, :]
        both = []
        for row, units, density in ((row_a, rows_a, density_a), (row_b, rows_b, density_b)):
            real = row >= 0.0
            weight = jnp.where(
                real,
                ((1.0 - picked_by(cents, units, row)) + base_term)
                / jnp.where(real, density, 1.0),
                0.0,
            )
            total = total + jnp.sum(weight, axis=1, keepdims=True)
            both.append(weight)
        weights.append(both)
    out_ref[...] = jnp.broadcast_to(jnp.where(at_work, total, 0.0), out_ref.shape)
    for r in range(2):
        for side in range(2):
            for i, d in enumerate(order):
                source = me ^ (d + side * chips)
                at = 4 * (source * groups + (group ^ 1)) + r
                out_ref[pl.ds(at, 1), :cap] = weights[r][side][:, i * cap : (i + 1) * cap]


def finish_kernel(chips, cap, groups, strata_dev, ids_ref, got_ref, out_ref):
    rows = ids_ref.shape[1]
    group = lax.axis_index("grp")
    half = group % 2
    got = got_ref[...]
    row_of = lax.broadcasted_iota(jnp.int32, got.shape, 0) % 4
    total = jnp.sum(jnp.where(row_of == 2, got, 0.0), axis=0, keepdims=True)[:, :1]
    ids = ids_ref[...]
    weight = jnp.zeros((1, rows), jnp.float32)
    for i in range(chips):
        owner = (half * chips + i) * groups + (group ^ 1)
        for r in range(2):
            shard = (half ^ r) * chips + i
            begin = jnp.sum((ids < shard * strata_dev).astype(jnp.int32))
            start = jnp.minimum(begin, rows - cap)
            part = got_ref[pl.ds(4 * owner + r, 1), :]
            part = jnp.broadcast_to(jnp.concatenate([part] * (rows // LANES), axis=1), (8, rows))
            part = pltpu.roll(part, start, axis=1)[:1, :]
            mine = (ids >= shard * strata_dev) & (ids < (shard + 1) * strata_dev)
            weight = jnp.where(mine, part, weight)
    out_ref[...] = weight * (float(rows * 2 * chips * groups) / total)


def body(embeddings, strata, centroids):
    shards, groups = lax.axis_size("blk"), lax.axis_size("grp")
    chips = shards // 2
    rows, width = embeddings.shape[1:]
    strata_dev = centroids.shape[1]
    cap = 2 * rows // shards
    chunks = width // LANES
    depth = chunks * 2 * cap + TAIL
    each = chips * cap
    every = [(b, g) for b in range(shards) for g in range(groups)]
    kind_a = [(b, g) for b, g in every if b // chips == g % 2]
    kind_b = [(b, g) for b, g in every if b // chips != g % 2]

    def send(array, pairs):
        return lax.ppermute(
            array, AXES, [(b * groups + g, to_b * groups + to_g) for (b, g), (to_b, to_g) in pairs]
        )

    def shape(*dims, dtype=jnp.bfloat16):
        return pltpu.VMEM(dims, dtype)

    held = [pltpu.VMEM((rows, width), jnp.bfloat16), pltpu.VMEM((shards * cap, rows), jnp.bfloat16)]
    order = [0, *reversed(range(1, chips))]
    swap = [((b, g), (b ^ chips, g ^ 1)) for b, g in kind_b]
    far_rows = send(embeddings[0], swap)
    *near, extra = pl.pallas_call(
        functools.partial(near_kernel, chips, cap),
        out_shape=[
            shape(depth + (chunks * strata_dev if d == 0 else 0), LANES) for d in range(chips)
        ]
        + [shape(strata_dev + TAIL, width)],
        in_specs=[ANY, VMEM, ANY],
        out_specs=[VMEM] * (chips + 1),
        scratch_shapes=[
            pltpu.VMEM((rows, width), jnp.bfloat16),
            pltpu.VMEM((1, rows), jnp.int32),
            *held,
            pltpu.SemaphoreType.DMA((5,)),
        ],
        compiler_params=params(44),
        cost_estimate=pl.CostEstimate(flops=0, transcendentals=0, bytes_accessed=0),
        name="near",
    )(strata, centroids[0], embeddings[0])
    blocks_a = []
    for d in order:
        block = near[d]
        if d == 1:
            block, _ = lax.optimization_barrier((block, blocks_a[0]))
        blocks_a.append(send(block, [((b, g), (b ^ d, g ^ 1)) for b, g in kind_a]))
    extra = send(extra, swap)
    blocks_b = pl.pallas_call(
        functools.partial(far_kernel, chips, cap, strata_dev),
        out_shape=[shape(depth, LANES)] * chips,
        in_specs=[VMEM, VMEM],
        out_specs=[VMEM] * chips,
        scratch_shapes=held,
        compiler_params=params(20),
        name="far",
    )(extra, far_rows)
    blocks_b = [
        blocks_b[d]
        if d == 0
        else send(blocks_b[d], [((b, g), (b ^ d, g)) for b, g in kind_b])
        for d in order
    ]
    units_a, col_a, facts = pl.pallas_call(
        functools.partial(early_kernel, chips, cap, strata_dev),
        out_shape=[
            shape(2 * each, width),
            shape(2 * each, LANES, dtype=jnp.float32),
            shape(8, each, dtype=jnp.float32),
        ],
        in_specs=[VMEM] * chips,
        out_specs=[VMEM] * 3,
        compiler_params=params(20),
        name="early",
    )(*blocks_a)
    sent = pl.pallas_call(
        functools.partial(late_kernel, order, cap, groups),
        out_shape=jax.ShapeDtypeStruct((shards * groups * 4, LANES), jnp.float32),
        in_specs=[VMEM] * (chips + 5),
        out_specs=VMEM,
        scratch_shapes=[
            pltpu.VMEM((2 * each, width), jnp.bfloat16),
            pltpu.VMEM((2 * each, LANES), jnp.float32),
            pltpu.VMEM((strata_dev, width), jnp.bfloat16),
        ],
        compiler_params=params(24),
        name="late",
    )(units_a, col_a, facts, extra, blocks_a[0], *blocks_b)
    got = lax.all_to_all(
        sent.reshape(shards * groups, 4, LANES), AXES, 0, 0, tiled=True
    ).reshape(shards * groups * 4, LANES)
    return pl.pallas_call(
        functools.partial(finish_kernel, chips, cap, groups, strata_dev),
        out_shape=jax.ShapeDtypeStruct((1, rows), jnp.float32),
        in_specs=[VMEM, VMEM],
        out_specs=VMEM,
        compiler_params=params(8),
        name="finish",
    )(strata, got)


def solution(mesh):
    placed = (P("grp", "blk", None), P("grp", "blk"), P("grp", "blk", None))
    return jax.shard_map(
        body, mesh=mesh, in_specs=placed, out_specs=P("grp", "blk"), check_vma=False
    )
```

time: 86 us -> 68.7 us (0.80)
  starting transfers between devices: 35.2 us -> 17.1 us
  blocking collectives: 15 us -> 32 us
  Pallas kernels: 24.7 us -> 9.92 us
  waiting for transfers between devices: 9.1 us -> 6.47 us
  local copies, waits for them, and re-layouts: 1.14 us -> 2.66 us
    ppermute x11 -> x9, starting transfers between devices: 35.2 us -> 17.1 us  [send(): lax.ppermute(array, AXES, [(b * groups + g, to_b * groups + to_g) for (b,...]
    all_to_all x1, blocking collectives: 15 us -> 32 us  [body(): lax.all_to_all(sent.reshape(shards * groups, 4, LANES), AXES, 0, 0, tiled...]
    pallas_call x4, Pallas kernels: 23.1 us -> 9.11 us  [the longest x1 3.81 us: body(): pl.pallas_call(functools.partial(late_kernel, order, cap, groups), out_sh...]
    ppermute x11 -> x9, waiting for transfers between devices: 9.1 us -> 6.47 us  [send(): lax.ppermute(array, AXES, [(b * groups + g, to_b * groups + to_g) for (b,...]
    unnamed x20 -> x6, local copies, waits for them, and re-layouts: 1.14 us -> 2.66 us
  transfers between devices with their start and end apart: 11 -> 9, of which waited for: 1 -> 2; matrix products, arithmetic and copies ran while one was open for 0% -> 0% of each run, Pallas kernels for 16% -> 8%
where the time goes in v4:
time: 68.7 us; the launch traced here: 68.3 us
  blocking collectives  32 us (47%)
  starting transfers between devices  17.1 us (25%)
  Pallas kernels  9.92 us (14%)
  waiting for transfers between devices  6.47 us (9%)
  local copies, waits for them, and re-layouts  2.66 us (4%)
    all_to_all x1, blocking collectives, body(): lax.all_to_all(sent.reshape(shards * groups, 4, LANES), AXES, 0, 0, tiled...  32 us
    ppermute x9, starting transfers between devices, send(): lax.ppermute(array, AXES, [(b * groups + g, to_b * groups + to_g) for (b,...  17.1 us
    ppermute x9, waiting for transfers between devices, send(): lax.ppermute(array, AXES, [(b * groups + g, to_b * groups + to_g) for (b,...  6.47 us
    pallas_call x1, Pallas kernels, body(): pl.pallas_call(functools.partial(late_kernel, order, cap, groups), out_sh...  3.81 us
    unnamed x6, local copies, waits for them, and re-layouts  2.66 us
    pallas_call x1, Pallas kernels, body(): pl.pallas_call(functools.partial(near_kernel, chips, cap), out_shape=[sha...  2.07 us
    pallas_call x1, Pallas kernels, body(): pl.pallas_call(functools.partial(early_kernel, chips, cap, strata_dev), o...  1.63 us
    pallas_call x1, Pallas kernels, body(): pl.pallas_call(functools.partial(far_kernel, chips, cap, strata_dev), out...  1.59 us
  transfers between devices with their start and end apart: 9, of which 2 were waited for; matrix products, arithmetic and copies ran while one was open for 0% of the time, Pallas kernels for 8%

profile of v4, /device:TPU:0, one launch (start us, length us, event | category | flops | bytes accessed | tf_op | source)
XLA Modules:
  0.0 68.3 jit_solution(3034195462963477828)
XLA Ops:
  0.0 0.7 %collective-permute-start.5 = (bf16[512,1024]{1,0:T(8,128)(2,1)}, bf16[512,1024]{1,0:T(8,128)(2,1)S(1)}, u32[]{:S(2)}, u32[]{:S(2)}) collective-permute-start(bf16[512,1024]{1,0:T(8,128)(2,1)} %bitcast.4), channel_id=1, source_target_pairs={{1,16},{3,18},{5,20},{7,22},{9,24},{11,26},{13,28},{15,30},{16,1},... | collective-permute-start | bytes 3145736 | tf_op jit(solution)/shard_map/ppermute | solution.py:263
  0.7 0.0 copy-start
  0.7 1.2 %copy-done = bf16[1,512,1024]{2,1,0:T(8,128)(2,1)S(1)} copy-done((bf16[1,512,1024]{2,1,0:T(8,128)(2,1)S(1)}, bf16[1,512,1024]{2,1,0:T(8,128)(2,1)}, u32[]{:S(2)}) %copy-start) | copy-done | bytes 1048600
  2.0 0.0 copy-start.1
  2.0 0.8 %copy-done.1 = bf16[1,16,1024]{2,1,0:T(8,128)(2,1)S(1)} copy-done((bf16[1,16,1024]{2,1,0:T(8,128)(2,1)S(1)}, bf16[1,16,1024]{2,1,0:T(8,128)(2,1)}, u32[]{:S(2)}) %copy-start.1) | copy-done | bytes 32792
  2.7 0.0 copy-start.2
  2.7 0.7 copy-done.2
  3.4 2.1 %near.1 = (bf16[2192,128]{1,0:T(8,128)(2,1)S(1)}, bf16[2064,128]{1,0:T(8,128)(2,1)S(1)}, bf16[2064,128]{1,0:T(8,128)(2,1)S(1)}, bf16[2064,128]{1,0:T(8,128)(2,1)S(1)}, bf16[32,1024]{1,0:T(8,128)(2,1)S(1)}) custom-call(s32[1,512]{1,0:T(1,128)S(1)} %copy-done.2, bf16[16,1024]{1,0:T(8,128)(2,1)S(1)} %bitcast.8, bf16[512,1024]{1,0:T(8,128)(2,1)S(1)} %bitcast.5), custom_call_target="tpu_custom_call" | custom-call | tf_op jit(solution)/shard_map/near/pallas_call | solution.py:274
  5.5 7.3 %collective-permute-start = (bf16[2192,128]{1,0:T(8,128)(2,1)S(1)}, bf16[2192,128]{1,0:T(8,128)(2,1)S(1)}, u32[]{:S(2)}, u32[]{:S(2)}) collective-permute-start(bf16[2192,128]{1,0:T(8,128)(2,1)S(1)} %get-tuple-element.18), channel_id=1, source_target_pairs={{0,1},{2,3},{4,5},{6,7},{8,9},{10,11},{12,13},{14,15},{17,16},{19,... | collective-permute-start | bytes 1683464 | tf_op jit(solution)/shard_map/ppermute | solution.py:263
  12.8 3.4 %collective-permute-start.1 = (bf16[2064,128]{1,0:T(8,128)(2,1)S(1)}, bf16[2064,128]{1,0:T(8,128)(2,1)S(1)}, u32[]{:S(2)}, u32[]{:S(2)}) collective-permute-start(bf16[2064,128]{1,0:T(8,128)(2,1)S(1)} %get-tuple-element.19), channel_id=1, source_target_pairs={{0,13},{2,15},{4,9},{6,11},{8,5},{10,7},{12,1},{14,3},{17,28},{19,... | collective-permute-start | bytes 1585160 | tf_op jit(solution)/shard_map/ppermute | solution.py:263
  16.2 0.7 collective-permute-start.4
  16.9 1.6 %collective-permute-start.2 = (bf16[2064,128]{1,0:T(8,128)(2,1)S(1)}, bf16[2064,128]{1,0:T(8,128)(2,1)S(1)}, u32[]{:S(2)}, u32[]{:S(2)}) collective-permute-start(bf16[2064,128]{1,0:T(8,128)(2,1)S(1)} %get-tuple-element.20), channel_id=1, source_target_pairs={{0,9},{2,11},{4,13},{6,15},{8,1},{10,3},{12,5},{14,7},{17,24},{19,... | collective-permute-start | bytes 1585160 | tf_op jit(solution)/shard_map/ppermute | solution.py:263
  18.5 0.0 collective-permute-done.rest_0_.block0
  18.5 1.3 %collective-permute-start.3 = (bf16[2064,128]{1,0:T(8,128)(2,1)S(1)}, bf16[2064,128]{1,0:T(8,128)(2,1)S(1)}, u32[]{:S(2)}, u32[]{:S(2)}) collective-permute-start(bf16[2064,128]{1,0:T(8,128)(2,1)S(1)} %get-tuple-element.22), channel_id=1, source_target_pairs={{0,5},{2,7},{4,1},{6,3},{8,13},{10,15},{12,9},{14,11},{17,20},{19,... | collective-permute-start | bytes 1585160 | tf_op jit(solution)/shard_map/ppermute | solution.py:263
  19.8 0.0 collective-permute-done.4.extra
  19.8 0.0 collective-permute-done.5.rows_ref
  19.8 1.6 %far.1 = (bf16[2064,128]{1,0:T(8,128)(2,1)S(1)}, bf16[2064,128]{1,0:T(8,128)(2,1)S(1)}, bf16[2064,128]{1,0:T(8,128)(2,1)S(1)}, bf16[2064,128]{1,0:T(8,128)(2,1)S(1)}) custom-call(bf16[32,1024]{1,0:T(8,128)(2,1)S(1)} %collective-permute-done.4.extra, bf16[512,1024]{1,0:T(8,128)(2,1)S(1)} %collective-permute-done.5.rows_ref), custom_call_target="tpu_custom_call" | custom-call | tf_op jit(solution)/shard_map/far/pallas_call | solution.py:299
  21.4 0.7 %collective-permute-start.6 = (bf16[2064,128]{1,0:T(8,128)(2,1)S(1)}, bf16[2064,128]{1,0:T(8,128)(2,1)S(1)}, u32[]{:S(2)}, u32[]{:S(2)}) collective-permute-start(bf16[2064,128]{1,0:T(8,128)(2,1)S(1)} %get-tuple-element.28), channel_id=1, source_target_pairs={{1,13},{3,15},{5,9},{7,11},{9,5},{11,7},{13,1},{15,3},{16,28},{18,... | collective-permute-start | bytes 1585160 | tf_op jit(solution)/shard_map/ppermute | solution.py:263
  22.1 0.7 %collective-permute-start.7 = (bf16[2064,128]{1,0:T(8,128)(2,1)S(1)}, bf16[2064,128]{1,0:T(8,128)(2,1)S(1)}, u32[]{:S(2)}, u32[]{:S(2)}) collective-permute-start(bf16[2064,128]{1,0:T(8,128)(2,1)S(1)} %get-tuple-element.29), channel_id=1, source_target_pairs={{1,9},{3,11},{5,13},{7,15},{9,1},{11,3},{13,5},{15,7},{16,24},{18,... | collective-permute-start | bytes 1585160 | tf_op jit(solution)/shard_map/ppermute | solution.py:263
  22.8 1.5 %collective-permute-done.1.rest_1_ = bf16[2064,128]{1,0:T(8,128)(2,1)S(1)} collective-permute-done((bf16[2064,128]{1,0:T(8,128)(2,1)S(1)}, bf16[2064,128]{1,0:T(8,128)(2,1)S(1)}, u32[]{:S(2)}, u32[]{:S(2)}) %collective-permute-start.1) | collective-permute-done | bytes 528416 | tf_op jit(solution)/shard_map/ppermute | solution.py:263
  24.3 0.7 %collective-permute-start.8 = (bf16[2064,128]{1,0:T(8,128)(2,1)S(1)}, bf16[2064,128]{1,0:T(8,128)(2,1)S(1)}, u32[]{:S(2)}, u32[]{:S(2)}) collective-permute-start(bf16[2064,128]{1,0:T(8,128)(2,1)S(1)} %get-tuple-element.30), channel_id=1, source_target_pairs={{1,5},{3,7},{5,1},{7,3},{9,13},{11,15},{13,9},{15,11},{16,20},{18,... | collective-permute-start | bytes 1585160 | tf_op jit(solution)/shard_map/ppermute | solution.py:263
  25.0 5.0 %collective-permute-done.2.rest_2_ = bf16[2064,128]{1,0:T(8,128)(2,1)S(1)} collective-permute-done((bf16[2064,128]{1,0:T(8,128)(2,1)S(1)}, bf16[2064,128]{1,0:T(8,128)(2,1)S(1)}, u32[]{:S(2)}, u32[]{:S(2)}) %collective-permute-start.2) | collective-permute-done | bytes 528416 | tf_op jit(solution)/shard_map/ppermute | solution.py:263
  30.0 0.0 collective-permute-done.3.rest_3_
  30.0 1.6 %early.1 = (bf16[1024,1024]{1,0:T(8,128)(2,1)S(1)}, f32[1024,128]{1,0:T(8,128)S(1)}, f32[8,512]{1,0:T(8,128)S(1)}) custom-call(bf16[2192,128]{1,0:T(8,128)(2,1)S(1)} %collective-permute-done.rest_0_.block0, bf16[2064,128]{1,0:T(8,128)(2,1)S(1)} %collective-permute-done.1.rest_1_, bf16[2064,128]{1,0:T(8,128)(2,1)S(1)} %collective-permute-done.2.rest_2_, ...), custom_call_target="tpu_custom_call" | custom-call | tf_op jit(solution)/shard_map/early/pallas_call | solution.py:314
  31.6 0.0 collective-permute-done.6.rest_1_
  31.6 0.0 collective-permute-done.7.rest_2_
  31.6 0.0 collective-permute-done.8.rest_3_
  31.7 3.8 %late.1 = f32[128,128]{1,0:T(8,128)S(1)} custom-call(bf16[1024,1024]{1,0:T(8,128)(2,1)S(1)} %get-tuple-element.23.units_a, f32[1024,128]{1,0:T(8,128)S(1)} %get-tuple-element.24.col_a, f32[8,512]{1,0:T(8,128)S(1)} %get-tuple-element.25.facts, bf16[32,1024]{1,0:T(8,128)(2,1)S(1)} %collective-permute-done.4.extra, ...), custom_call_target="tpu_custom_call" | custom-call | tf_op jit(solution)/shard_map/late/pallas_call | solution.py:326
  35.5 32.0 %all_to_all.5 = f32[32,4,128]{2,1,0:T(4,128)S(1)} all-to-all(f32[32,4,128]{2,1,0:T(4,128)S(1)} %bitcast.6), channel_id=1, replica_groups=mesh['blk'=8,'grp'=4] {'blk','grp'}, dimensions={0} | all-to-all | bytes 131072 | tf_op jit(solution)/shard_map/all_to_all | solution.py:339
  67.5 0.8 %finish.1 = f32[1,512]{1,0:T(1,128)} custom-call(s32[1,512]{1,0:T(1,128)S(1)} %copy-done.2, f32[128,128]{1,0:T(8,128)S(1)} %bitcast.7), custom_call_target="tpu_custom_call" | custom-call | tf_op jit(solution)/shard_map/finish/pallas_call | solution.py:342
Async XLA Ops:
  0.0 19.8 %collective-permute-start.5 = (bf16[512,1024]{1,0:T(8,128)(2,1)}, bf16[512,1024]{1,0:T(8,128)(2,1)S(1)}, u32[]{:S(2)}, u32[]{:S(2)}) collective-permute-start(bf16[512,1024]{1,0:T(8,128)(2,1)} %bitcast.4), channel_id=1, source_target_pairs={{1,16},{3,18},{5,20},{7,22},{9,24},{11,26},{13,28},{15,30},{16,1},... | collective-permute-start | bytes 3145736 | tf_op jit(solution)/shard_map/ppermute | solution.py:263
  0.7 1.2 %copy-start = (bf16[1,512,1024]{2,1,0:T(8,128)(2,1)S(1)}, bf16[1,512,1024]{2,1,0:T(8,128)(2,1)}, u32[]{:S(2)}) copy-start(bf16[1,512,1024]{2,1,0:T(8,128)(2,1)} %param.3) | copy-start | bytes 3145732
  2.0 0.8 %copy-start.1 = (bf16[1,16,1024]{2,1,0:T(8,128)(2,1)S(1)}, bf16[1,16,1024]{2,1,0:T(8,128)(2,1)}, u32[]{:S(2)}) copy-start(bf16[1,16,1024]{2,1,0:T(8,128)(2,1)} %param.5) | copy-start | bytes 98308
  2.7 0.7 copy-start.2
  5.5 13.0 %collective-permute-start = (bf16[2192,128]{1,0:T(8,128)(2,1)S(1)}, bf16[2192,128]{1,0:T(8,128)(2,1)S(1)}, u32[]{:S(2)}, u32[]{:S(2)}) collective-permute-start(bf16[2192,128]{1,0:T(8,128)(2,1)S(1)} %get-tuple-element.18), channel_id=1, source_target_pairs={{0,1},{2,3},{4,5},{6,7},{8,9},{10,11},{12,13},{14,15},{17,16},{19,... | collective-permute-start | bytes 1683464 | tf_op jit(solution)/shard_map/ppermute | solution.py:263
  12.8 11.6 %collective-permute-start.1 = (bf16[2064,128]{1,0:T(8,128)(2,1)S(1)}, bf16[2064,128]{1,0:T(8,128)(2,1)S(1)}, u32[]{:S(2)}, u32[]{:S(2)}) collective-permute-start(bf16[2064,128]{1,0:T(8,128)(2,1)S(1)} %get-tuple-element.19), channel_id=1, source_target_pairs={{0,13},{2,15},{4,9},{6,11},{8,5},{10,7},{12,1},{14,3},{17,28},{19,... | collective-permute-start | bytes 1585160 | tf_op jit(solution)/shard_map/ppermute | solution.py:263
  16.2 3.6 %collective-permute-start.4 = (bf16[32,1024]{1,0:T(8,128)(2,1)S(1)}, bf16[32,1024]{1,0:T(8,128)(2,1)S(1)}, u32[]{:S(2)}, u32[]{:S(2)}) collective-permute-start(bf16[32,1024]{1,0:T(8,128)(2,1)S(1)} %get-tuple-element.26), channel_id=1, source_target_pairs={{1,16},{3,18},{5,20},{7,22},{9,24},{11,26},{13,28},{15,30},{16,1},... | collective-permute-start | bytes 196616 | tf_op jit(solution)/shard_map/ppermute | solution.py:263
  16.9 13.1 %collective-permute-start.2 = (bf16[2064,128]{1,0:T(8,128)(2,1)S(1)}, bf16[2064,128]{1,0:T(8,128)(2,1)S(1)}, u32[]{:S(2)}, u32[]{:S(2)}) collective-permute-start(bf16[2064,128]{1,0:T(8,128)(2,1)S(1)} %get-tuple-element.20), channel_id=1, source_target_pairs={{0,9},{2,11},{4,13},{6,15},{8,1},{10,3},{12,5},{14,7},{17,24},{19,... | collective-permute-start | bytes 1585160 | tf_op jit(solution)/shard_map/ppermute | solution.py:263
  18.5 11.5 %collective-permute-start.3 = (bf16[2064,128]{1,0:T(8,128)(2,1)S(1)}, bf16[2064,128]{1,0:T(8,128)(2,1)S(1)}, u32[]{:S(2)}, u32[]{:S(2)}) collective-permute-start(bf16[2064,128]{1,0:T(8,128)(2,1)S(1)} %get-tuple-element.22), channel_id=1, source_target_pairs={{0,5},{2,7},{4,1},{6,3},{8,13},{10,15},{12,9},{14,11},{17,20},{19,... | collective-permute-start | bytes 1585160 | tf_op jit(solution)/shard_map/ppermute | solution.py:263
  21.4 10.2 %collective-permute-start.6 = (bf16[2064,128]{1,0:T(8,128)(2,1)S(1)}, bf16[2064,128]{1,0:T(8,128)(2,1)S(1)}, u32[]{:S(2)}, u32[]{:S(2)}) collective-permute-start(bf16[2064,128]{1,0:T(8,128)(2,1)S(1)} %get-tuple-element.28), channel_id=1, source_target_pairs={{1,13},{3,15},{5,9},{7,11},{9,5},{11,7},{13,1},{15,3},{16,28},{18,... | collective-permute-start | bytes 1585160 | tf_op jit(solution)/shard_map/ppermute | solution.py:263
  22.1 9.5 %collective-permute-start.7 = (bf16[2064,128]{1,0:T(8,128)(2,1)S(1)}, bf16[2064,128]{1,0:T(8,128)(2,1)S(1)}, u32[]{:S(2)}, u32[]{:S(2)}) collective-permute-start(bf16[2064,128]{1,0:T(8,128)(2,1)S(1)} %get-tuple-element.29), channel_id=1, source_target_pairs={{1,9},{3,11},{5,13},{7,15},{9,1},{11,3},{13,5},{15,7},{16,24},{18,... | collective-permute-start | bytes 1585160 | tf_op jit(solution)/shard_map/ppermute | solution.py:263
  24.3 7.3 %collective-permute-start.8 = (bf16[2064,128]{1,0:T(8,128)(2,1)S(1)}, bf16[2064,128]{1,0:T(8,128)(2,1)S(1)}, u32[]{:S(2)}, u32[]{:S(2)}) collective-permute-start(bf16[2064,128]{1,0:T(8,128)(2,1)S(1)} %get-tuple-element.30), channel_id=1, source_target_pairs={{1,5},{3,7},{5,1},{7,3},{9,13},{11,15},{13,9},{15,11},{16,20},{18,... | collective-permute-start | bytes 1585160 | tf_op jit(solution)/shard_map/ppermute | solution.py:263

commit v5 on v4

--- a/solution.py
+++ b/solution.py
@@ -157,70 +157,101 @@
     return jnp.sum(jnp.where(which == id_row, near, 0.0), axis=0, keepdims=True)
 
 
+def transposed_sum(kernel):
+    part = kernel[:, :LANES]
+    for c in range(1, kernel.shape[1] // LANES):
+        part = part + kernel[:, c * LANES : (c + 1) * LANES]
+    return jnp.concatenate(
+        [
+            jnp.sum(part[i * LANES : (i + 1) * LANES, :].T, axis=0, keepdims=True)
+            for i in range(part.shape[0] // LANES)
+        ],
+        axis=1,
+    )
+
+
+def join(groups, units, id_col, ids):
+    earlier, new = [[] for _ in groups], []
+    for r, row in enumerate(ids):
+        key = key_of(row)
+        each = row.shape[1]
+        mine = units[r * each : (r + 1) * each, :]
+        sums = fold(masked_exp(across(mine, mine), id_col[r * each : (r + 1) * each, :], key))
+        for sums_of, (old_units, old_col, old_facts) in zip(earlier, groups):
+            size = old_facts.shape[1]
+            at = slice(r * size, (r + 1) * size)
+            kernel = masked_exp(across(old_units[at, :], mine), old_col[at, :], key)
+            sums = sums + fold(kernel)
+            sums_of.append(old_facts[r : r + 1, :] + transposed_sum(kernel))
+        new.append(jnp.sum(sums, axis=0, keepdims=True))
+    return earlier, new
+
+
 def early_kernel(chips, cap, strata_dev, *rest):
     blocks, (units, id_col, facts) = rest[:chips], rest[chips:]
-    each = chips * cap
-    id_rows = unpack(blocks, cap, strata_dev, units, id_col)
-    for r, row in enumerate(id_rows):
-        mine = units[r * each : (r + 1) * each, :]
-        kernel = masked_exp(across(mine, mine), id_col[r * each : (r + 1) * each, :], key_of(row))
-        facts[r : r + 1, :] = jnp.sum(fold(kernel), axis=0, keepdims=True)
+    ids = unpack(blocks, cap, strata_dev, units, id_col)
+    _, density = join([], units, id_col, ids)
+    for r, row in enumerate(ids):
+        facts[r : r + 1, :] = density[r]
         facts[2 + r : 3 + r, :] = row
 
 
-def late_kernel(order, cap, groups, units_a, col_a, facts, extra, block0, *rest):
-    chips = len(order)
-    blocks, (out_ref, units_b, col_b, cent0) = rest[:chips], rest[chips:]
-    strata_dev, width = cent0.shape
+def mid_kernel(count, cap, units_a, col_a, facts_a, extra, block0, *rest):
+    blocks, (units, id_col, facts, facts_out, cents) = rest[:count], rest[count:]
+    strata_dev, width = cents.shape[0] // 2, cents.shape[1]
     depth = width // LANES * 2 * cap + TAIL
     for c in range(width // LANES):
         at = depth + c * strata_dev
-        cent0[:, c * LANES : (c + 1) * LANES] = block0[at : at + strata_dev, :]
-    ids_b = unpack(blocks, cap, strata_dev, units_b, col_b)
-    each = chips * cap
+        cents[:strata_dev, c * LANES : (c + 1) * LANES] = block0[at : at + strata_dev, :]
+    cents[strata_dev:, :] = extra[:strata_dev, :]
+    ids = unpack(blocks, cap, strata_dev, units, id_col)
+    (old,), density = join([(units_a, col_a, facts_a)], units, id_col, ids)
+    for r, row in enumerate(ids):
+        near = cents[r * strata_dev : (r + 1) * strata_dev, :]
+        facts[r : r + 1, :] = density[r]
+        facts[2 + r : 3 + r, :] = row
+        each = row.shape[1]
+        facts[4 + r : 5 + r, :] = picked_by(near, units[r * each : (r + 1) * each, :], row)
+        row = facts_a[2 + r : 3 + r, :]
+        facts_out[r : r + 1, :] = old[r]
+        facts_out[2 + r : 3 + r, :] = row
+        each = row.shape[1]
+        facts_out[4 + r : 5 + r, :] = picked_by(near, units_a[r * each : (r + 1) * each, :], row)
+
+
+def late_kernel(order, cap, groups, units_a, col_a, facts_a, units_m, col_m, facts_m, cents, *rest):
+    blocks, (out_ref, units, id_col) = rest[:-3], rest[-3:]
+    chips = len(order)
+    strata_dev = cents.shape[0] // 2
     me, group = lax.axis_index("blk"), lax.axis_index("grp")
     at_work = (me // chips) != (group % 2)
+    ids = unpack(blocks, cap, strata_dev, units, id_col)
+    old = [(units_a, col_a, facts_a), (units_m, col_m, facts_m)]
+    earlier, density = join(old, units, id_col, ids)
     total = jnp.zeros((1, 1), jnp.float32)
     weights = []
-    for r in range(2):
-        part_of = slice(r * each, (r + 1) * each)
-        row_a, row_b = facts[2 + r : 3 + r, :], ids_b[r]
-        key_b = key_of(row_b)
-        rows_a, rows_b = units_a[part_of, :], units_b[part_of, :]
-        kernel = masked_exp(across(rows_a, rows_b), col_a[part_of, :], key_b)
-        sums = fold(kernel)
-        part = kernel[:, :LANES]
-        for c in range(1, each // LANES):
-            part = part + kernel[:, c * LANES : (c + 1) * LANES]
-        density_a = facts[r : r + 1, :] + jnp.concatenate(
-            [
-                jnp.sum(part[i * LANES : (i + 1) * LANES, :].T, axis=0, keepdims=True)
-                for i in range(each // LANES)
-            ],
-            axis=1,
+    for r, row in enumerate(ids):
+        near = cents[r * strata_dev : (r + 1) * strata_dev, :]
+        each = row.shape[1]
+        states = [
+            (facts_a[2 + r : 3 + r, :], facts_a[4 + r : 5 + r, :], earlier[0][r]),
+            (facts_m[2 + r : 3 + r, :], facts_m[4 + r : 5 + r, :], earlier[1][r]),
+            (row, picked_by(near, units[r * each : (r + 1) * each, :], row), density[r]),
+        ]
+        all_of = [jnp.concatenate(parts, axis=1) for parts in zip(*states)]
+        row, picked, dense = all_of
+        real = row >= 0.0
+        weight = jnp.where(
+            real, ((1.0 - picked) + base_term) / jnp.where(real, dense, 1.0), 0.0
         )
-        kernel = masked_exp(across(rows_b, rows_b), col_b[part_of, :], key_b)
-        density_b = jnp.sum(sums + fold(kernel), axis=0, keepdims=True)
-        cents = cent0[...] if r == 0 else extra[:strata_dev, :]
-        both = []
-        for row, units, density in ((row_a, rows_a, density_a), (row_b, rows_b, density_b)):
-            real = row >= 0.0
-            weight = jnp.where(
-                real,
-                ((1.0 - picked_by(cents, units, row)) + base_term)
-                / jnp.where(real, density, 1.0),
-                0.0,
-            )
-            total = total + jnp.sum(weight, axis=1, keepdims=True)
-            both.append(weight)
-        weights.append(both)
+        total = total + jnp.sum(weight, axis=1, keepdims=True)
+        weights.append(weight)
     out_ref[...] = jnp.broadcast_to(jnp.where(at_work, total, 0.0), out_ref.shape)
     for r in range(2):
-        for side in range(2):
-            for i, d in enumerate(order):
-                source = me ^ (d + side * chips)
-                at = 4 * (source * groups + (group ^ 1)) + r
-                out_ref[pl.ds(at, 1), :cap] = weights[r][side][:, i * cap : (i + 1) * cap]
+        for i in range(2 * chips):
+            source = me ^ (order[i % chips] + i // chips * chips)
+            at = 4 * (source * groups + (group ^ 1)) + r
+            out_ref[pl.ds(at, 1), :cap] = weights[r][:, i * cap : (i + 1) * cap]
 
 
 def finish_kernel(chips, cap, groups, strata_dev, ids_ref, got_ref, out_ref):
@@ -292,7 +323,7 @@
     blocks_a = []
     for d in order:
         block = near[d]
-        if d == 1:
+        if d == order[-1]:
             block, _ = lax.optimization_barrier((block, blocks_a[0]))
         blocks_a.append(send(block, [((b, g), (b ^ d, g ^ 1)) for b, g in kind_a]))
     extra = send(extra, swap)
@@ -323,19 +354,33 @@
         compiler_params=params(20),
         name="early",
     )(*blocks_a)
+    middle = chips // 2
+    units_m, col_m, facts_m, facts_a, cents = pl.pallas_call(
+        functools.partial(mid_kernel, middle, cap),
+        out_shape=[
+            shape(2 * middle * cap, width),
+            shape(2 * middle * cap, LANES, dtype=jnp.float32),
+            shape(8, middle * cap, dtype=jnp.float32),
+            shape(8, each, dtype=jnp.float32),
+            shape(2 * strata_dev, width),
+        ],
+        in_specs=[VMEM] * (middle + 5),
+        out_specs=[VMEM] * 5,
+        compiler_params=params(20),
+        name="mid",
+    )(units_a, col_a, facts, extra, blocks_a[0], *blocks_b[:middle])
     sent = pl.pallas_call(
         functools.partial(late_kernel, order, cap, groups),
         out_shape=jax.ShapeDtypeStruct((shards * groups * 4, LANES), jnp.float32),
-        in_specs=[VMEM] * (chips + 5),
+        in_specs=[VMEM] * (7 + chips - middle),
         out_specs=VMEM,
         scratch_shapes=[
-            pltpu.VMEM((2 * each, width), jnp.bfloat16),
-            pltpu.VMEM((2 * each, LANES), jnp.float32),
-            pltpu.VMEM((strata_dev, width), jnp.bfloat16),
+            pltpu.VMEM((2 * (chips - middle) * cap, width), jnp.bfloat16),
+            pltpu.VMEM((2 * (chips - middle) * cap, LANES), jnp.float32),
         ],
-        compiler_params=params(24),
+        compiler_params=params(20),
         name="late",
-    )(units_a, col_a, facts, extra, blocks_a[0], *blocks_b)
+    )(units_a, col_a, facts_a, units_m, col_m, facts_m, cents, *blocks_b[middle:])
     got = lax.all_to_all(
         sent.reshape(shards * groups, 4, LANES), AXES, 0, 0, tiled=True
     ).reshape(shards * groups * 4, LANES)

time: 68.7 us -> 66.6 us (0.969)
  blocking collectives: 32 us -> 30.1 us
    pallas_call x1, Pallas kernels: 3.81 us -> 1.75 us  [body(): pl.pallas_call(functools.partial(late_kernel, order, cap, groups), out_sh...]
    pallas_call x0 -> x1, Pallas kernels: none -> 1.88 us  [body(): pl.pallas_call(functools.partial(mid_kernel, middle, cap), out_shape=[sha...]
    all_to_all x1, blocking collectives: 32 us -> 30.1 us  [body(): lax.all_to_all(sent.reshape(shards * groups, 4, LANES), AXES, 0, 0, tiled...]
  transfers between devices with their start and end apart: 9 -> 9, of which waited for: 2 -> 2; matrix products, arithmetic and copies ran while one was open for 0% -> 0% of each run, Pallas kernels for 8% -> 11%
where the time goes in v5:
time: 66.6 us; the launch traced here: 66.2 us
  blocking collectives  30.1 us (45%)
  starting transfers between devices  17.1 us (26%)
  Pallas kernels  9.73 us (15%)
  waiting for transfers between devices  6.47 us (10%)
  local copies, waits for them, and re-layouts  2.66 us (4%)
    all_to_all x1, blocking collectives, body(): lax.all_to_all(sent.reshape(shards * groups, 4, LANES), AXES, 0, 0, tiled...  30.1 us
    ppermute x9, starting transfers between devices, send(): lax.ppermute(array, AXES, [(b * groups + g, to_b * groups + to_g) for (b,...  17.1 us
    ppermute x9, waiting for transfers between devices, send(): lax.ppermute(array, AXES, [(b * groups + g, to_b * groups + to_g) for (b,...  6.47 us
    unnamed x6, local copies, waits for them, and re-layouts  2.66 us
    pallas_call x1, Pallas kernels, body(): pl.pallas_call(functools.partial(near_kernel, chips, cap), out_shape=[sha...  2.07 us
    pallas_call x1, Pallas kernels, body(): pl.pallas_call(functools.partial(mid_kernel, middle, cap), out_shape=[sha...  1.88 us
    pallas_call x1, Pallas kernels, body(): pl.pallas_call(functools.partial(late_kernel, order, cap, groups), out_sh...  1.75 us
    pallas_call x1, Pallas kernels, body(): pl.pallas_call(functools.partial(early_kernel, chips, cap, strata_dev), o...  1.62 us
  transfers between devices with their start and end apart: 9, of which 2 were waited for; matrix products, arithmetic and copies ran while one was open for 0% of the time, Pallas kernels for 11%

profile of v5, /device:TPU:0, one launch (start us, length us, event | category | flops | bytes accessed | tf_op | source)
XLA Modules:
  0.0 66.2 jit_solution(13982120290071355625)
XLA Ops:
  0.0 0.7 %collective-permute-start.5 = (bf16[512,1024]{1,0:T(8,128)(2,1)}, bf16[512,1024]{1,0:T(8,128)(2,1)S(1)}, u32[]{:S(2)}, u32[]{:S(2)}) collective-permute-start(bf16[512,1024]{1,0:T(8,128)(2,1)} %bitcast.4), channel_id=1, source_target_pairs={{1,16},{3,18},{5,20},{7,22},{9,24},{11,26},{13,28},{15,30},{16,1},... | collective-permute-start | bytes 3145736 | tf_op jit(solution)/shard_map/ppermute | solution.py:294
  0.7 0.0 copy-start
  0.7 1.2 %copy-done = bf16[1,512,1024]{2,1,0:T(8,128)(2,1)S(1)} copy-done((bf16[1,512,1024]{2,1,0:T(8,128)(2,1)S(1)}, bf16[1,512,1024]{2,1,0:T(8,128)(2,1)}, u32[]{:S(2)}) %copy-start) | copy-done | bytes 1048600
  2.0 0.0 copy-start.1
  2.0 0.8 %copy-done.1 = bf16[1,16,1024]{2,1,0:T(8,128)(2,1)S(1)} copy-done((bf16[1,16,1024]{2,1,0:T(8,128)(2,1)S(1)}, bf16[1,16,1024]{2,1,0:T(8,128)(2,1)}, u32[]{:S(2)}) %copy-start.1) | copy-done | bytes 32792
  2.7 0.0 copy-start.2
  2.7 0.7 %copy-done.2 = s32[1,512]{1,0:T(1,128)S(1)} copy-done((s32[1,512]{1,0:T(1,128)S(1)}, s32[1,512]{1,0:T(1,128)}, u32[]{:S(2)}) %copy-start.2) | copy-done | bytes 2072
  3.4 2.1 %near.1 = (bf16[2192,128]{1,0:T(8,128)(2,1)S(1)}, bf16[2064,128]{1,0:T(8,128)(2,1)S(1)}, bf16[2064,128]{1,0:T(8,128)(2,1)S(1)}, bf16[2064,128]{1,0:T(8,128)(2,1)S(1)}, bf16[32,1024]{1,0:T(8,128)(2,1)S(1)}) custom-call(s32[1,512]{1,0:T(1,128)S(1)} %copy-done.2, bf16[16,1024]{1,0:T(8,128)(2,1)S(1)} %bitcast.8, bf16[512,1024]{1,0:T(8,128)(2,1)S(1)} %bitcast.5), custom_call_target="tpu_custom_call" | custom-call | tf_op jit(solution)/shard_map/near/pallas_call | solution.py:305
  5.5 7.3 %collective-permute-start = (bf16[2192,128]{1,0:T(8,128)(2,1)S(1)}, bf16[2192,128]{1,0:T(8,128)(2,1)S(1)}, u32[]{:S(2)}, u32[]{:S(2)}) collective-permute-start(bf16[2192,128]{1,0:T(8,128)(2,1)S(1)} %get-tuple-element.23), channel_id=1, source_target_pairs={{0,1},{2,3},{4,5},{6,7},{8,9},{10,11},{12,13},{14,15},{17,16},{19,... | collective-permute-start | bytes 1683464 | tf_op jit(solution)/shard_map/ppermute | solution.py:294
  12.8 3.4 %collective-permute-start.1 = (bf16[2064,128]{1,0:T(8,128)(2,1)S(1)}, bf16[2064,128]{1,0:T(8,128)(2,1)S(1)}, u32[]{:S(2)}, u32[]{:S(2)}) collective-permute-start(bf16[2064,128]{1,0:T(8,128)(2,1)S(1)} %get-tuple-element.24), channel_id=1, source_target_pairs={{0,13},{2,15},{4,9},{6,11},{8,5},{10,7},{12,1},{14,3},{17,28},{19,... | collective-permute-start | bytes 1585160 | tf_op jit(solution)/shard_map/ppermute | solution.py:294
  16.2 0.7 %collective-permute-start.4 = (bf16[32,1024]{1,0:T(8,128)(2,1)S(1)}, bf16[32,1024]{1,0:T(8,128)(2,1)S(1)}, u32[]{:S(2)}, u32[]{:S(2)}) collective-permute-start(bf16[32,1024]{1,0:T(8,128)(2,1)S(1)} %get-tuple-element.31), channel_id=1, source_target_pairs={{1,16},{3,18},{5,20},{7,22},{9,24},{11,26},{13,28},{15,30},{16,1},... | collective-permute-start | bytes 196616 | tf_op jit(solution)/shard_map/ppermute | solution.py:294
  16.9 1.6 %collective-permute-start.2 = (bf16[2064,128]{1,0:T(8,128)(2,1)S(1)}, bf16[2064,128]{1,0:T(8,128)(2,1)S(1)}, u32[]{:S(2)}, u32[]{:S(2)}) collective-permute-start(bf16[2064,128]{1,0:T(8,128)(2,1)S(1)} %get-tuple-element.25), channel_id=1, source_target_pairs={{0,9},{2,11},{4,13},{6,15},{8,1},{10,3},{12,5},{14,7},{17,24},{19,... | collective-permute-start | bytes 1585160 | tf_op jit(solution)/shard_map/ppermute | solution.py:294
  18.5 0.0 collective-permute-done.rest_0_.block0
  18.5 1.3 %collective-permute-start.3 = (bf16[2064,128]{1,0:T(8,128)(2,1)S(1)}, bf16[2064,128]{1,0:T(8,128)(2,1)S(1)}, u32[]{:S(2)}, u32[]{:S(2)}) collective-permute-start(bf16[2064,128]{1,0:T(8,128)(2,1)S(1)} %get-tuple-element.27), channel_id=1, source_target_pairs={{0,5},{2,7},{4,1},{6,3},{8,13},{10,15},{12,9},{14,11},{17,20},{19,... | collective-permute-start | bytes 1585160 | tf_op jit(solution)/shard_map/ppermute | solution.py:294
  19.8 0.0 collective-permute-done.4.extra
  19.8 0.0 collective-permute-done.5.rows_ref
  19.8 1.6 %far.1 = (bf16[2064,128]{1,0:T(8,128)(2,1)S(1)}, bf16[2064,128]{1,0:T(8,128)(2,1)S(1)}, bf16[2064,128]{1,0:T(8,128)(2,1)S(1)}, bf16[2064,128]{1,0:T(8,128)(2,1)S(1)}) custom-call(bf16[32,1024]{1,0:T(8,128)(2,1)S(1)} %collective-permute-done.4.extra, bf16[512,1024]{1,0:T(8,128)(2,1)S(1)} %collective-permute-done.5.rows_ref), custom_call_target="tpu_custom_call" | custom-call | tf_op jit(solution)/shard_map/far/pallas_call | solution.py:330
  21.4 0.7 %collective-permute-start.6 = (bf16[2064,128]{1,0:T(8,128)(2,1)S(1)}, bf16[2064,128]{1,0:T(8,128)(2,1)S(1)}, u32[]{:S(2)}, u32[]{:S(2)}) collective-permute-start(bf16[2064,128]{1,0:T(8,128)(2,1)S(1)} %get-tuple-element.33), channel_id=1, source_target_pairs={{1,13},{3,15},{5,9},{7,11},{9,5},{11,7},{13,1},{15,3},{16,28},{18,... | collective-permute-start | bytes 1585160 | tf_op jit(solution)/shard_map/ppermute | solution.py:294
  22.1 0.7 %collective-permute-start.7 = (bf16[2064,128]{1,0:T(8,128)(2,1)S(1)}, bf16[2064,128]{1,0:T(8,128)(2,1)S(1)}, u32[]{:S(2)}, u32[]{:S(2)}) collective-permute-start(bf16[2064,128]{1,0:T(8,128)(2,1)S(1)} %get-tuple-element.39), channel_id=1, source_target_pairs={{1,9},{3,11},{5,13},{7,15},{9,1},{11,3},{13,5},{15,7},{16,24},{18,... | collective-permute-start | bytes 1585160 | tf_op jit(solution)/shard_map/ppermute | solution.py:294
  22.8 1.5 %collective-permute-done.1.rest_1_ = bf16[2064,128]{1,0:T(8,128)(2,1)S(1)} collective-permute-done((bf16[2064,128]{1,0:T(8,128)(2,1)S(1)}, bf16[2064,128]{1,0:T(8,128)(2,1)S(1)}, u32[]{:S(2)}, u32[]{:S(2)}) %collective-permute-start.1) | collective-permute-done | bytes 528416 | tf_op jit(solution)/shard_map/ppermute | solution.py:294
  24.3 0.7 %collective-permute-start.8 = (bf16[2064,128]{1,0:T(8,128)(2,1)S(1)}, bf16[2064,128]{1,0:T(8,128)(2,1)S(1)}, u32[]{:S(2)}, u32[]{:S(2)}) collective-permute-start(bf16[2064,128]{1,0:T(8,128)(2,1)S(1)} %get-tuple-element.40), channel_id=1, source_target_pairs={{1,5},{3,7},{5,1},{7,3},{9,13},{11,15},{13,9},{15,11},{16,20},{18,... | collective-permute-start | bytes 1585160 | tf_op jit(solution)/shard_map/ppermute | solution.py:294
  25.0 5.0 %collective-permute-done.2.rest_2_ = bf16[2064,128]{1,0:T(8,128)(2,1)S(1)} collective-permute-done((bf16[2064,128]{1,0:T(8,128)(2,1)S(1)}, bf16[2064,128]{1,0:T(8,128)(2,1)S(1)}, u32[]{:S(2)}, u32[]{:S(2)}) %collective-permute-start.2) | collective-permute-done | bytes 528416 | tf_op jit(solution)/shard_map/ppermute | solution.py:294
  30.0 0.0 collective-permute-done.3.rest_3_
  30.0 1.6 %early.1 = (bf16[1024,1024]{1,0:T(8,128)(2,1)S(1)}, f32[1024,128]{1,0:T(8,128)S(1)}, f32[8,512]{1,0:T(8,128)S(1)}) custom-call(bf16[2192,128]{1,0:T(8,128)(2,1)S(1)} %collective-permute-done.rest_0_.block0, bf16[2064,128]{1,0:T(8,128)(2,1)S(1)} %collective-permute-done.1.rest_1_, bf16[2064,128]{1,0:T(8,128)(2,1)S(1)} %collective-permute-done.2.rest_2_, ...), custom_call_target="tpu_custom_call" | custom-call | tf_op jit(solution)/shard_map/early/pallas_call | solution.py:345
  31.6 0.0 collective-permute-done.6.rest_1_
  31.6 1.9 %mid.1 = (bf16[512,1024]{1,0:T(8,128)(2,1)S(1)}, f32[512,128]{1,0:T(8,128)S(1)}, f32[8,256]{1,0:T(8,128)S(1)}, f32[8,512]{1,0:T(8,128)S(1)}, bf16[32,1024]{1,0:T(8,128)(2,1)S(1)}) custom-call(bf16[1024,1024]{1,0:T(8,128)(2,1)S(1)} %get-tuple-element.28.units_a, f32[1024,128]{1,0:T(8,128)S(1)} %get-tuple-element.29.col_a, ...), custom_call_target="tpu_custom_call" | custom-call | tf_op jit(solution)/shard_map/mid/pallas_call | solution.py:358
  33.5 0.0 collective-permute-done.7.rest_0_
  33.5 0.0 collective-permute-done.8.rest_1_
  33.5 1.8 %late.1 = f32[128,128]{1,0:T(8,128)S(1)} custom-call(bf16[1024,1024]{1,0:T(8,128)(2,1)S(1)} %get-tuple-element.28.units_a, f32[1024,128]{1,0:T(8,128)S(1)} %get-tuple-element.29.col_a, f32[8,512]{1,0:T(8,128)S(1)} %get-tuple-element.34.facts_a, bf16[512,1024]{1,0:T(8,128)(2,1)S(1)} %get-tuple-element.35.units_m, f32[512,128]{1,0:T(8,128)S(1)} %get-tuple-element.36.col_m, ...), custom_call_target="tpu_custom_call" | custom-call | tf_op jit(solution)/shard_map/late/pallas_call | solution.py:372
  35.3 30.1 %all_to_all.5 = f32[32,4,128]{2,1,0:T(4,128)S(1)} all-to-all(f32[32,4,128]{2,1,0:T(4,128)S(1)} %bitcast.6), channel_id=1, replica_groups=mesh['blk'=8,'grp'=4] {'blk','grp'}, dimensions={0} | all-to-all | bytes 131072 | tf_op jit(solution)/shard_map/all_to_all | solution.py:384
  65.4 0.8 %finish.1 = f32[1,512]{1,0:T(1,128)} custom-call(s32[1,512]{1,0:T(1,128)S(1)} %copy-done.2, f32[128,128]{1,0:T(8,128)S(1)} %bitcast.7), custom_call_target="tpu_custom_call" | custom-call | tf_op jit(solution)/shard_map/finish/pallas_call | solution.py:387
Async XLA Ops:
  0.0 19.8 %collective-permute-start.5 = (bf16[512,1024]{1,0:T(8,128)(2,1)}, bf16[512,1024]{1,0:T(8,128)(2,1)S(1)}, u32[]{:S(2)}, u32[]{:S(2)}) collective-permute-start(bf16[512,1024]{1,0:T(8,128)(2,1)} %bitcast.4), channel_id=1, source_target_pairs={{1,16},{3,18},{5,20},{7,22},{9,24},{11,26},{13,28},{15,30},{16,1},... | collective-permute-start | bytes 3145736 | tf_op jit(solution)/shard_map/ppermute | solution.py:294
  0.7 1.2 %copy-start = (bf16[1,512,1024]{2,1,0:T(8,128)(2,1)S(1)}, bf16[1,512,1024]{2,1,0:T(8,128)(2,1)}, u32[]{:S(2)}) copy-start(bf16[1,512,1024]{2,1,0:T(8,128)(2,1)} %param.3) | copy-start | bytes 3145732
  2.0 0.8 %copy-start.1 = (bf16[1,16,1024]{2,1,0:T(8,128)(2,1)S(1)}, bf16[1,16,1024]{2,1,0:T(8,128)(2,1)}, u32[]{:S(2)}) copy-start(bf16[1,16,1024]{2,1,0:T(8,128)(2,1)} %param.5) | copy-start | bytes 98308
  2.7 0.7 %copy-start.2 = (s32[1,512]{1,0:T(1,128)S(1)}, s32[1,512]{1,0:T(1,128)}, u32[]{:S(2)}) copy-start(s32[1,512]{1,0:T(1,128)} %ids_ref.1) | copy-start | bytes 6148
  5.5 13.0 %collective-permute-start = (bf16[2192,128]{1,0:T(8,128)(2,1)S(1)}, bf16[2192,128]{1,0:T(8,128)(2,1)S(1)}, u32[]{:S(2)}, u32[]{:S(2)}) collective-permute-start(bf16[2192,128]{1,0:T(8,128)(2,1)S(1)} %get-tuple-element.23), channel_id=1, source_target_pairs={{0,1},{2,3},{4,5},{6,7},{8,9},{10,11},{12,13},{14,15},{17,16},{19,... | collective-permute-start | bytes 1683464 | tf_op jit(solution)/shard_map/ppermute | solution.py:294
  12.8 11.6 %collective-permute-start.1 = (bf16[2064,128]{1,0:T(8,128)(2,1)S(1)}, bf16[2064,128]{1,0:T(8,128)(2,1)S(1)}, u32[]{:S(2)}, u32[]{:S(2)}) collective-permute-start(bf16[2064,128]{1,0:T(8,128)(2,1)S(1)} %get-tuple-element.24), channel_id=1, source_target_pairs={{0,13},{2,15},{4,9},{6,11},{8,5},{10,7},{12,1},{14,3},{17,28},{19,... | collective-permute-start | bytes 1585160 | tf_op jit(solution)/shard_map/ppermute | solution.py:294
  16.2 3.6 %collective-permute-start.4 = (bf16[32,1024]{1,0:T(8,128)(2,1)S(1)}, bf16[32,1024]{1,0:T(8,128)(2,1)S(1)}, u32[]{:S(2)}, u32[]{:S(2)}) collective-permute-start(bf16[32,1024]{1,0:T(8,128)(2,1)S(1)} %get-tuple-element.31), channel_id=1, source_target_pairs={{1,16},{3,18},{5,20},{7,22},{9,24},{11,26},{13,28},{15,30},{16,1},... | collective-permute-start | bytes 196616 | tf_op jit(solution)/shard_map/ppermute | solution.py:294
  16.9 13.1 %collective-permute-start.2 = (bf16[2064,128]{1,0:T(8,128)(2,1)S(1)}, bf16[2064,128]{1,0:T(8,128)(2,1)S(1)}, u32[]{:S(2)}, u32[]{:S(2)}) collective-permute-start(bf16[2064,128]{1,0:T(8,128)(2,1)S(1)} %get-tuple-element.25), channel_id=1, source_target_pairs={{0,9},{2,11},{4,13},{6,15},{8,1},{10,3},{12,5},{14,7},{17,24},{19,... | collective-permute-start | bytes 1585160 | tf_op jit(solution)/shard_map/ppermute | solution.py:294
  18.5 11.5 %collective-permute-start.3 = (bf16[2064,128]{1,0:T(8,128)(2,1)S(1)}, bf16[2064,128]{1,0:T(8,128)(2,1)S(1)}, u32[]{:S(2)}, u32[]{:S(2)}) collective-permute-start(bf16[2064,128]{1,0:T(8,128)(2,1)S(1)} %get-tuple-element.27), channel_id=1, source_target_pairs={{0,5},{2,7},{4,1},{6,3},{8,13},{10,15},{12,9},{14,11},{17,20},{19,... | collective-permute-start | bytes 1585160 | tf_op jit(solution)/shard_map/ppermute | solution.py:294
  21.4 10.2 %collective-permute-start.6 = (bf16[2064,128]{1,0:T(8,128)(2,1)S(1)}, bf16[2064,128]{1,0:T(8,128)(2,1)S(1)}, u32[]{:S(2)}, u32[]{:S(2)}) collective-permute-start(bf16[2064,128]{1,0:T(8,128)(2,1)S(1)} %get-tuple-element.33), channel_id=1, source_target_pairs={{1,13},{3,15},{5,9},{7,11},{9,5},{11,7},{13,1},{15,3},{16,28},{18,... | collective-permute-start | bytes 1585160 | tf_op jit(solution)/shard_map/ppermute | solution.py:294
  22.1 11.4 %collective-permute-start.7 = (bf16[2064,128]{1,0:T(8,128)(2,1)S(1)}, bf16[2064,128]{1,0:T(8,128)(2,1)S(1)}, u32[]{:S(2)}, u32[]{:S(2)}) collective-permute-start(bf16[2064,128]{1,0:T(8,128)(2,1)S(1)} %get-tuple-element.39), channel_id=1, source_target_pairs={{1,9},{3,11},{5,13},{7,15},{9,1},{11,3},{13,5},{15,7},{16,24},{18,... | collective-permute-start | bytes 1585160 | tf_op jit(solution)/shard_map/ppermute | solution.py:294
  24.3 9.2 %collective-permute-start.8 = (bf16[2064,128]{1,0:T(8,128)(2,1)S(1)}, bf16[2064,128]{1,0:T(8,128)(2,1)S(1)}, u32[]{:S(2)}, u32[]{:S(2)}) collective-permute-start(bf16[2064,128]{1,0:T(8,128)(2,1)S(1)} %get-tuple-element.40), channel_id=1, source_target_pairs={{1,5},{3,7},{5,1},{7,3},{9,13},{11,15},{13,9},{15,11},{16,20},{18,... | collective-permute-start | bytes 1585160 | tf_op jit(solution)/shard_map/ppermute | solution.py:294

commit v6 on v5

--- a/solution.py
+++ b/solution.py
@@ -98,22 +98,26 @@
     for load in loads:
         load.start()
     cent = unit_values(cent_ref[...])
-    extra[:strata_dev, :] = cent
     depth = width // LANES * 2 * cap + TAIL
     for c in range(width // LANES):
         at = depth + c * strata_dev
         outs[0][at : at + strata_dev, :] = cent[:, c * LANES : (c + 1) * LANES]
     loads[0].wait()
     ids = ids_ref[...].astype(jnp.float32)
-    extra[strata_dev:, :] = jnp.zeros((TAIL, width), jnp.bfloat16)
-    extra[strata_dev:, :rows] = jnp.broadcast_to(ids, (TAIL, rows)).astype(jnp.bfloat16)
+    extra[...] = jnp.concatenate(
+        [
+            jnp.broadcast_to(ids[:, i * LANES : (i + 1) * LANES], (TAIL // 4, LANES))
+            for i in range(rows // LANES)
+        ],
+        axis=0,
+    ).astype(jnp.bfloat16)
     pack_into(ids, loads[1:], rows_ref, outs, held, pick, cap, strata_dev)
 
 
 def far_kernel(chips, cap, strata_dev, extra, rows_ref, *rest):
     outs, (held, pick) = rest[:chips], rest[chips:]
-    rows = rows_ref.shape[0]
-    ids = extra[strata_dev:, :rows].astype(jnp.float32)[:1, :]
+    spread = extra[...].astype(jnp.float32)
+    ids = jnp.concatenate([spread[i : i + 1, :] for i in range(0, TAIL, TAIL // 4)], axis=1)
     pack_into(ids, [], rows_ref, outs, held, pick, cap, strata_dev)
 
 
@@ -196,14 +200,14 @@
         facts[2 + r : 3 + r, :] = row
 
 
-def mid_kernel(count, cap, units_a, col_a, facts_a, extra, block0, *rest):
+def mid_kernel(count, cap, units_a, col_a, facts_a, far_cents, block0, *rest):
     blocks, (units, id_col, facts, facts_out, cents) = rest[:count], rest[count:]
     strata_dev, width = cents.shape[0] // 2, cents.shape[1]
     depth = width // LANES * 2 * cap + TAIL
     for c in range(width // LANES):
         at = depth + c * strata_dev
         cents[:strata_dev, c * LANES : (c + 1) * LANES] = block0[at : at + strata_dev, :]
-    cents[strata_dev:, :] = extra[:strata_dev, :]
+    cents[strata_dev:, :] = unit_values(far_cents[...])
     ids = unpack(blocks, cap, strata_dev, units, id_col)
     (old,), density = join([(units_a, col_a, facts_a)], units, id_col, ids)
     for r, row in enumerate(ids):
@@ -307,7 +311,7 @@
         out_shape=[
             shape(depth + (chunks * strata_dev if d == 0 else 0), LANES) for d in range(chips)
         ]
-        + [shape(strata_dev + TAIL, width)],
+        + [shape(TAIL, LANES)],
         in_specs=[ANY, VMEM, ANY],
         out_specs=[VMEM] * (chips + 1),
         scratch_shapes=[
@@ -336,6 +340,8 @@
         compiler_params=params(20),
         name="far",
     )(extra, far_rows)
+    far_cents, _ = lax.optimization_barrier((centroids[0], blocks_b[0]))
+    far_cents = send(far_cents, swap)
     blocks_b = [
         blocks_b[d]
         if d == 0
@@ -368,7 +374,7 @@
         out_specs=[VMEM] * 5,
         compiler_params=params(20),
         name="mid",
-    )(units_a, col_a, facts, extra, blocks_a[0], *blocks_b[:middle])
+    )(units_a, col_a, facts, far_cents, blocks_a[0], *blocks_b[:middle])
     sent = pl.pallas_call(
         functools.partial(late_kernel, order, cap, groups),
         out_shape=jax.ShapeDtypeStruct((shards * groups * 4, LANES), jnp.float32),

time: 66.6 us -> 65.3 us (0.980)
  blocking collectives: 30.1 us -> 28.8 us
    all_to_all x1, blocking collectives: 30.1 us -> 28.8 us  [body(): lax.all_to_all(sent.reshape(shards * groups, 4, LANES), AXES, 0, 0, tiled...]
    ppermute x9 -> x10, waiting for transfers between devices: 6.47 us -> 5.9 us  [send(): lax.ppermute(array, AXES, [(b * groups + g, to_b * groups + to_g) for (b,...]
    ppermute x9 -> x10, starting transfers between devices: 17.1 us -> 17.6 us  [send(): lax.ppermute(array, AXES, [(b * groups + g, to_b * groups + to_g) for (b,...]
  transfers between devices with their start and end apart: 9 -> 10, of which waited for: 2 -> 2; matrix products, arithmetic and copies ran while one was open for 0% -> 0% of each run, Pallas kernels for 11% -> 11%
where the time goes in v6:
time: 65.3 us; the launch traced here: 64.9 us
  blocking collectives  28.8 us (44%)
  starting transfers between devices  17.6 us (27%)
  Pallas kernels  9.74 us (15%)
  waiting for transfers between devices  5.9 us (9%)
  local copies, waits for them, and re-layouts  2.66 us (4%)
    all_to_all x1, blocking collectives, body(): lax.all_to_all(sent.reshape(shards * groups, 4, LANES), AXES, 0, 0, tiled...  28.8 us
    ppermute x10, starting transfers between devices, send(): lax.ppermute(array, AXES, [(b * groups + g, to_b * groups + to_g) for (b,...  17.6 us
    ppermute x10, waiting for transfers between devices, send(): lax.ppermute(array, AXES, [(b * groups + g, to_b * groups + to_g) for (b,...  5.9 us
    unnamed x6, local copies, waits for them, and re-layouts  2.66 us
    pallas_call x1, Pallas kernels, body(): pl.pallas_call(functools.partial(near_kernel, chips, cap), out_shape=[sha...  2.07 us
    pallas_call x1, Pallas kernels, body(): pl.pallas_call(functools.partial(mid_kernel, middle, cap), out_shape=[sha...  1.88 us
    pallas_call x1, Pallas kernels, body(): pl.pallas_call(functools.partial(late_kernel, order, cap, groups), out_sh...  1.75 us
    pallas_call x1, Pallas kernels, body(): pl.pallas_call(functools.partial(early_kernel, chips, cap, strata_dev), o...  1.62 us
  transfers between devices with their start and end apart: 10, of which 2 were waited for; matrix products, arithmetic and copies ran while one was open for 0% of the time, Pallas kernels for 11%

profile of v6, /device:TPU:0, one launch (start us, length us, event | category | flops | bytes accessed | tf_op | source)
XLA Modules:
  0.0 64.9 jit_solution(17589822731382472884)
XLA Ops:
  0.0 0.7 %collective-permute-start.5 = (bf16[512,1024]{1,0:T(8,128)(2,1)}, bf16[512,1024]{1,0:T(8,128)(2,1)S(1)}, u32[]{:S(2)}, u32[]{:S(2)}) collective-permute-start(bf16[512,1024]{1,0:T(8,128)(2,1)} %bitcast.4), channel_id=1, source_target_pairs={{1,16},{3,18},{5,20},{7,22},{9,24},{11,26},{13,28},{15,30},{16,1},... | collective-permute-start | bytes 3145736 | tf_op jit(solution)/shard_map/ppermute | solution.py:298
  0.7 0.0 copy-start
  0.7 1.2 %copy-done = bf16[1,512,1024]{2,1,0:T(8,128)(2,1)S(1)} copy-done((bf16[1,512,1024]{2,1,0:T(8,128)(2,1)S(1)}, bf16[1,512,1024]{2,1,0:T(8,128)(2,1)}, u32[]{:S(2)}) %copy-start) | copy-done | bytes 1048600
  2.0 0.8 %copy-done.1 = bf16[1,16,1024]{2,1,0:T(8,128)(2,1)S(1)} copy-done((bf16[1,16,1024]{2,1,0:T(8,128)(2,1)S(1)}, bf16[1,16,1024]{2,1,0:T(8,128)(2,1)}, u32[]{:S(2)}) %copy-start.1) | copy-done | bytes 32792
  2.7 0.0 copy-start.2
  2.7 0.7 %copy-done.2 = s32[1,512]{1,0:T(1,128)S(1)} copy-done((s32[1,512]{1,0:T(1,128)S(1)}, s32[1,512]{1,0:T(1,128)}, u32[]{:S(2)}) %copy-start.2) | copy-done | bytes 2072
  3.4 2.1 %near.1 = (bf16[2192,128]{1,0:T(8,128)(2,1)S(1)}, bf16[2064,128]{1,0:T(8,128)(2,1)S(1)}, bf16[2064,128]{1,0:T(8,128)(2,1)S(1)}, bf16[2064,128]{1,0:T(8,128)(2,1)S(1)}, bf16[16,128]{1,0:T(8,128)(2,1)S(1)}) custom-call(s32[1,512]{1,0:T(1,128)S(1)} %copy-done.2, bf16[16,1024]{1,0:T(8,128)(2,1)S(1)} %bitcast.8, bf16[512,1024]{1,0:T(8,128)(2,1)S(1)} %bitcast.5), custom_call_target="tpu_custom_call" | custom-call | tf_op jit(solution)/shard_map/near/pallas_call | solution.py:309
  5.5 7.3 %collective-permute-start = (bf16[2192,128]{1,0:T(8,128)(2,1)S(1)}, bf16[2192,128]{1,0:T(8,128)(2,1)S(1)}, u32[]{:S(2)}, u32[]{:S(2)}) collective-permute-start(bf16[2192,128]{1,0:T(8,128)(2,1)S(1)} %get-tuple-element.24), channel_id=1, source_target_pairs={{0,1},{2,3},{4,5},{6,7},{8,9},{10,11},{12,13},{14,15},{17,16},{19,... | collective-permute-start | bytes 1683464 | tf_op jit(solution)/shard_map/ppermute | solution.py:298
  12.8 3.4 %collective-permute-start.1 = (bf16[2064,128]{1,0:T(8,128)(2,1)S(1)}, bf16[2064,128]{1,0:T(8,128)(2,1)S(1)}, u32[]{:S(2)}, u32[]{:S(2)}) collective-permute-start(bf16[2064,128]{1,0:T(8,128)(2,1)S(1)} %get-tuple-element.25), channel_id=1, source_target_pairs={{0,13},{2,15},{4,9},{6,11},{8,5},{10,7},{12,1},{14,3},{17,28},{19,... | collective-permute-start | bytes 1585160 | tf_op jit(solution)/shard_map/ppermute | solution.py:298
  16.2 1.3 %collective-permute-start.2 = (bf16[2064,128]{1,0:T(8,128)(2,1)S(1)}, bf16[2064,128]{1,0:T(8,128)(2,1)S(1)}, u32[]{:S(2)}, u32[]{:S(2)}) collective-permute-start(bf16[2064,128]{1,0:T(8,128)(2,1)S(1)} %get-tuple-element.26), channel_id=1, source_target_pairs={{0,9},{2,11},{4,13},{6,15},{8,1},{10,3},{12,5},{14,7},{17,24},{19,... | collective-permute-start | bytes 1585160 | tf_op jit(solution)/shard_map/ppermute | solution.py:298
  17.5 0.7 %collective-permute-start.4 = (bf16[16,128]{1,0:T(8,128)(2,1)S(1)}, bf16[16,128]{1,0:T(8,128)(2,1)S(1)}, u32[]{:S(2)}, u32[]{:S(2)}) collective-permute-start(bf16[16,128]{1,0:T(8,128)(2,1)S(1)} %get-tuple-element.32), channel_id=1, source_target_pairs={{1,16},{3,18},{5,20},{7,22},{9,24},{11,26},{13,28},{15,30},{16,1},... | collective-permute-start | bytes 12296 | tf_op jit(solution)/shard_map/ppermute | solution.py:298
  18.2 0.0 collective-permute-done.rest_0_.block0
  18.2 1.5 %collective-permute-start.3 = (bf16[2064,128]{1,0:T(8,128)(2,1)S(1)}, bf16[2064,128]{1,0:T(8,128)(2,1)S(1)}, u32[]{:S(2)}, u32[]{:S(2)}) collective-permute-start(bf16[2064,128]{1,0:T(8,128)(2,1)S(1)} %get-tuple-element.28), channel_id=1, source_target_pairs={{0,5},{2,7},{4,1},{6,3},{8,13},{10,15},{12,9},{14,11},{17,20},{19,... | collective-permute-start | bytes 1585160 | tf_op jit(solution)/shard_map/ppermute | solution.py:298
  19.7 0.0 collective-permute-done.4.extra
  19.7 0.0 collective-permute-done.5.rows_ref
  19.7 1.6 %far.1 = (bf16[2064,128]{1,0:T(8,128)(2,1)S(1)}, bf16[2064,128]{1,0:T(8,128)(2,1)S(1)}, bf16[2064,128]{1,0:T(8,128)(2,1)S(1)}, bf16[2064,128]{1,0:T(8,128)(2,1)S(1)}) custom-call(bf16[16,128]{1,0:T(8,128)(2,1)S(1)} %collective-permute-done.4.extra, bf16[512,1024]{1,0:T(8,128)(2,1)S(1)} %collective-permute-done.5.rows_ref), custom_call_target="tpu_custom_call" | custom-call | tf_op jit(solution)/shard_map/far/pallas_call | solution.py:334
  21.3 0.7 %collective-permute-start.7 = (bf16[2064,128]{1,0:T(8,128)(2,1)S(1)}, bf16[2064,128]{1,0:T(8,128)(2,1)S(1)}, u32[]{:S(2)}, u32[]{:S(2)}) collective-permute-start(bf16[2064,128]{1,0:T(8,128)(2,1)S(1)} %get-tuple-element.35), channel_id=1, source_target_pairs={{1,13},{3,15},{5,9},{7,11},{9,5},{11,7},{13,1},{15,3},{16,28},{18,... | collective-permute-start | bytes 1585160 | tf_op jit(solution)/shard_map/ppermute | solution.py:298
  22.0 0.7 %collective-permute-start.8 = (bf16[2064,128]{1,0:T(8,128)(2,1)S(1)}, bf16[2064,128]{1,0:T(8,128)(2,1)S(1)}, u32[]{:S(2)}, u32[]{:S(2)}) collective-permute-start(bf16[2064,128]{1,0:T(8,128)(2,1)S(1)} %get-tuple-element.41), channel_id=1, source_target_pairs={{1,9},{3,11},{5,13},{7,15},{9,1},{11,3},{13,5},{15,7},{16,24},{18,... | collective-permute-start | bytes 1585160 | tf_op jit(solution)/shard_map/ppermute | solution.py:298
  22.8 0.9 %collective-permute-done.1.rest_1_ = bf16[2064,128]{1,0:T(8,128)(2,1)S(1)} collective-permute-done((bf16[2064,128]{1,0:T(8,128)(2,1)S(1)}, bf16[2064,128]{1,0:T(8,128)(2,1)S(1)}, u32[]{:S(2)}, u32[]{:S(2)}) %collective-permute-start.1) | collective-permute-done | bytes 528416 | tf_op jit(solution)/shard_map/ppermute | solution.py:298
  23.7 0.7 %collective-permute-start.9 = (bf16[2064,128]{1,0:T(8,128)(2,1)S(1)}, bf16[2064,128]{1,0:T(8,128)(2,1)S(1)}, u32[]{:S(2)}, u32[]{:S(2)}) collective-permute-start(bf16[2064,128]{1,0:T(8,128)(2,1)S(1)} %get-tuple-element.42), channel_id=1, source_target_pairs={{1,5},{3,7},{5,1},{7,3},{9,13},{11,15},{13,9},{15,11},{16,20},{18,... | collective-permute-start | bytes 1585160 | tf_op jit(solution)/shard_map/ppermute | solution.py:298
  24.4 5.0 %collective-permute-done.2.rest_2_ = bf16[2064,128]{1,0:T(8,128)(2,1)S(1)} collective-permute-done((bf16[2064,128]{1,0:T(8,128)(2,1)S(1)}, bf16[2064,128]{1,0:T(8,128)(2,1)S(1)}, u32[]{:S(2)}, u32[]{:S(2)}) %collective-permute-start.2) | collective-permute-done | bytes 528416 | tf_op jit(solution)/shard_map/ppermute | solution.py:298
  29.3 0.7 %collective-permute-start.6 = (bf16[16,1024]{1,0:T(8,128)(2,1)S(1)}, bf16[16,1024]{1,0:T(8,128)(2,1)S(1)}, u32[]{:S(2)}, u32[]{:S(2)}) collective-permute-start(bf16[16,1024]{1,0:T(8,128)(2,1)S(1)} %bitcast.9), channel_id=1, source_target_pairs={{1,16},{3,18},{5,20},{7,22},{9,24},{11,26},{13,28},{15,30},{16,1},... | collective-permute-start | bytes 98312 | tf_op jit(solution)/shard_map/ppermute | solution.py:298
  30.0 0.0 collective-permute-done.3.rest_3_
  30.0 1.6 %early.1 = (bf16[1024,1024]{1,0:T(8,128)(2,1)S(1)}, f32[1024,128]{1,0:T(8,128)S(1)}, f32[8,512]{1,0:T(8,128)S(1)}) custom-call(bf16[2192,128]{1,0:T(8,128)(2,1)S(1)} %collective-permute-done.rest_0_.block0, bf16[2064,128]{1,0:T(8,128)(2,1)S(1)} %collective-permute-done.1.rest_1_, bf16[2064,128]{1,0:T(8,128)(2,1)S(1)} %collective-permute-done.2.rest_2_, ...), custom_call_target="tpu_custom_call" | custom-call | tf_op jit(solution)/shard_map/early/pallas_call | solution.py:351
  31.6 0.0 collective-permute-done.6.far_cents
  31.6 0.0 collective-permute-done.7.rest_1_
  31.6 1.9 %mid.1 = (bf16[512,1024]{1,0:T(8,128)(2,1)S(1)}, f32[512,128]{1,0:T(8,128)S(1)}, f32[8,256]{1,0:T(8,128)S(1)}, f32[8,512]{1,0:T(8,128)S(1)}, bf16[32,1024]{1,0:T(8,128)(2,1)S(1)}) custom-call(bf16[1024,1024]{1,0:T(8,128)(2,1)S(1)} %get-tuple-element.29.units_a, f32[1024,128]{1,0:T(8,128)S(1)} %get-tuple-element.30.col_a, ...), custom_call_target="tpu_custom_call" | custom-call | tf_op jit(solution)/shard_map/mid/pallas_call | solution.py:364
  33.5 0.0 collective-permute-done.8.rest_0_
  33.5 0.0 collective-permute-done.9.rest_1_
  33.6 1.8 %late.1 = f32[128,128]{1,0:T(8,128)S(1)} custom-call(bf16[1024,1024]{1,0:T(8,128)(2,1)S(1)} %get-tuple-element.29.units_a, f32[1024,128]{1,0:T(8,128)S(1)} %get-tuple-element.30.col_a, f32[8,512]{1,0:T(8,128)S(1)} %get-tuple-element.36.facts_a, bf16[512,1024]{1,0:T(8,128)(2,1)S(1)} %get-tuple-element.37.units_m, f32[512,128]{1,0:T(8,128)S(1)} %get-tuple-element.38.col_m, ...), custom_call_target="tpu_custom_call" | custom-call | tf_op jit(solution)/shard_map/late/pallas_call | solution.py:378
  35.3 28.8 %all_to_all.5 = f32[32,4,128]{2,1,0:T(4,128)S(1)} all-to-all(f32[32,4,128]{2,1,0:T(4,128)S(1)} %bitcast.6), channel_id=1, replica_groups=mesh['blk'=8,'grp'=4] {'blk','grp'}, dimensions={0} | all-to-all | bytes 131072 | tf_op jit(solution)/shard_map/all_to_all | solution.py:390
  64.1 0.8 %finish.1 = f32[1,512]{1,0:T(1,128)} custom-call(s32[1,512]{1,0:T(1,128)S(1)} %copy-done.2, f32[128,128]{1,0:T(8,128)S(1)} %bitcast.7), custom_call_target="tpu_custom_call" | custom-call | tf_op jit(solution)/shard_map/finish/pallas_call | solution.py:393
  (1 shorter events, 0.0 us)
Async XLA Ops:
  0.0 19.7 %collective-permute-start.5 = (bf16[512,1024]{1,0:T(8,128)(2,1)}, bf16[512,1024]{1,0:T(8,128)(2,1)S(1)}, u32[]{:S(2)}, u32[]{:S(2)}) collective-permute-start(bf16[512,1024]{1,0:T(8,128)(2,1)} %bitcast.4), channel_id=1, source_target_pairs={{1,16},{3,18},{5,20},{7,22},{9,24},{11,26},{13,28},{15,30},{16,1},... | collective-permute-start | bytes 3145736 | tf_op jit(solution)/shard_map/ppermute | solution.py:298
  0.7 1.2 %copy-start = (bf16[1,512,1024]{2,1,0:T(8,128)(2,1)S(1)}, bf16[1,512,1024]{2,1,0:T(8,128)(2,1)}, u32[]{:S(2)}) copy-start(bf16[1,512,1024]{2,1,0:T(8,128)(2,1)} %param.3) | copy-start | bytes 3145732
  2.0 0.8 %copy-start.1 = (bf16[1,16,1024]{2,1,0:T(8,128)(2,1)S(1)}, bf16[1,16,1024]{2,1,0:T(8,128)(2,1)}, u32[]{:S(2)}) copy-start(bf16[1,16,1024]{2,1,0:T(8,128)(2,1)} %param.5) | copy-start | bytes 98308
  2.7 0.7 %copy-start.2 = (s32[1,512]{1,0:T(1,128)S(1)}, s32[1,512]{1,0:T(1,128)}, u32[]{:S(2)}) copy-start(s32[1,512]{1,0:T(1,128)} %ids_ref.1) | copy-start | bytes 6148
  5.5 12.7 %collective-permute-start = (bf16[2192,128]{1,0:T(8,128)(2,1)S(1)}, bf16[2192,128]{1,0:T(8,128)(2,1)S(1)}, u32[]{:S(2)}, u32[]{:S(2)}) collective-permute-start(bf16[2192,128]{1,0:T(8,128)(2,1)S(1)} %get-tuple-element.24), channel_id=1, source_target_pairs={{0,1},{2,3},{4,5},{6,7},{8,9},{10,11},{12,13},{14,15},{17,16},{19,... | collective-permute-start | bytes 1683464 | tf_op jit(solution)/shard_map/ppermute | solution.py:298
  12.8 10.9 %collective-permute-start.1 = (bf16[2064,128]{1,0:T(8,128)(2,1)S(1)}, bf16[2064,128]{1,0:T(8,128)(2,1)S(1)}, u32[]{:S(2)}, u32[]{:S(2)}) collective-permute-start(bf16[2064,128]{1,0:T(8,128)(2,1)S(1)} %get-tuple-element.25), channel_id=1, source_target_pairs={{0,13},{2,15},{4,9},{6,11},{8,5},{10,7},{12,1},{14,3},{17,28},{19,... | collective-permute-start | bytes 1585160 | tf_op jit(solution)/shard_map/ppermute | solution.py:298
  16.2 13.1 %collective-permute-start.2 = (bf16[2064,128]{1,0:T(8,128)(2,1)S(1)}, bf16[2064,128]{1,0:T(8,128)(2,1)S(1)}, u32[]{:S(2)}, u32[]{:S(2)}) collective-permute-start(bf16[2064,128]{1,0:T(8,128)(2,1)S(1)} %get-tuple-element.26), channel_id=1, source_target_pairs={{0,9},{2,11},{4,13},{6,15},{8,1},{10,3},{12,5},{14,7},{17,24},{19,... | collective-permute-start | bytes 1585160 | tf_op jit(solution)/shard_map/ppermute | solution.py:298
  17.5 2.2 %collective-permute-start.4 = (bf16[16,128]{1,0:T(8,128)(2,1)S(1)}, bf16[16,128]{1,0:T(8,128)(2,1)S(1)}, u32[]{:S(2)}, u32[]{:S(2)}) collective-permute-start(bf16[16,128]{1,0:T(8,128)(2,1)S(1)} %get-tuple-element.32), channel_id=1, source_target_pairs={{1,16},{3,18},{5,20},{7,22},{9,24},{11,26},{13,28},{15,30},{16,1},... | collective-permute-start | bytes 12296 | tf_op jit(solution)/shard_map/ppermute | solution.py:298
  18.2 11.8 %collective-permute-start.3 = (bf16[2064,128]{1,0:T(8,128)(2,1)S(1)}, bf16[2064,128]{1,0:T(8,128)(2,1)S(1)}, u32[]{:S(2)}, u32[]{:S(2)}) collective-permute-start(bf16[2064,128]{1,0:T(8,128)(2,1)S(1)} %get-tuple-element.28), channel_id=1, source_target_pairs={{0,5},{2,7},{4,1},{6,3},{8,13},{10,15},{12,9},{14,11},{17,20},{19,... | collective-permute-start | bytes 1585160 | tf_op jit(solution)/shard_map/ppermute | solution.py:298
  21.3 10.3 %collective-permute-start.7 = (bf16[2064,128]{1,0:T(8,128)(2,1)S(1)}, bf16[2064,128]{1,0:T(8,128)(2,1)S(1)}, u32[]{:S(2)}, u32[]{:S(2)}) collective-permute-start(bf16[2064,128]{1,0:T(8,128)(2,1)S(1)} %get-tuple-element.35), channel_id=1, source_target_pairs={{1,13},{3,15},{5,9},{7,11},{9,5},{11,7},{13,1},{15,3},{16,28},{18,... | collective-permute-start | bytes 1585160 | tf_op jit(solution)/shard_map/ppermute | solution.py:298
  22.0 11.5 %collective-permute-start.8 = (bf16[2064,128]{1,0:T(8,128)(2,1)S(1)}, bf16[2064,128]{1,0:T(8,128)(2,1)S(1)}, u32[]{:S(2)}, u32[]{:S(2)}) collective-permute-start(bf16[2064,128]{1,0:T(8,128)(2,1)S(1)} %get-tuple-element.41), channel_id=1, source_target_pairs={{1,9},{3,11},{5,13},{7,15},{9,1},{11,3},{13,5},{15,7},{16,24},{18,... | collective-permute-start | bytes 1585160 | tf_op jit(solution)/shard_map/ppermute | solution.py:298
  23.7 9.9 %collective-permute-start.9 = (bf16[2064,128]{1,0:T(8,128)(2,1)S(1)}, bf16[2064,128]{1,0:T(8,128)(2,1)S(1)}, u32[]{:S(2)}, u32[]{:S(2)}) collective-permute-start(bf16[2064,128]{1,0:T(8,128)(2,1)S(1)} %get-tuple-element.42), channel_id=1, source_target_pairs={{1,5},{3,7},{5,1},{7,3},{9,13},{11,15},{13,9},{15,11},{16,20},{18,... | collective-permute-start | bytes 1585160 | tf_op jit(solution)/shard_map/ppermute | solution.py:298
  29.3 2.3 %collective-permute-start.6 = (bf16[16,1024]{1,0:T(8,128)(2,1)S(1)}, bf16[16,1024]{1,0:T(8,128)(2,1)S(1)}, u32[]{:S(2)}, u32[]{:S(2)}) collective-permute-start(bf16[16,1024]{1,0:T(8,128)(2,1)S(1)} %bitcast.9), channel_id=1, source_target_pairs={{1,16},{3,18},{5,20},{7,22},{9,24},{11,26},{13,28},{15,30},{16,1},... | collective-permute-start | bytes 98312 | tf_op jit(solution)/shard_map/ppermute | solution.py:298

commit v7 on v6

v7 whole, which is shorter than its diff:
```python
import functools
import math

import jax
import jax.numpy as jnp
from jax import lax
from jax.experimental import pallas as pl
from jax.experimental.pallas import tpu as pltpu
from jax.sharding import PartitionSpec as P


base_term = 0.05
epsilon = 1e-06
LANES = 128
TAIL = 16
AXES = ("blk", "grp")

VMEM = pl.BlockSpec(memory_space=pltpu.VMEM)
ANY = pl.BlockSpec(memory_space=pl.ANY)


def params(mib):
    return pltpu.CompilerParams(vmem_limit_bytes=mib << 20)


def unit_values(rows):
    values = rows.astype(jnp.float32)
    mean = jnp.mean(values * values, axis=-1, keepdims=True)
    scaling = lax.rsqrt(mean + epsilon) / math.sqrt(rows.shape[-1])
    return (values * scaling).astype(jnp.bfloat16)


def across(left, right):
    return lax.dot_general(
        left, right, (((1,), (1,)), ((), ())), preferred_element_type=jnp.float32
    )


def is_inner(chips):
    me = lax.axis_index("blk")
    return (me % chips) // (chips // 2) != me // chips


def shard_of(k, chips, half):
    owner = half * chips + ((lax.axis_index("blk") % chips) ^ (k // 2))
    return owner ^ ((k % 2) * (chips + chips // 2))


def pack_into(ids, loads, rows_ref, outs, held, pick, cap, strata_dev, half):
    rows, width = rows_ref.shape
    chips = len(outs)
    shards = 2 * chips
    number = lax.broadcasted_iota(jnp.int32, (shards, 1), 0)
    lowest = (shard_of(number, chips, half) * strata_dev).astype(jnp.float32)
    begin = jnp.sum((ids < lowest).astype(jnp.float32), axis=1, keepdims=True)
    start = jnp.minimum(begin, float(rows - cap))
    number = lax.broadcasted_iota(jnp.int32, (shards * strata_dev, 1), 0)
    stratum = shard_of(number // strata_dev, chips, half) * strata_dev + number % strata_dev
    ends = jnp.sum((ids <= stratum.astype(jnp.float32)).astype(jnp.float32), axis=1, keepdims=True)
    slot = lax.broadcasted_iota(jnp.int32, (cap, rows), 0).astype(jnp.float32)
    row = lax.broadcasted_iota(jnp.int32, (cap, rows), 1).astype(jnp.float32)
    ahead = row - slot
    lane = lax.broadcasted_iota(jnp.int32, (1, LANES), 1).astype(jnp.float32)
    for k in range(shards):
        first = start[k : k + 1, :]
        pick[k * cap : (k + 1) * cap, :] = (ahead == first).astype(jnp.bfloat16)
        at = lane + first
        passed = (ends[k * strata_dev : (k + 1) * strata_dev, :] <= at).astype(jnp.float32)
        local = jnp.where(
            at >= begin[k : k + 1, :], jnp.sum(passed, axis=0, keepdims=True), float(strata_dev)
        )
        tail = width // LANES * 2 * cap + (k % 2) * 8
        outs[k // 2][tail : tail + 8, :] = jnp.broadcast_to(local, (8, LANES)).astype(jnp.bfloat16)
    step = rows // max(len(loads), 1)
    for i, load in enumerate(loads):
        load.wait()
        held[i * step : (i + 1) * step, :] = unit_values(rows_ref[i * step : (i + 1) * step, :])
    if not loads:
        held[...] = unit_values(rows_ref[...])
    wide = 2 * LANES
    for c in range(width // wide):
        runs = jnp.dot(
            pick[...], held[:, c * wide : (c + 1) * wide], preferred_element_type=jnp.float32
        ).astype(jnp.bfloat16)
        for d, out in enumerate(outs):
            for part in range(2):
                at = (2 * c + part) * 2 * cap
                out[at : at + 2 * cap, :] = runs[
                    d * 2 * cap : (d + 1) * 2 * cap, part * LANES : (part + 1) * LANES
                ]


def near_kernel(chips, cap, ids_any, cent_ref, rows_any, *rest):
    outs, (extra, rows_ref, ids_ref, held, pick, sems) = rest[:chips], rest[chips:]
    strata_dev, width = cent_ref.shape
    rows = rows_ref.shape[0]
    pieces = 4
    loads = [pltpu.make_async_copy(ids_any, ids_ref, sems.at[pieces])]
    for i in range(pieces):
        at = pl.ds(i * (rows // pieces), rows // pieces)
        loads.append(pltpu.make_async_copy(rows_any.at[at, :], rows_ref.at[at, :], sems.at[i]))
    for load in loads:
        load.start()
    cent = unit_values(cent_ref[...])
    depth = width // LANES * 2 * cap + TAIL
    for c in range(width // LANES):
        at = depth + c * strata_dev
        for out in (outs[0], outs[chips // 2]):
            out[at : at + strata_dev, :] = cent[:, c * LANES : (c + 1) * LANES]
    loads[0].wait()
    ids = ids_ref[...].astype(jnp.float32)
    for c in range(width // LANES):
        at = TAIL + c * strata_dev
        extra[at : at + strata_dev, :] = cent[:, c * LANES : (c + 1) * LANES]
    extra[:TAIL, :] = jnp.concatenate(
        [
            jnp.broadcast_to(ids[:, i * LANES : (i + 1) * LANES], (TAIL // 4, LANES))
            for i in range(rows // LANES)
        ],
        axis=0,
    ).astype(jnp.bfloat16)
    half = lax.axis_index("grp") % 2
    pack_into(ids, loads[1:], rows_ref, outs, held, pick, cap, strata_dev, half)


def far_kernel(chips, cap, strata_dev, extra, rows_ref, *rest):
    inner = is_inner(chips)
    direct, outs, (held, pick) = rest[: chips // 2], rest[chips // 2 : -2], rest[-2:]

    @pl.when(inner)
    def _():
        spread = extra[:TAIL, :].astype(jnp.float32)
        ids = jnp.concatenate([spread[i : i + 1, :] for i in range(0, TAIL, TAIL // 4)], axis=1)
        half = lax.axis_index("blk") // chips
        pack_into(ids, [], rows_ref, outs, held, pick, cap, strata_dev, half)

    @pl.when(jnp.logical_not(inner))
    def _():
        for block, out in zip(direct, outs[chips // 2 :]):
            out[...] = block[: out.shape[0], :]


def unpack(blocks, cap, strata_dev, units, id_col, others=None, use_others=None):
    each = len(blocks) * cap
    width = units.shape[1]
    depth = width // LANES * 2 * cap

    def lay(some):
        for i, block in enumerate(some):
            for r in range(2):
                at = r * each + i * cap
                for c in range(width // LANES):
                    units[at : at + cap, c * LANES : (c + 1) * LANES] = block[
                        (2 * c + r) * cap : (2 * c + r + 1) * cap, :
                    ]

    if others is None:
        lay(blocks)
    else:
        pl.when(use_others)(lambda: lay(others))
        pl.when(jnp.logical_not(use_others))(lambda: lay(blocks))
    id_rows = [[], []]
    for i, block in enumerate(blocks):
        tail = block[depth : depth + TAIL, :].astype(jnp.float32)
        if others is not None:
            other = others[i][depth : depth + TAIL, :].astype(jnp.float32)
            tail = jnp.where(
                jnp.broadcast_to(use_others.astype(jnp.int32), tail.shape) > 0, other, tail
            )
        for r in range(2):
            at = r * each + i * cap
            ids = tail[8 * r : 8 * r + 1, :]
            ids = jnp.where(ids < float(strata_dev), ids, -1.0)
            id_rows[r].append(ids[:, :cap])
            id_col[at : at + cap, :] = jnp.broadcast_to(ids, (LANES, LANES)).T[:cap, :]
    return [jnp.concatenate(rows, axis=1) for rows in id_rows]


def masked_exp(scores, id_col, id_key):
    same = jnp.concatenate([id_col] * (scores.shape[1] // LANES), axis=1) == id_key
    return jnp.where(same, jnp.exp((scores - 1.0) * 4.0), 0.0)


def fold(kernel):
    rows, lanes = kernel.shape
    return jnp.sum(kernel.reshape(rows // 8, 8, lanes), axis=0)


def key_of(id_row):
    return jnp.where(id_row >= 0.0, id_row, -2.0)


def own_centroid(near, id_row):
    which = lax.broadcasted_iota(jnp.int32, near.shape, 0).astype(jnp.float32)
    return jnp.sum(jnp.where(which == id_row, near, 0.0), axis=0, keepdims=True)


def transposed_sum(kernel):
    part = kernel[:, :LANES]
    for c in range(1, kernel.shape[1] // LANES):
        part = part + kernel[:, c * LANES : (c + 1) * LANES]
    return jnp.concatenate(
        [
            jnp.sum(part[i * LANES : (i + 1) * LANES, :].T, axis=0, keepdims=True)
            for i in range(part.shape[0] // LANES)
        ],
        axis=1,
    )


def join(groups, units, id_col, ids, cents=None):
    earlier, new, picked = [[] for _ in groups], [], []
    for r, row in enumerate(ids):
        key = key_of(row)
        each = row.shape[1]
        mine = units[r * each : (r + 1) * each, :]
        left = mine
        if cents is not None:
            strata_dev = cents.shape[0] // 2
            left = jnp.concatenate([mine, cents[r * strata_dev : (r + 1) * strata_dev, :]], axis=0)
        scores = across(left, mine)
        if cents is not None:
            picked.append(own_centroid(scores[each:, :], row))
        sums = fold(masked_exp(scores[:each, :], id_col[r * each : (r + 1) * each, :], key))
        for sums_of, (old_units, old_col, old_density) in zip(earlier, groups):
            size = old_density[r].shape[1]
            at = slice(r * size, (r + 1) * size)
            kernel = masked_exp(across(old_units[at, :], mine), old_col[at, :], key)
            sums = sums + fold(kernel)
            sums_of.append(old_density[r] + transposed_sum(kernel))
        new.append(jnp.sum(sums, axis=0, keepdims=True))
    return earlier, new, picked


def parts_of(value):
    high = value.astype(jnp.bfloat16).astype(jnp.float32)
    middle = (value - high).astype(jnp.bfloat16).astype(jnp.float32)
    return [high, middle, value - high - middle]


def early_kernel(chips, cap, strata_dev, after, *rest):
    blocks, (held, id_col) = rest[:chips], rest[chips:]
    in_a = lax.axis_index("grp") % 2 == lax.axis_index("blk") // chips

    @pl.when(in_a)
    def _():
        width = held.shape[1]
        each = chips * cap
        depth = width // LANES * 2 * cap + TAIL
        ids = unpack(blocks, cap, strata_dev, held, id_col)
        for c in range(width // LANES):
            at = depth + c * strata_dev
            held[2 * each : 2 * each + strata_dev, c * LANES : (c + 1) * LANES] = blocks[0][
                at : at + strata_dev, :
            ]
        _, density, _ = join([], held, id_col, ids)
        rows = [*parts_of(density[0]), *parts_of(density[1]), *ids]
        tail = jnp.concatenate(rows + rows, axis=0).astype(jnp.bfloat16)
        held[2 * each + strata_dev :, :each] = tail


def mid_kernel(chips, cap, group_a, extra, *rest):
    direct, spread, (units, id_col, facts, facts_a, col_a, cents) = (
        rest[: chips // 2],
        rest[chips // 2 : chips],
        rest[chips:],
    )
    inner = is_inner(chips)
    strata_dev, width = cents.shape[0] // 2, cents.shape[1]
    depth = width // LANES * 2 * cap + TAIL
    each = chips * cap

    def place(block, base):
        for c in range(width // LANES):
            at = base + c * strata_dev
            cents[strata_dev:, c * LANES : (c + 1) * LANES] = block[at : at + strata_dev, :]

    cents[:strata_dev, :] = group_a[2 * each : 2 * each + strata_dev, :]
    pl.when(inner)(lambda: place(extra, TAIL))
    pl.when(jnp.logical_not(inner))(lambda: place(direct[0], depth))
    tail = group_a[2 * each + strata_dev :, :each].astype(jnp.float32)
    density_a = []
    for r in range(2):
        density_a.append(
            tail[3 * r : 3 * r + 1, :] + tail[3 * r + 1 : 3 * r + 2, :] + tail[3 * r + 2 : 3 * r + 3, :]
        )
        row = tail[6 + r : 7 + r, :]
        col_a[r * each : (r + 1) * each, :] = upright(row)
        facts_a[2 + r : 3 + r, :] = row
        near = cents[r * strata_dev : (r + 1) * strata_dev, :]
        facts_a[4 + r : 5 + r, :] = own_centroid(
            across(near, group_a[r * each : (r + 1) * each, :]), row
        )
    ids = unpack(direct, cap, strata_dev, units, id_col, spread, inner)
    (old,), density, picked = join([(group_a, col_a, density_a)], units, id_col, ids, cents)
    for r, row in enumerate(ids):
        facts[r : r + 1, :] = density[r]
        facts[2 + r : 3 + r, :] = row
        facts[4 + r : 5 + r, :] = picked[r]
        facts_a[r : r + 1, :] = old[r]


def upright(row):
    return jnp.concatenate(
        [
            jnp.broadcast_to(row[:, i * LANES : (i + 1) * LANES], (LANES, LANES)).T
            for i in range(row.shape[1] // LANES)
        ],
        axis=0,
    )


def late_kernel(order, cap, groups, units_a, col_a, facts_a, units_m, col_m, facts_m, cents, *rest):
    blocks, (out_ref, units, id_col) = rest[:-3], rest[-3:]
    strata_dev = cents.shape[0] // 2
    chips = len(order) // 2
    me, group = lax.axis_index("blk"), lax.axis_index("grp")
    at_work = (me // chips) != (group % 2)
    ids = unpack(blocks, cap, strata_dev, units, id_col)
    old = [
        (some, col, [facts[r : r + 1, :] for r in range(2)])
        for some, col, facts in ((units_a, col_a, facts_a), (units_m, col_m, facts_m))
    ]
    earlier, density, picked_new = join(old, units, id_col, ids, cents)
    total = jnp.zeros((1, 1), jnp.float32)
    weights = []
    for r, row in enumerate(ids):
        states = [
            (facts_a[2 + r : 3 + r, :], facts_a[4 + r : 5 + r, :], earlier[0][r]),
            (facts_m[2 + r : 3 + r, :], facts_m[4 + r : 5 + r, :], earlier[1][r]),
            (row, picked_new[r], density[r]),
        ]
        row, picked, dense = [jnp.concatenate(parts, axis=1) for parts in zip(*states)]
        real = row >= 0.0
        weight = jnp.where(
            real, ((1.0 - picked) + base_term) / jnp.where(real, dense, 1.0), 0.0
        )
        total = total + jnp.sum(weight, axis=1, keepdims=True)
        weights.append(weight)
    out_ref[...] = jnp.broadcast_to(jnp.where(at_work, total, 0.0), out_ref.shape)
    for r in range(2):
        for i in range(2 * chips):
            source = me ^ order[i]
            at = 4 * (source * groups + (group ^ 1)) + r
            out_ref[pl.ds(at, 1), :cap] = weights[r][:, i * cap : (i + 1) * cap]


def finish_kernel(chips, cap, groups, strata_dev, ids_ref, got_ref, out_ref):
    rows = ids_ref.shape[1]
    group = lax.axis_index("grp")
    half = group % 2
    got = got_ref[...]
    row_of = lax.broadcasted_iota(jnp.int32, got.shape, 0) % 4
    total = jnp.sum(jnp.where(row_of == 2, got, 0.0), axis=0, keepdims=True)[:, :1]
    ids = ids_ref[...]
    weight = jnp.zeros((1, rows), jnp.float32)
    for i in range(chips):
        owner = (half * chips + i) * groups + (group ^ 1)
        for r in range(2):
            shard = (half * chips + i) ^ (r * (chips + chips // 2))
            begin = jnp.sum((ids < shard * strata_dev).astype(jnp.int32))
            start = jnp.minimum(begin, rows - cap)
            part = got_ref[pl.ds(4 * owner + r, 1), :]
            part = jnp.broadcast_to(jnp.concatenate([part] * (rows // LANES), axis=1), (8, rows))
            part = pltpu.roll(part, start, axis=1)[:1, :]
            mine = (ids >= shard * strata_dev) & (ids < (shard + 1) * strata_dev)
            weight = jnp.where(mine, part, weight)
    out_ref[...] = weight * (float(rows * 2 * chips * groups) / total)


def body(embeddings, strata, centroids):
    shards, groups = lax.axis_size("blk"), lax.axis_size("grp")
    chips = shards // 2
    rows, width = embeddings.shape[1:]
    strata_dev = centroids.shape[1]
    cap = 2 * rows // shards
    chunks = width // LANES
    depth = chunks * 2 * cap + TAIL
    each = chips * cap
    every = [(b, g) for b in range(shards) for g in range(groups)]
    kind_a = [(b, g) for b, g in every if b // chips == g % 2]
    kind_b = [(b, g) for b, g in every if b // chips != g % 2]
    inner = [(b, g) for b, g in kind_b if b % chips // (chips // 2) != b // chips]
    outer = [(b, g) for b, g in kind_b if (b, g) not in inner]
    side = chips // 2
    flip = chips + side

    def send(array, pairs):
        return lax.ppermute(
            array, AXES, [(b * groups + g, to_b * groups + to_g) for (b, g), (to_b, to_g) in pairs]
        )

    def shape(*dims, dtype=jnp.bfloat16):
        return pltpu.VMEM(dims, dtype)

    held = [pltpu.VMEM((rows, width), jnp.bfloat16), pltpu.VMEM((shards * cap, rows), jnp.bfloat16)]
    order = [0, *reversed(range(1, chips))]
    swap = [((b, g), (b ^ flip, g ^ 1)) for b, g in inner]
    far_rows = send(embeddings[0], swap)
    *near, extra = pl.pallas_call(
        functools.partial(near_kernel, chips, cap),
        out_shape=[
            shape(depth + (chunks * strata_dev if d in (0, side) else 0), LANES) for d in range(chips)
        ]
        + [shape(TAIL + chunks * strata_dev, LANES)],
        in_specs=[ANY, VMEM, ANY],
        out_specs=[VMEM] * (chips + 1),
        scratch_shapes=[
            pltpu.VMEM((rows, width), jnp.bfloat16),
            pltpu.VMEM((1, rows), jnp.int32),
            *held,
            pltpu.SemaphoreType.DMA((5,)),
        ],
        compiler_params=params(44),
        cost_estimate=pl.CostEstimate(flops=0, transcendentals=0, bytes_accessed=0),
        name="near",
    )(strata, centroids[0], embeddings[0])
    blocks_a = [
        near[d] if d == 0 else send(near[d], [((b, g), (b ^ d, g)) for b, g in kind_a])
        for d in order
    ]
    extra = send(extra, swap)
    out = pl.pallas_call(
        functools.partial(far_kernel, chips, cap, strata_dev),
        out_shape=[shape(depth, LANES)] * chips,
        in_specs=[VMEM] * (2 + side),
        out_specs=[VMEM] * chips,
        scratch_shapes=held,
        compiler_params=params(20),
        name="far",
    )(extra, far_rows, *near[:side])
    direct = []
    for e in range(side):
        block, _ = lax.optimization_barrier((near[side + e], out[0]))
        direct.append(send(block, [((b, g), (b ^ (flip + e), g ^ 1)) for b, g in outer]))
    spread = [
        out[e] if e == 0 else send(out[e], [((b, g), (b ^ e, g)) for b, g in inner])
        for e in range(side)
    ]
    last = [
        send(
            out[side + e],
            [((b, g), (b ^ (chips + e), g ^ 1)) for b, g in outer]
            + [((b, g), (b ^ (side + e), g)) for b, g in inner],
        )
        for e in range(side)
    ]
    group_a = pl.pallas_call(
        functools.partial(early_kernel, chips, cap, strata_dev),
        out_shape=shape(2 * each + strata_dev + TAIL, width),
        in_specs=[ANY] + [VMEM] * chips,
        out_specs=VMEM,
        scratch_shapes=[pltpu.VMEM((2 * each, LANES), jnp.float32)],
        compiler_params=params(20),
        name="early",
    )(out[0], *blocks_a)
    group_a = send(group_a, [((b, g), (b, g ^ 1)) for b, g in kind_a])
    units_m, col_m, facts_m, facts_a, col_a, cents = pl.pallas_call(
        functools.partial(mid_kernel, chips, cap),
        out_shape=[
            shape(2 * side * cap, width),
            shape(2 * side * cap, LANES, dtype=jnp.float32),
            shape(8, side * cap, dtype=jnp.float32),
            shape(8, each, dtype=jnp.float32),
            shape(2 * each, LANES, dtype=jnp.float32),
            shape(2 * strata_dev, width),
        ],
        in_specs=[VMEM] * (chips + 2),
        out_specs=[VMEM] * 6,
        compiler_params=params(20),
        name="mid",
    )(group_a, extra, *direct, *spread)
    sent = pl.pallas_call(
        functools.partial(
            late_kernel,
            [*order, *(flip + e for e in range(side)), *(chips + e for e in range(side))],
            cap,
            groups,
        ),
        out_shape=jax.ShapeDtypeStruct((shards * groups * 4, LANES), jnp.float32),
        in_specs=[VMEM] * (7 + side),
        out_specs=VMEM,
        scratch_shapes=[
            pltpu.VMEM((2 * side * cap, width), jnp.bfloat16),
            pltpu.VMEM((2 * side * cap, LANES), jnp.float32),
        ],
        compiler_params=params(20),
        name="late",
    )(group_a, col_a, facts_a, units_m, col_m, facts_m, cents, *last)
    got = lax.all_to_all(
        sent.reshape(shards * groups, 4, LANES), AXES, 0, 0, tiled=True
    ).reshape(shards * groups * 4, LANES)
    return pl.pallas_call(
        functools.partial(finish_kernel, chips, cap, groups, strata_dev),
        out_shape=jax.ShapeDtypeStruct((1, rows), jnp.float32),
        in_specs=[VMEM, VMEM],
        out_specs=VMEM,
        compiler_params=params(8),
        name="finish",
    )(strata, got)


def solution(mesh):
    placed = (P("grp", "blk", None), P("grp", "blk"), P("grp", "blk", None))
    return jax.shard_map(
        body, mesh=mesh, in_specs=placed, out_specs=P("grp", "blk"), check_vma=False
    )
```

time: 65.3 us -> 62.8 us (0.962)
  blocking collectives: 28.8 us -> 18 us
  waiting for transfers between devices: 5.9 us -> 16.5 us
  Pallas kernels: 9.74 us -> 8.49 us
  starting transfers between devices: 17.6 us -> 16.6 us
    all_to_all x1, blocking collectives: 28.8 us -> 18 us  [body(): lax.all_to_all(sent.reshape(shards * groups, 4, LANES), AXES, 0, 0, tiled...]
    ppermute x10 -> x11, waiting for transfers between devices: 5.9 us -> 16.5 us  [send(): lax.ppermute(array, AXES, [(b * groups + g, to_b * groups + to_g) for (b,...]
    pallas_call x1, Pallas kernels: 1.6 us -> 0.1 us  [body(): pl.pallas_call(functools.partial(far_kernel, chips, cap, strata_dev), out...]
    ppermute x10 -> x11, starting transfers between devices: 17.6 us -> 16.6 us  [send(): lax.ppermute(array, AXES, [(b * groups + g, to_b * groups + to_g) for (b,...]
  transfers between devices with their start and end apart: 10 -> 11, of which waited for: 2 -> 2; matrix products, arithmetic and copies ran while one was open for 0% -> 0% of each run, Pallas kernels for 11% -> 7%
where the time goes in v7:
time: 62.8 us; the launch traced here: 62.4 us
  blocking collectives  18 us (29%)
  starting transfers between devices  16.6 us (26%)
  waiting for transfers between devices  16.5 us (26%)
  Pallas kernels  8.49 us (14%)
  local copies, waits for them, and re-layouts  2.66 us (4%)
    all_to_all x1, blocking collectives, body(): lax.all_to_all(sent.reshape(shards * groups, 4, LANES), AXES, 0, 0, tiled...  18 us
    ppermute x11, starting transfers between devices, send(): lax.ppermute(array, AXES, [(b * groups + g, to_b * groups + to_g) for (b,...  16.6 us
    ppermute x11, waiting for transfers between devices, send(): lax.ppermute(array, AXES, [(b * groups + g, to_b * groups + to_g) for (b,...  16.5 us
    unnamed x6, local copies, waits for them, and re-layouts  2.66 us
    pallas_call x1, Pallas kernels, body(): pl.pallas_call(functools.partial(mid_kernel, chips, cap), out_shape=[shap...  2.16 us
    pallas_call x1, Pallas kernels, body(): pl.pallas_call(functools.partial(near_kernel, chips, cap), out_shape=[sha...  2.07 us
    pallas_call x1, Pallas kernels, body(): pl.pallas_call(functools.partial(late_kernel, [*order, *(flip + e for e i...  1.71 us
    pallas_call x1, Pallas kernels, body(): pl.pallas_call(functools.partial(early_kernel, chips, cap, strata_dev), o...  1.64 us
  transfers between devices with their start and end apart: 11, of which 2 were waited for; matrix products, arithmetic and copies ran while one was open for 0% of the time, Pallas kernels for 7%

profile of v7, /device:TPU:0, one launch (start us, length us, event | category | flops | bytes accessed | tf_op | source)
XLA Modules:
  0.0 62.4 jit_solution(17015384344180395703)
XLA Ops:
  0.0 0.7 %collective-permute-start.1 = (bf16[512,1024]{1,0:T(8,128)(2,1)}, bf16[512,1024]{1,0:T(8,128)(2,1)S(1)}, u32[]{:S(2)}, u32[]{:S(2)}) collective-permute-start(bf16[512,1024]{1,0:T(8,128)(2,1)} %bitcast.4), channel_id=1, source_target_pairs={{9,16},{11,18},{13,20},{15,22},{16,9},{18,11},{20,13},{22,15}} | collective-permute-start | bytes 3145736 | tf_op jit(solution)/shard_map/ppermute | solution.py:389
  0.7 1.2 %copy-done = bf16[1,512,1024]{2,1,0:T(8,128)(2,1)S(1)} copy-done((bf16[1,512,1024]{2,1,0:T(8,128)(2,1)S(1)}, bf16[1,512,1024]{2,1,0:T(8,128)(2,1)}, u32[]{:S(2)}) %copy-start) | copy-done | bytes 1048600
  2.0 0.8 %copy-done.1 = bf16[1,16,1024]{2,1,0:T(8,128)(2,1)S(1)} copy-done((bf16[1,16,1024]{2,1,0:T(8,128)(2,1)S(1)}, bf16[1,16,1024]{2,1,0:T(8,128)(2,1)}, u32[]{:S(2)}) %copy-start.1) | copy-done | bytes 32792
  2.7 0.7 %copy-done.2 = s32[1,512]{1,0:T(1,128)S(1)} copy-done((s32[1,512]{1,0:T(1,128)S(1)}, s32[1,512]{1,0:T(1,128)}, u32[]{:S(2)}) %copy-start.2) | copy-done | bytes 2072
  3.4 2.1 %near.1 = (bf16[2192,128]{1,0:T(8,128)(2,1)S(1)}, bf16[2064,128]{1,0:T(8,128)(2,1)S(1)}, bf16[2192,128]{1,0:T(8,128)(2,1)S(1)}, bf16[2064,128]{1,0:T(8,128)(2,1)S(1)}, bf16[144,128]{1,0:T(8,128)(2,1)S(1)}) custom-call(s32[1,512]{1,0:T(1,128)S(1)} %copy-done.2, bf16[16,1024]{1,0:T(8,128)(2,1)S(1)} %bitcast.8, bf16[512,1024]{1,0:T(8,128)(2,1)S(1)} %bitcast.5), custom_call_target="tpu_custom_call" | custom-call | tf_op jit(solution)/shard_map/near/pallas_call | solution.py:400
  5.5 4.9 %collective-permute-start.3 = (bf16[2192,128]{1,0:T(8,128)(2,1)S(1)}, bf16[2192,128]{1,0:T(8,128)(2,1)S(1)}, u32[]{:S(2)}, u32[]{:S(2)}) collective-permute-start(bf16[2192,128]{1,0:T(8,128)(2,1)S(1)} %get-tuple-element.28), channel_id=1, source_target_pairs={{0,8},{2,10},{4,12},{6,14},{8,0},{10,2},{12,4},{14,6},{17,25},{19,... | collective-permute-start | bytes 1683464 | tf_op jit(solution)/shard_map/ppermute | solution.py:389
  10.4 3.4 %collective-permute-start.4 = (bf16[2064,128]{1,0:T(8,128)(2,1)S(1)}, bf16[2064,128]{1,0:T(8,128)(2,1)S(1)}, u32[]{:S(2)}, u32[]{:S(2)}) collective-permute-start(bf16[2064,128]{1,0:T(8,128)(2,1)S(1)} %get-tuple-element.24.rest_1_), channel_id=1, source_target_pairs={{0,4},{2,6},{4,0},{6,2},{8,12},{10,14},{12,8},{14,10},{17,21},{19,... | collective-permute-start | bytes 1585160 | tf_op jit(solution)/shard_map/ppermute | solution.py:389
  13.8 1.9 %collective-permute-start.2 = (bf16[2064,128]{1,0:T(8,128)(2,1)S(1)}, bf16[2064,128]{1,0:T(8,128)(2,1)S(1)}, u32[]{:S(2)}, u32[]{:S(2)}) collective-permute-start(bf16[2064,128]{1,0:T(8,128)(2,1)S(1)} %get-tuple-element.29), channel_id=1, source_target_pairs={{0,12},{2,14},{4,8},{6,10},{8,4},{10,6},{12,0},{14,2},{17,29},{19,... | collective-permute-start | bytes 1585160 | tf_op jit(solution)/shard_map/ppermute | solution.py:389
  15.8 0.7 %collective-permute-start = (bf16[144,128]{1,0:T(8,128)(2,1)S(1)}, bf16[144,128]{1,0:T(8,128)(2,1)S(1)}, u32[]{:S(2)}, u32[]{:S(2)}) collective-permute-start(bf16[144,128]{1,0:T(8,128)(2,1)S(1)} %get-tuple-element.22), channel_id=1, source_target_pairs={{9,16},{11,18},{13,20},{15,22},{16,9},{18,11},{20,13},{22,15}} | collective-permute-start | bytes 110600 | tf_op jit(solution)/shard_map/ppermute | solution.py:389
  16.4 0.0 collective-permute-done.extra
  16.5 0.0 collective-permute-done.1.rows_ref
  16.5 0.1 far.1
  16.6 16.3 %collective-permute-done.4.rest_3_ = bf16[2064,128]{1,0:T(8,128)(2,1)S(1)} collective-permute-done((bf16[2064,128]{1,0:T(8,128)(2,1)S(1)}, bf16[2064,128]{1,0:T(8,128)(2,1)S(1)}, u32[]{:S(2)}, u32[]{:S(2)}) %collective-permute-start.4) | collective-permute-done | bytes 528416 | tf_op jit(solution)/shard_map/ppermute | solution.py:389
  32.9 0.0 collective-permute-done.2.rest_1_
  32.9 0.0 collective-permute-done.3.rest_2_
  32.9 1.6 %early.1 = bf16[1056,1024]{1,0:T(8,128)(2,1)S(1)} custom-call(bf16[2064,128]{1,0:T(8,128)(2,1)S(1)} %get-tuple-element.25.after.rest_2_, bf16[2192,128]{1,0:T(8,128)(2,1)S(1)} %get-tuple-element.23.rest_0_, bf16[2064,128]{1,0:T(8,128)(2,1)S(1)} %collective-permute-done.2.rest_1_, bf16[2192,128]{1,0:T(8,128)(2,1)S(1)} %collective-permute-done.3.rest_2_, ...), custom_call_target="tpu_custom_call" | custom-call | tf_op jit(solution)/shard_map/early/pallas_call | solution.py:448
  34.5 1.4 %collective-permute-start.5 = (bf16[1056,1024]{1,0:T(8,128)(2,1)S(1)}, bf16[1056,1024]{1,0:T(8,128)(2,1)S(1)}, u32[]{:S(2)}, u32[]{:S(2)}) collective-permute-start(bf16[1056,1024]{1,0:T(8,128)(2,1)S(1)} %early.1), channel_id=1, source_target_pairs={{0,1},{2,3},{4,5},{6,7},{8,9},{10,11},{12,13},{14,15},{17,16},{19,... | collective-permute-start | bytes 6488072 | tf_op jit(solution)/shard_map/ppermute | solution.py:389
  35.9 0.7 %collective-permute-start.7 = (bf16[2064,128]{1,0:T(8,128)(2,1)S(1)}, bf16[2064,128]{1,0:T(8,128)(2,1)S(1)}, u32[]{:S(2)}, u32[]{:S(2)}) collective-permute-start(bf16[2064,128]{1,0:T(8,128)(2,1)S(1)} %get-tuple-element.29), channel_id=1, source_target_pairs={{1,28},{3,30},{5,24},{7,26},{24,5},{26,7},{28,1},{30,3}} | collective-permute-start | bytes 1585160 | tf_op jit(solution)/shard_map/ppermute | solution.py:389
  36.6 0.7 %collective-permute-start.6 = (bf16[2192,128]{1,0:T(8,128)(2,1)S(1)}, bf16[2192,128]{1,0:T(8,128)(2,1)S(1)}, u32[]{:S(2)}, u32[]{:S(2)}) collective-permute-start(bf16[2192,128]{1,0:T(8,128)(2,1)S(1)} %get-tuple-element.28), channel_id=1, source_target_pairs={{1,24},{3,26},{5,28},{7,30},{24,1},{26,3},{28,5},{30,7}} | collective-permute-start | bytes 1683464 | tf_op jit(solution)/shard_map/ppermute | solution.py:389
  37.4 0.7 %collective-permute-start.8 = (bf16[2064,128]{1,0:T(8,128)(2,1)S(1)}, bf16[2064,128]{1,0:T(8,128)(2,1)S(1)}, u32[]{:S(2)}, u32[]{:S(2)}) collective-permute-start(bf16[2064,128]{1,0:T(8,128)(2,1)S(1)} %get-tuple-element.30), channel_id=1, source_target_pairs={{9,13},{11,15},{13,9},{15,11},{16,20},{18,22},{20,16},{22,18}} | collective-permute-start | bytes 1585160 | tf_op jit(solution)/shard_map/ppermute | solution.py:389
  38.1 0.7 %collective-permute-start.9 = (bf16[2064,128]{1,0:T(8,128)(2,1)S(1)}, bf16[2064,128]{1,0:T(8,128)(2,1)S(1)}, u32[]{:S(2)}, u32[]{:S(2)}) collective-permute-start(bf16[2064,128]{1,0:T(8,128)(2,1)S(1)} %get-tuple-element.37), channel_id=1, source_target_pairs={{1,16},{3,18},{5,20},{7,22},{24,9},{26,11},{28,13},{30,15},{9,1},{... | collective-permute-start | bytes 1585160 | tf_op jit(solution)/shard_map/ppermute | solution.py:389
  38.8 0.0 collective-permute-done.7.rest_1_
  38.8 0.7 %collective-permute-start.10 = (bf16[2064,128]{1,0:T(8,128)(2,1)S(1)}, bf16[2064,128]{1,0:T(8,128)(2,1)S(1)}, u32[]{:S(2)}, u32[]{:S(2)}) collective-permute-start(bf16[2064,128]{1,0:T(8,128)(2,1)S(1)} %get-tuple-element.38), channel_id=1, source_target_pairs={{1,20},{3,22},{5,16},{7,18},{24,13},{26,15},{28,9},{30,11},{9,5},{... | collective-permute-start | bytes 1585160 | tf_op jit(solution)/shard_map/ppermute | solution.py:389
  39.5 0.0 collective-permute-done.8.rest_3_
  39.5 0.0 collective-permute-done.6.rest_0_
  39.5 0.2 collective-permute-done.5.group_a.units_a
  39.7 2.2 %mid.1 = (bf16[512,1024]{1,0:T(8,128)(2,1)S(1)}, f32[512,128]{1,0:T(8,128)S(1)}, f32[8,256]{1,0:T(8,128)S(1)}, f32[8,512]{1,0:T(8,128)S(1)}, f32[1024,128]{1,0:T(8,128)S(1)}, /*index=5*/bf16[32,1024]{1,0:T(8,128)(2,1)S(1)}) custom-call(bf16[1056,1024]{1,0:T(8,128)(2,1)S(1)} %collective-permute-done.5.group_a.units_a, ...), custom_call_target="tpu_custom_call" | custom-call | tf_op jit(solution)/shard_map/mid/pallas_call | solution.py:458
  41.8 0.0 collective-permute-done.9.rest_0_
  41.8 0.0 collective-permute-done.10.rest_1_
  41.9 1.7 %late.1 = f32[128,128]{1,0:T(8,128)S(1)} custom-call(bf16[1056,1024]{1,0:T(8,128)(2,1)S(1)} %collective-permute-done.5.group_a.units_a, f32[1024,128]{1,0:T(8,128)S(1)} %get-tuple-element.31.col_a, f32[8,512]{1,0:T(8,128)S(1)} %get-tuple-element.32.facts_a, bf16[512,1024]{1,0:T(8,128)(2,1)S(1)} %get-tuple-element.33.units_m, ...), custom_call_target="tpu_custom_call" | custom-call | tf_op jit(solution)/shard_map/late/pallas_call | solution.py:473
  43.6 18.0 %all_to_all.5 = f32[32,4,128]{2,1,0:T(4,128)S(1)} all-to-all(f32[32,4,128]{2,1,0:T(4,128)S(1)} %bitcast.6), channel_id=1, replica_groups=mesh['blk'=8,'grp'=4] {'blk','grp'}, dimensions={0} | all-to-all | bytes 131072 | tf_op jit(solution)/shard_map/all_to_all | solution.py:490
  61.6 0.8 %finish.1 = f32[1,512]{1,0:T(1,128)} custom-call(s32[1,512]{1,0:T(1,128)S(1)} %copy-done.2, f32[128,128]{1,0:T(8,128)S(1)} %bitcast.7), custom_call_target="tpu_custom_call" | custom-call | tf_op jit(solution)/shard_map/finish/pallas_call | solution.py:493
  (3 shorter events, 0.0 us)
Async XLA Ops:
  0.0 16.5 %collective-permute-start.1 = (bf16[512,1024]{1,0:T(8,128)(2,1)}, bf16[512,1024]{1,0:T(8,128)(2,1)S(1)}, u32[]{:S(2)}, u32[]{:S(2)}) collective-permute-start(bf16[512,1024]{1,0:T(8,128)(2,1)} %bitcast.4), channel_id=1, source_target_pairs={{9,16},{11,18},{13,20},{15,22},{16,9},{18,11},{20,13},{22,15}} | collective-permute-start | bytes 3145736 | tf_op jit(solution)/shard_map/ppermute | solution.py:389
  0.7 1.2 %copy-start = (bf16[1,512,1024]{2,1,0:T(8,128)(2,1)S(1)}, bf16[1,512,1024]{2,1,0:T(8,128)(2,1)}, u32[]{:S(2)}) copy-start(bf16[1,512,1024]{2,1,0:T(8,128)(2,1)} %param.3) | copy-start | bytes 3145732
  2.0 0.8 %copy-start.1 = (bf16[1,16,1024]{2,1,0:T(8,128)(2,1)S(1)}, bf16[1,16,1024]{2,1,0:T(8,128)(2,1)}, u32[]{:S(2)}) copy-start(bf16[1,16,1024]{2,1,0:T(8,128)(2,1)} %param.5) | copy-start | bytes 98308
  2.7 0.7 %copy-start.2 = (s32[1,512]{1,0:T(1,128)S(1)}, s32[1,512]{1,0:T(1,128)}, u32[]{:S(2)}) copy-start(s32[1,512]{1,0:T(1,128)} %ids_ref.1) | copy-start | bytes 6148
  5.5 27.4 %collective-permute-start.3 = (bf16[2192,128]{1,0:T(8,128)(2,1)S(1)}, bf16[2192,128]{1,0:T(8,128)(2,1)S(1)}, u32[]{:S(2)}, u32[]{:S(2)}) collective-permute-start(bf16[2192,128]{1,0:T(8,128)(2,1)S(1)} %get-tuple-element.28), channel_id=1, source_target_pairs={{0,8},{2,10},{4,12},{6,14},{8,0},{10,2},{12,4},{14,6},{17,25},{19,... | collective-permute-start | bytes 1683464 | tf_op jit(solution)/shard_map/ppermute | solution.py:389
  10.4 22.4 %collective-permute-start.4 = (bf16[2064,128]{1,0:T(8,128)(2,1)S(1)}, bf16[2064,128]{1,0:T(8,128)(2,1)S(1)}, u32[]{:S(2)}, u32[]{:S(2)}) collective-permute-start(bf16[2064,128]{1,0:T(8,128)(2,1)S(1)} %get-tuple-element.24.rest_1_), channel_id=1, source_target_pairs={{0,4},{2,6},{4,0},{6,2},{8,12},{10,14},{12,8},{14,10},{17,21},{19,... | collective-permute-start | bytes 1585160 | tf_op jit(solution)/shard_map/ppermute | solution.py:389
  13.8 19.0 %collective-permute-start.2 = (bf16[2064,128]{1,0:T(8,128)(2,1)S(1)}, bf16[2064,128]{1,0:T(8,128)(2,1)S(1)}, u32[]{:S(2)}, u32[]{:S(2)}) collective-permute-start(bf16[2064,128]{1,0:T(8,128)(2,1)S(1)} %get-tuple-element.29), channel_id=1, source_target_pairs={{0,12},{2,14},{4,8},{6,10},{8,4},{10,6},{12,0},{14,2},{17,29},{19,... | collective-permute-start | bytes 1585160 | tf_op jit(solution)/shard_map/ppermute | solution.py:389
  15.8 0.7 %collective-permute-start = (bf16[144,128]{1,0:T(8,128)(2,1)S(1)}, bf16[144,128]{1,0:T(8,128)(2,1)S(1)}, u32[]{:S(2)}, u32[]{:S(2)}) collective-permute-start(bf16[144,128]{1,0:T(8,128)(2,1)S(1)} %get-tuple-element.22), channel_id=1, source_target_pairs={{9,16},{11,18},{13,20},{15,22},{16,9},{18,11},{20,13},{22,15}} | collective-permute-start | bytes 110600 | tf_op jit(solution)/shard_map/ppermute | solution.py:389
  34.5 5.2 %collective-permute-start.5 = (bf16[1056,1024]{1,0:T(8,128)(2,1)S(1)}, bf16[1056,1024]{1,0:T(8,128)(2,1)S(1)}, u32[]{:S(2)}, u32[]{:S(2)}) collective-permute-start(bf16[1056,1024]{1,0:T(8,128)(2,1)S(1)} %early.1), channel_id=1, source_target_pairs={{0,1},{2,3},{4,5},{6,7},{8,9},{10,11},{12,13},{14,15},{17,16},{19,... | collective-permute-start | bytes 6488072 | tf_op jit(solution)/shard_map/ppermute | solution.py:389
  35.9 2.8 %collective-permute-start.7 = (bf16[2064,128]{1,0:T(8,128)(2,1)S(1)}, bf16[2064,128]{1,0:T(8,128)(2,1)S(1)}, u32[]{:S(2)}, u32[]{:S(2)}) collective-permute-start(bf16[2064,128]{1,0:T(8,128)(2,1)S(1)} %get-tuple-element.29), channel_id=1, source_target_pairs={{1,28},{3,30},{5,24},{7,26},{24,5},{26,7},{28,1},{30,3}} | collective-permute-start | bytes 1585160 | tf_op jit(solution)/shard_map/ppermute | solution.py:389
  36.6 2.8 %collective-permute-start.6 = (bf16[2192,128]{1,0:T(8,128)(2,1)S(1)}, bf16[2192,128]{1,0:T(8,128)(2,1)S(1)}, u32[]{:S(2)}, u32[]{:S(2)}) collective-permute-start(bf16[2192,128]{1,0:T(8,128)(2,1)S(1)} %get-tuple-element.28), channel_id=1, source_target_pairs={{1,24},{3,26},{5,28},{7,30},{24,1},{26,3},{28,5},{30,7}} | collective-permute-start | bytes 1683464 | tf_op jit(solution)/shard_map/ppermute | solution.py:389
  37.4 2.1 %collective-permute-start.8 = (bf16[2064,128]{1,0:T(8,128)(2,1)S(1)}, bf16[2064,128]{1,0:T(8,128)(2,1)S(1)}, u32[]{:S(2)}, u32[]{:S(2)}) collective-permute-start(bf16[2064,128]{1,0:T(8,128)(2,1)S(1)} %get-tuple-element.30), channel_id=1, source_target_pairs={{9,13},{11,15},{13,9},{15,11},{16,20},{18,22},{20,16},{22,18}} | collective-permute-start | bytes 1585160 | tf_op jit(solution)/shard_map/ppermute | solution.py:389
  38.1 3.8 %collective-permute-start.9 = (bf16[2064,128]{1,0:T(8,128)(2,1)S(1)}, bf16[2064,128]{1,0:T(8,128)(2,1)S(1)}, u32[]{:S(2)}, u32[]{:S(2)}) collective-permute-start(bf16[2064,128]{1,0:T(8,128)(2,1)S(1)} %get-tuple-element.37), channel_id=1, source_target_pairs={{1,16},{3,18},{5,20},{7,22},{24,9},{26,11},{28,13},{30,15},{9,1},{... | collective-permute-start | bytes 1585160 | tf_op jit(solution)/shard_map/ppermute | solution.py:389
  38.8 3.1 %collective-permute-start.10 = (bf16[2064,128]{1,0:T(8,128)(2,1)S(1)}, bf16[2064,128]{1,0:T(8,128)(2,1)S(1)}, u32[]{:S(2)}, u32[]{:S(2)}) collective-permute-start(bf16[2064,128]{1,0:T(8,128)(2,1)S(1)} %get-tuple-element.38), channel_id=1, source_target_pairs={{1,20},{3,22},{5,16},{7,18},{24,13},{26,15},{28,9},{30,11},{9,5},{... | collective-permute-start | bytes 1585160 | tf_op jit(solution)/shard_map/ppermute | solution.py:389

commit v8 on v7

--- a/solution.py
+++ b/solution.py
@@ -411,7 +411,7 @@
             *held,
             pltpu.SemaphoreType.DMA((5,)),
         ],
-        compiler_params=params(44),
+        compiler_params=params(56),
         cost_estimate=pl.CostEstimate(flops=0, transcendentals=0, bytes_accessed=0),
         name="near",
     )(strata, centroids[0], embeddings[0])

time: 62.8 us -> 61.5 us (0.979)
  local copies, waits for them, and re-layouts: 2.66 us -> 0.01 us
  Pallas kernels: 8.49 us -> 9.89 us
    unnamed x6 -> x2, local copies, waits for them, and re-layouts: 2.66 us -> 0.01 us
    pallas_call x1, Pallas kernels: 2.07 us -> 3.46 us  [body(): pl.pallas_call(functools.partial(near_kernel, chips, cap), out_shape=[sha...]
  transfers between devices with their start and end apart: 11 -> 11, of which waited for: 2 -> 2; matrix products, arithmetic and copies ran while one was open for 0% -> 0% of each run, Pallas kernels for 7% -> 9%
where the time goes in v8:
time: 61.5 us; the launch traced here: 61.1 us
  blocking collectives  18 us (29%)
  starting transfers between devices  16.6 us (27%)
  waiting for transfers between devices  16.5 us (27%)
  Pallas kernels  9.89 us (16%)
    all_to_all x1, blocking collectives, body(): lax.all_to_all(sent.reshape(shards * groups, 4, LANES), AXES, 0, 0, tiled...  18 us
    ppermute x11, starting transfers between devices, send(): lax.ppermute(array, AXES, [(b * groups + g, to_b * groups + to_g) for (b,...  16.6 us
    ppermute x11, waiting for transfers between devices, send(): lax.ppermute(array, AXES, [(b * groups + g, to_b * groups + to_g) for (b,...  16.5 us
    pallas_call x1, Pallas kernels, body(): pl.pallas_call(functools.partial(near_kernel, chips, cap), out_shape=[sha...  3.46 us
    pallas_call x1, Pallas kernels, body(): pl.pallas_call(functools.partial(mid_kernel, chips, cap), out_shape=[shap...  2.16 us
    pallas_call x1, Pallas kernels, body(): pl.pallas_call(functools.partial(late_kernel, [*order, *(flip + e for e i...  1.72 us
    pallas_call x1, Pallas kernels, body(): pl.pallas_call(functools.partial(early_kernel, chips, cap, strata_dev), o...  1.65 us
  transfers between devices with their start and end apart: 11, of which 2 were waited for; matrix products, arithmetic and copies ran while one was open for 0% of the time, Pallas kernels for 9%

profile of v8, /device:TPU:0, one launch (start us, length us, event | category | flops | bytes accessed | tf_op | source)
XLA Modules:
  0.0 61.1 jit_solution(2919138086883716944)
XLA Ops:
  0.0 0.7 %collective-permute-start.1 = (bf16[512,1024]{1,0:T(8,128)(2,1)}, bf16[512,1024]{1,0:T(8,128)(2,1)S(1)}, u32[]{:S(2)}, u32[]{:S(2)}) collective-permute-start(bf16[512,1024]{1,0:T(8,128)(2,1)} %bitcast.6), channel_id=1, source_target_pairs={{9,16},{11,18},{13,20},{15,22},{16,9},{18,11},{20,13},{22,15}} | collective-permute-start | bytes 3145736 | tf_op jit(solution)/shard_map/ppermute | solution.py:389
  0.7 3.5 %near.1 = (bf16[2192,128]{1,0:T(8,128)(2,1)S(1)}, bf16[2064,128]{1,0:T(8,128)(2,1)S(1)}, bf16[2192,128]{1,0:T(8,128)(2,1)S(1)}, bf16[2064,128]{1,0:T(8,128)(2,1)S(1)}, bf16[144,128]{1,0:T(8,128)(2,1)S(1)}) custom-call(s32[1,512]{1,0:T(1,128)} %ids_ref.1, bf16[16,1024]{1,0:T(8,128)(2,1)} %bitcast.8, bf16[512,1024]{1,0:T(8,128)(2,1)} %bitcast.7), custom_call_target="tpu_custom_call" | custom-call | tf_op jit(solution)/shard_map/near/pallas_call | solution.py:400
  4.2 4.9 %collective-permute-start.3 = (bf16[2192,128]{1,0:T(8,128)(2,1)S(1)}, bf16[2192,128]{1,0:T(8,128)(2,1)S(1)}, u32[]{:S(2)}, u32[]{:S(2)}) collective-permute-start(bf16[2192,128]{1,0:T(8,128)(2,1)S(1)} %get-tuple-element.28), channel_id=1, source_target_pairs={{0,8},{2,10},{4,12},{6,14},{8,0},{10,2},{12,4},{14,6},{17,25},{19,... | collective-permute-start | bytes 1683464 | tf_op jit(solution)/shard_map/ppermute | solution.py:389
  9.1 3.4 %collective-permute-start.4 = (bf16[2064,128]{1,0:T(8,128)(2,1)S(1)}, bf16[2064,128]{1,0:T(8,128)(2,1)S(1)}, u32[]{:S(2)}, u32[]{:S(2)}) collective-permute-start(bf16[2064,128]{1,0:T(8,128)(2,1)S(1)} %get-tuple-element.24.rest_1_), channel_id=1, source_target_pairs={{0,4},{2,6},{4,0},{6,2},{8,12},{10,14},{12,8},{14,10},{17,21},{19,... | collective-permute-start | bytes 1585160 | tf_op jit(solution)/shard_map/ppermute | solution.py:389
  12.6 1.9 %collective-permute-start.2 = (bf16[2064,128]{1,0:T(8,128)(2,1)S(1)}, bf16[2064,128]{1,0:T(8,128)(2,1)S(1)}, u32[]{:S(2)}, u32[]{:S(2)}) collective-permute-start(bf16[2064,128]{1,0:T(8,128)(2,1)S(1)} %get-tuple-element.29), channel_id=1, source_target_pairs={{0,12},{2,14},{4,8},{6,10},{8,4},{10,6},{12,0},{14,2},{17,29},{19,... | collective-permute-start | bytes 1585160 | tf_op jit(solution)/shard_map/ppermute | solution.py:389
  14.5 0.7 %collective-permute-start = (bf16[144,128]{1,0:T(8,128)(2,1)S(1)}, bf16[144,128]{1,0:T(8,128)(2,1)S(1)}, u32[]{:S(2)}, u32[]{:S(2)}) collective-permute-start(bf16[144,128]{1,0:T(8,128)(2,1)S(1)} %get-tuple-element.22), channel_id=1, source_target_pairs={{9,16},{11,18},{13,20},{15,22},{16,9},{18,11},{20,13},{22,15}} | collective-permute-start | bytes 110600 | tf_op jit(solution)/shard_map/ppermute | solution.py:389
  15.2 0.0 collective-permute-done.extra
  15.2 0.0 collective-permute-done.1.rows_ref
  15.2 0.1 far.1
  15.3 16.3 %collective-permute-done.4.rest_3_ = bf16[2064,128]{1,0:T(8,128)(2,1)S(1)} collective-permute-done((bf16[2064,128]{1,0:T(8,128)(2,1)S(1)}, bf16[2064,128]{1,0:T(8,128)(2,1)S(1)}, u32[]{:S(2)}, u32[]{:S(2)}) %collective-permute-start.4) | collective-permute-done | bytes 528416 | tf_op jit(solution)/shard_map/ppermute | solution.py:389
  31.6 0.0 collective-permute-done.2.rest_1_
  31.6 0.0 collective-permute-done.3.rest_2_
  31.6 1.6 %early.1 = bf16[1056,1024]{1,0:T(8,128)(2,1)S(1)} custom-call(bf16[2064,128]{1,0:T(8,128)(2,1)S(1)} %get-tuple-element.25.after.rest_2_, bf16[2192,128]{1,0:T(8,128)(2,1)S(1)} %get-tuple-element.23.rest_0_, bf16[2064,128]{1,0:T(8,128)(2,1)S(1)} %collective-permute-done.2.rest_1_, bf16[2192,128]{1,0:T(8,128)(2,1)S(1)} %collective-permute-done.3.rest_2_, ...), custom_call_target="tpu_custom_call" | custom-call | tf_op jit(solution)/shard_map/early/pallas_call | solution.py:448
  33.2 1.4 %collective-permute-start.5 = (bf16[1056,1024]{1,0:T(8,128)(2,1)S(1)}, bf16[1056,1024]{1,0:T(8,128)(2,1)S(1)}, u32[]{:S(2)}, u32[]{:S(2)}) collective-permute-start(bf16[1056,1024]{1,0:T(8,128)(2,1)S(1)} %early.1), channel_id=1, source_target_pairs={{0,1},{2,3},{4,5},{6,7},{8,9},{10,11},{12,13},{14,15},{17,16},{19,... | collective-permute-start | bytes 6488072 | tf_op jit(solution)/shard_map/ppermute | solution.py:389
  34.7 0.7 %collective-permute-start.7 = (bf16[2064,128]{1,0:T(8,128)(2,1)S(1)}, bf16[2064,128]{1,0:T(8,128)(2,1)S(1)}, u32[]{:S(2)}, u32[]{:S(2)}) collective-permute-start(bf16[2064,128]{1,0:T(8,128)(2,1)S(1)} %get-tuple-element.29), channel_id=1, source_target_pairs={{1,28},{3,30},{5,24},{7,26},{24,5},{26,7},{28,1},{30,3}} | collective-permute-start | bytes 1585160 | tf_op jit(solution)/shard_map/ppermute | solution.py:389
  35.4 0.7 %collective-permute-start.6 = (bf16[2192,128]{1,0:T(8,128)(2,1)S(1)}, bf16[2192,128]{1,0:T(8,128)(2,1)S(1)}, u32[]{:S(2)}, u32[]{:S(2)}) collective-permute-start(bf16[2192,128]{1,0:T(8,128)(2,1)S(1)} %get-tuple-element.28), channel_id=1, source_target_pairs={{1,24},{3,26},{5,28},{7,30},{24,1},{26,3},{28,5},{30,7}} | collective-permute-start | bytes 1683464 | tf_op jit(solution)/shard_map/ppermute | solution.py:389
  36.1 0.7 %collective-permute-start.8 = (bf16[2064,128]{1,0:T(8,128)(2,1)S(1)}, bf16[2064,128]{1,0:T(8,128)(2,1)S(1)}, u32[]{:S(2)}, u32[]{:S(2)}) collective-permute-start(bf16[2064,128]{1,0:T(8,128)(2,1)S(1)} %get-tuple-element.30), channel_id=1, source_target_pairs={{9,13},{11,15},{13,9},{15,11},{16,20},{18,22},{20,16},{22,18}} | collective-permute-start | bytes 1585160 | tf_op jit(solution)/shard_map/ppermute | solution.py:389
  36.8 0.7 %collective-permute-start.9 = (bf16[2064,128]{1,0:T(8,128)(2,1)S(1)}, bf16[2064,128]{1,0:T(8,128)(2,1)S(1)}, u32[]{:S(2)}, u32[]{:S(2)}) collective-permute-start(bf16[2064,128]{1,0:T(8,128)(2,1)S(1)} %get-tuple-element.37), channel_id=1, source_target_pairs={{1,16},{3,18},{5,20},{7,22},{24,9},{26,11},{28,13},{30,15},{9,1},{... | collective-permute-start | bytes 1585160 | tf_op jit(solution)/shard_map/ppermute | solution.py:389
  37.5 0.0 collective-permute-done.7.rest_1_
  37.5 0.7 %collective-permute-start.10 = (bf16[2064,128]{1,0:T(8,128)(2,1)S(1)}, bf16[2064,128]{1,0:T(8,128)(2,1)S(1)}, u32[]{:S(2)}, u32[]{:S(2)}) collective-permute-start(bf16[2064,128]{1,0:T(8,128)(2,1)S(1)} %get-tuple-element.38), channel_id=1, source_target_pairs={{1,20},{3,22},{5,16},{7,18},{24,13},{26,15},{28,9},{30,11},{9,5},{... | collective-permute-start | bytes 1585160 | tf_op jit(solution)/shard_map/ppermute | solution.py:389
  38.2 0.0 collective-permute-done.8.rest_3_
  38.2 0.0 collective-permute-done.6.rest_0_
  38.2 0.2 collective-permute-done.5.group_a.units_a
  38.4 2.2 %mid.1 = (bf16[512,1024]{1,0:T(8,128)(2,1)S(1)}, f32[512,128]{1,0:T(8,128)S(1)}, f32[8,256]{1,0:T(8,128)S(1)}, f32[8,512]{1,0:T(8,128)S(1)}, f32[1024,128]{1,0:T(8,128)S(1)}, /*index=5*/bf16[32,1024]{1,0:T(8,128)(2,1)S(1)}) custom-call(bf16[1056,1024]{1,0:T(8,128)(2,1)S(1)} %collective-permute-done.5.group_a.units_a, ...), custom_call_target="tpu_custom_call" | custom-call | tf_op jit(solution)/shard_map/mid/pallas_call | solution.py:458
  40.6 0.0 collective-permute-done.9.rest_0_
  40.6 0.0 collective-permute-done.10.rest_1_
  40.6 0.0 copy-start
  40.6 1.7 %late.1 = f32[128,128]{1,0:T(8,128)S(1)} custom-call(bf16[1056,1024]{1,0:T(8,128)(2,1)S(1)} %collective-permute-done.5.group_a.units_a, f32[1024,128]{1,0:T(8,128)S(1)} %get-tuple-element.31.col_a, f32[8,512]{1,0:T(8,128)S(1)} %get-tuple-element.32.facts_a, bf16[512,1024]{1,0:T(8,128)(2,1)S(1)} %get-tuple-element.33.units_m, ...), custom_call_target="tpu_custom_call" | custom-call | tf_op jit(solution)/shard_map/late/pallas_call | solution.py:473
  42.3 18.0 %all_to_all.5 = f32[32,4,128]{2,1,0:T(4,128)S(1)} all-to-all(f32[32,4,128]{2,1,0:T(4,128)S(1)} %bitcast.4), channel_id=1, replica_groups=mesh['blk'=8,'grp'=4] {'blk','grp'}, dimensions={0} | all-to-all | bytes 131072 | tf_op jit(solution)/shard_map/all_to_all | solution.py:490
  60.3 0.0 copy-done
  60.3 0.8 %finish.1 = f32[1,512]{1,0:T(1,128)} custom-call(s32[1,512]{1,0:T(1,128)S(1)} %copy-done, f32[128,128]{1,0:T(8,128)S(1)} %bitcast.5), custom_call_target="tpu_custom_call" | custom-call | tf_op jit(solution)/shard_map/finish/pallas_call | solution.py:493
Async XLA Ops:
  0.0 15.2 %collective-permute-start.1 = (bf16[512,1024]{1,0:T(8,128)(2,1)}, bf16[512,1024]{1,0:T(8,128)(2,1)S(1)}, u32[]{:S(2)}, u32[]{:S(2)}) collective-permute-start(bf16[512,1024]{1,0:T(8,128)(2,1)} %bitcast.6), channel_id=1, source_target_pairs={{9,16},{11,18},{13,20},{15,22},{16,9},{18,11},{20,13},{22,15}} | collective-permute-start | bytes 3145736 | tf_op jit(solution)/shard_map/ppermute | solution.py:389
  4.2 27.4 %collective-permute-start.3 = (bf16[2192,128]{1,0:T(8,128)(2,1)S(1)}, bf16[2192,128]{1,0:T(8,128)(2,1)S(1)}, u32[]{:S(2)}, u32[]{:S(2)}) collective-permute-start(bf16[2192,128]{1,0:T(8,128)(2,1)S(1)} %get-tuple-element.28), channel_id=1, source_target_pairs={{0,8},{2,10},{4,12},{6,14},{8,0},{10,2},{12,4},{14,6},{17,25},{19,... | collective-permute-start | bytes 1683464 | tf_op jit(solution)/shard_map/ppermute | solution.py:389
  9.1 22.4 %collective-permute-start.4 = (bf16[2064,128]{1,0:T(8,128)(2,1)S(1)}, bf16[2064,128]{1,0:T(8,128)(2,1)S(1)}, u32[]{:S(2)}, u32[]{:S(2)}) collective-permute-start(bf16[2064,128]{1,0:T(8,128)(2,1)S(1)} %get-tuple-element.24.rest_1_), channel_id=1, source_target_pairs={{0,4},{2,6},{4,0},{6,2},{8,12},{10,14},{12,8},{14,10},{17,21},{19,... | collective-permute-start | bytes 1585160 | tf_op jit(solution)/shard_map/ppermute | solution.py:389
  12.6 19.0 %collective-permute-start.2 = (bf16[2064,128]{1,0:T(8,128)(2,1)S(1)}, bf16[2064,128]{1,0:T(8,128)(2,1)S(1)}, u32[]{:S(2)}, u32[]{:S(2)}) collective-permute-start(bf16[2064,128]{1,0:T(8,128)(2,1)S(1)} %get-tuple-element.29), channel_id=1, source_target_pairs={{0,12},{2,14},{4,8},{6,10},{8,4},{10,6},{12,0},{14,2},{17,29},{19,... | collective-permute-start | bytes 1585160 | tf_op jit(solution)/shard_map/ppermute | solution.py:389
  14.5 0.7 %collective-permute-start = (bf16[144,128]{1,0:T(8,128)(2,1)S(1)}, bf16[144,128]{1,0:T(8,128)(2,1)S(1)}, u32[]{:S(2)}, u32[]{:S(2)}) collective-permute-start(bf16[144,128]{1,0:T(8,128)(2,1)S(1)} %get-tuple-element.22), channel_id=1, source_target_pairs={{9,16},{11,18},{13,20},{15,22},{16,9},{18,11},{20,13},{22,15}} | collective-permute-start | bytes 110600 | tf_op jit(solution)/shard_map/ppermute | solution.py:389
  33.2 5.2 %collective-permute-start.5 = (bf16[1056,1024]{1,0:T(8,128)(2,1)S(1)}, bf16[1056,1024]{1,0:T(8,128)(2,1)S(1)}, u32[]{:S(2)}, u32[]{:S(2)}) collective-permute-start(bf16[1056,1024]{1,0:T(8,128)(2,1)S(1)} %early.1), channel_id=1, source_target_pairs={{0,1},{2,3},{4,5},{6,7},{8,9},{10,11},{12,13},{14,15},{17,16},{19,... | collective-permute-start | bytes 6488072 | tf_op jit(solution)/shard_map/ppermute | solution.py:389
  34.7 2.8 %collective-permute-start.7 = (bf16[2064,128]{1,0:T(8,128)(2,1)S(1)}, bf16[2064,128]{1,0:T(8,128)(2,1)S(1)}, u32[]{:S(2)}, u32[]{:S(2)}) collective-permute-start(bf16[2064,128]{1,0:T(8,128)(2,1)S(1)} %get-tuple-element.29), channel_id=1, source_target_pairs={{1,28},{3,30},{5,24},{7,26},{24,5},{26,7},{28,1},{30,3}} | collective-permute-start | bytes 1585160 | tf_op jit(solution)/shard_map/ppermute | solution.py:389
  35.4 2.8 %collective-permute-start.6 = (bf16[2192,128]{1,0:T(8,128)(2,1)S(1)}, bf16[2192,128]{1,0:T(8,128)(2,1)S(1)}, u32[]{:S(2)}, u32[]{:S(2)}) collective-permute-start(bf16[2192,128]{1,0:T(8,128)(2,1)S(1)} %get-tuple-element.28), channel_id=1, source_target_pairs={{1,24},{3,26},{5,28},{7,30},{24,1},{26,3},{28,5},{30,7}} | collective-permute-start | bytes 1683464 | tf_op jit(solution)/shard_map/ppermute | solution.py:389
  36.1 2.1 %collective-permute-start.8 = (bf16[2064,128]{1,0:T(8,128)(2,1)S(1)}, bf16[2064,128]{1,0:T(8,128)(2,1)S(1)}, u32[]{:S(2)}, u32[]{:S(2)}) collective-permute-start(bf16[2064,128]{1,0:T(8,128)(2,1)S(1)} %get-tuple-element.30), channel_id=1, source_target_pairs={{9,13},{11,15},{13,9},{15,11},{16,20},{18,22},{20,16},{22,18}} | collective-permute-start | bytes 1585160 | tf_op jit(solution)/shard_map/ppermute | solution.py:389
  36.8 3.8 %collective-permute-start.9 = (bf16[2064,128]{1,0:T(8,128)(2,1)S(1)}, bf16[2064,128]{1,0:T(8,128)(2,1)S(1)}, u32[]{:S(2)}, u32[]{:S(2)}) collective-permute-start(bf16[2064,128]{1,0:T(8,128)(2,1)S(1)} %get-tuple-element.37), channel_id=1, source_target_pairs={{1,16},{3,18},{5,20},{7,22},{24,9},{26,11},{28,13},{30,15},{9,1},{... | collective-permute-start | bytes 1585160 | tf_op jit(solution)/shard_map/ppermute | solution.py:389
  37.5 3.1 %collective-permute-start.10 = (bf16[2064,128]{1,0:T(8,128)(2,1)S(1)}, bf16[2064,128]{1,0:T(8,128)(2,1)S(1)}, u32[]{:S(2)}, u32[]{:S(2)}) collective-permute-start(bf16[2064,128]{1,0:T(8,128)(2,1)S(1)} %get-tuple-element.38), channel_id=1, source_target_pairs={{1,20},{3,22},{5,16},{7,18},{24,13},{26,15},{28,9},{30,11},{9,5},{... | collective-permute-start | bytes 1585160 | tf_op jit(solution)/shard_map/ppermute | solution.py:389
  40.6 19.7 %copy-start = (s32[1,512]{1,0:T(1,128)S(1)}, s32[1,512]{1,0:T(1,128)}, u32[]{:S(2)}) copy-start(s32[1,512]{1,0:T(1,128)} %ids_ref.1) | copy-start | bytes 6148

commit v9 on v8

--- a/solution.py
+++ b/solution.py
@@ -124,49 +124,49 @@
 
 
 def far_kernel(chips, cap, strata_dev, extra, rows_ref, *rest):
-    inner = is_inner(chips)
-    direct, outs, (held, pick) = rest[: chips // 2], rest[chips // 2 : -2], rest[-2:]
-
-    @pl.when(inner)
+    in_a = lax.axis_index("grp") % 2 == lax.axis_index("blk") // chips
+    packs = jnp.logical_or(in_a, is_inner(chips))
+    own, outs, (held, pick) = rest[: chips - 1], rest[chips - 1 : -2], rest[-2:]
+
+    @pl.when(packs)
     def _():
         spread = extra[:TAIL, :].astype(jnp.float32)
         ids = jnp.concatenate([spread[i : i + 1, :] for i in range(0, TAIL, TAIL // 4)], axis=1)
         half = lax.axis_index("blk") // chips
         pack_into(ids, [], rows_ref, outs, held, pick, cap, strata_dev, half)
 
-    @pl.when(jnp.logical_not(inner))
+    @pl.when(jnp.logical_not(packs))
     def _():
-        for block, out in zip(direct, outs[chips // 2 :]):
+        for block, out in zip(own, outs[1:]):
             out[...] = block[: out.shape[0], :]
 
 
-def unpack(blocks, cap, strata_dev, units, id_col, others=None, use_others=None):
+def unpack(blocks, cap, strata_dev, units, id_col, other=None, use_other=None):
     each = len(blocks) * cap
     width = units.shape[1]
     depth = width // LANES * 2 * cap
 
-    def lay(some):
-        for i, block in enumerate(some):
-            for r in range(2):
-                at = r * each + i * cap
-                for c in range(width // LANES):
-                    units[at : at + cap, c * LANES : (c + 1) * LANES] = block[
-                        (2 * c + r) * cap : (2 * c + r + 1) * cap, :
-                    ]
-
-    if others is None:
-        lay(blocks)
-    else:
-        pl.when(use_others)(lambda: lay(others))
-        pl.when(jnp.logical_not(use_others))(lambda: lay(blocks))
+    def lay(i, block):
+        for r in range(2):
+            at = r * each + i * cap
+            for c in range(width // LANES):
+                units[at : at + cap, c * LANES : (c + 1) * LANES] = block[
+                    (2 * c + r) * cap : (2 * c + r + 1) * cap, :
+                ]
+
     id_rows = [[], []]
     for i, block in enumerate(blocks):
         tail = block[depth : depth + TAIL, :].astype(jnp.float32)
-        if others is not None:
-            other = others[i][depth : depth + TAIL, :].astype(jnp.float32)
+        if i == 0 and other is not None:
+            pl.when(use_other)(lambda: lay(0, other))
+            pl.when(jnp.logical_not(use_other))(lambda: lay(0, blocks[0]))
             tail = jnp.where(
-                jnp.broadcast_to(use_others.astype(jnp.int32), tail.shape) > 0, other, tail
+                jnp.broadcast_to(use_other.astype(jnp.int32), tail.shape) > 0,
+                other[depth : depth + TAIL, :].astype(jnp.float32),
+                tail,
             )
+        else:
+            lay(i, block)
         for r in range(2):
             at = r * each + i * cap
             ids = tail[8 * r : 8 * r + 1, :]
@@ -260,11 +260,7 @@
 
 
 def mid_kernel(chips, cap, group_a, extra, *rest):
-    direct, spread, (units, id_col, facts, facts_a, col_a, cents) = (
-        rest[: chips // 2],
-        rest[chips // 2 : chips],
-        rest[chips:],
-    )
+    kept, blocks, (units, id_col, facts, facts_a, col_a, cents) = rest[0], rest[1:-6], rest[-6:]
     inner = is_inner(chips)
     strata_dev, width = cents.shape[0] // 2, cents.shape[1]
     depth = width // LANES * 2 * cap + TAIL
@@ -277,7 +273,7 @@
 
     cents[:strata_dev, :] = group_a[2 * each : 2 * each + strata_dev, :]
     pl.when(inner)(lambda: place(extra, TAIL))
-    pl.when(jnp.logical_not(inner))(lambda: place(direct[0], depth))
+    pl.when(jnp.logical_not(inner))(lambda: place(blocks[0], depth))
     tail = group_a[2 * each + strata_dev :, :each].astype(jnp.float32)
     density_a = []
     for r in range(2):
@@ -291,7 +287,7 @@
         facts_a[4 + r : 5 + r, :] = own_centroid(
             across(near, group_a[r * each : (r + 1) * each, :]), row
         )
-    ids = unpack(direct, cap, strata_dev, units, id_col, spread, inner)
+    ids = unpack(blocks, cap, strata_dev, units, id_col, kept, inner)
     (old,), density, picked = join([(group_a, col_a, density_a)], units, id_col, ids, cents)
     for r, row in enumerate(ids):
         facts[r : r + 1, :] = density[r]
@@ -394,8 +390,8 @@
         return pltpu.VMEM(dims, dtype)
 
     held = [pltpu.VMEM((rows, width), jnp.bfloat16), pltpu.VMEM((shards * cap, rows), jnp.bfloat16)]
-    order = [0, *reversed(range(1, chips))]
     swap = [((b, g), (b ^ flip, g ^ 1)) for b, g in inner]
+    swap += [((b, g), (b ^ side, g)) for b, g in kind_a]
     far_rows = send(embeddings[0], swap)
     *near, extra = pl.pallas_call(
         functools.partial(near_kernel, chips, cap),
@@ -416,27 +412,29 @@
         name="near",
     )(strata, centroids[0], embeddings[0])
     blocks_a = [
-        near[d] if d == 0 else send(near[d], [((b, g), (b ^ d, g)) for b, g in kind_a])
-        for d in order
+        near[e] if e == 0 else send(near[e], [((b, g), (b ^ e, g)) for b, g in kind_a])
+        for e in range(side)
     ]
     extra = send(extra, swap)
     out = pl.pallas_call(
         functools.partial(far_kernel, chips, cap, strata_dev),
         out_shape=[shape(depth, LANES)] * chips,
-        in_specs=[VMEM] * (2 + side),
+        in_specs=[VMEM] * (chips + 1),
         out_specs=[VMEM] * chips,
         scratch_shapes=held,
         compiler_params=params(20),
         name="far",
-    )(extra, far_rows, *near[:side])
-    direct = []
-    for e in range(side):
-        block, _ = lax.optimization_barrier((near[side + e], out[0]))
-        direct.append(send(block, [((b, g), (b ^ (flip + e), g ^ 1)) for b, g in outer]))
-    spread = [
-        out[e] if e == 0 else send(out[e], [((b, g), (b ^ e, g)) for b, g in inner])
-        for e in range(side)
-    ]
+    )(extra, far_rows, *near[side + 1 :], *near[:side])
+    block, _ = lax.optimization_barrier((near[side], out[0]))
+    first = [send(block, [((b, g), (b ^ flip, g ^ 1)) for b, g in outer])]
+    for e in range(1, side):
+        first.append(
+            send(
+                out[e],
+                [((b, g), (b ^ (flip + e), g ^ 1)) for b, g in outer]
+                + [((b, g), (b ^ e, g)) for b, g in inner],
+            )
+        )
     last = [
         send(
             out[side + e],
@@ -445,6 +443,9 @@
         )
         for e in range(side)
     ]
+    blocks_a.append(out[0])
+    for e in range(1, side):
+        blocks_a.append(send(out[e], [((b, g), (b ^ e, g)) for b, g in kind_a]))
     group_a = pl.pallas_call(
         functools.partial(early_kernel, chips, cap, strata_dev),
         out_shape=shape(2 * each + strata_dev + TAIL, width),
@@ -465,15 +466,15 @@
             shape(2 * each, LANES, dtype=jnp.float32),
             shape(2 * strata_dev, width),
         ],
-        in_specs=[VMEM] * (chips + 2),
+        in_specs=[VMEM] * (side + 3),
         out_specs=[VMEM] * 6,
         compiler_params=params(20),
         name="mid",
-    )(group_a, extra, *direct, *spread)
+    )(group_a, extra, out[0], *first)
     sent = pl.pallas_call(
         functools.partial(
             late_kernel,
-            [*order, *(flip + e for e in range(side)), *(chips + e for e in range(side))],
+            [*range(chips), *(flip + e for e in range(side)), *(chips + e for e in range(side))],
             cap,
             groups,
         ),

time: 61.5 us -> 60.6 us (0.985)
  blocking collectives: 18 us -> 10.9 us
  starting transfers between devices: 16.6 us -> 19.1 us
  waiting for transfers between devices: 16.5 us -> 18.8 us
  Pallas kernels: 9.89 us -> 11.3 us
    all_to_all x1, blocking collectives: 18 us -> 10.9 us  [body(): lax.all_to_all(sent.reshape(shards * groups, 4, LANES), AXES, 0, 0, tiled...]
    ppermute x11 -> x9, starting transfers between devices: 16.6 us -> 19.1 us  [send(): lax.ppermute(array, AXES, [(b * groups + g, to_b * groups + to_g) for (b,...]
    ppermute x11 -> x9, waiting for transfers between devices: 16.5 us -> 18.8 us  [send(): lax.ppermute(array, AXES, [(b * groups + g, to_b * groups + to_g) for (b,...]
    pallas_call x1, Pallas kernels: 0.1 us -> 1.6 us  [body(): pl.pallas_call(functools.partial(far_kernel, chips, cap, strata_dev), out...]
  transfers between devices with their start and end apart: 11 -> 9, of which waited for: 2 -> 3; matrix products, arithmetic and copies ran while one was open for 0% -> 0% of each run, Pallas kernels for 9% -> 12%
where the time goes in v9:
time: 60.6 us; the launch traced here: 60.2 us
  starting transfers between devices  19.1 us (32%)
  waiting for transfers between devices  18.8 us (31%)
  Pallas kernels  11.3 us (19%)
  blocking collectives  10.9 us (18%)
    ppermute x9, starting transfers between devices, send(): lax.ppermute(array, AXES, [(b * groups + g, to_b * groups + to_g) for (b,...  19.1 us
    ppermute x9, waiting for transfers between devices, send(): lax.ppermute(array, AXES, [(b * groups + g, to_b * groups + to_g) for (b,...  18.8 us
    all_to_all x1, blocking collectives, body(): lax.all_to_all(sent.reshape(shards * groups, 4, LANES), AXES, 0, 0, tiled...  10.9 us
    pallas_call x1, Pallas kernels, body(): pl.pallas_call(functools.partial(near_kernel, chips, cap), out_shape=[sha...  3.46 us
    pallas_call x1, Pallas kernels, body(): pl.pallas_call(functools.partial(mid_kernel, chips, cap), out_shape=[shap...  2.06 us
    pallas_call x1, Pallas kernels, body(): pl.pallas_call(functools.partial(late_kernel, [*range(chips), *(flip + e...  1.7 us
    pallas_call x1, Pallas kernels, body(): pl.pallas_call(functools.partial(early_kernel, chips, cap, strata_dev), o...  1.62 us
    pallas_call x1, Pallas kernels, body(): pl.pallas_call(functools.partial(far_kernel, chips, cap, strata_dev), out...  1.6 us
  transfers between devices with their start and end apart: 9, of which 3 were waited for; matrix products, arithmetic and copies ran while one was open for 0% of the time, Pallas kernels for 12%

profile of v9, /device:TPU:0, one launch (start us, length us, event | category | flops | bytes accessed | tf_op | source)
XLA Modules:
  0.0 60.2 jit_solution(10097834730944447987)
XLA Ops:
  0.0 4.9 %collective-permute-start.1 = (bf16[512,1024]{1,0:T(8,128)(2,1)}, bf16[512,1024]{1,0:T(8,128)(2,1)S(1)}, u32[]{:S(2)}, u32[]{:S(2)}) collective-permute-start(bf16[512,1024]{1,0:T(8,128)(2,1)} %bitcast.6), channel_id=1, source_target_pairs={{9,16},{11,18},{13,20},{15,22},{16,9},{18,11},{20,13},{22,15},{0,8... | collective-permute-start | bytes 3145736 | tf_op jit(solution)/shard_map/ppermute | solution.py:385
  4.9 3.5 %near.1 = (bf16[2192,128]{1,0:T(8,128)(2,1)S(1)}, bf16[2064,128]{1,0:T(8,128)(2,1)S(1)}, bf16[2192,128]{1,0:T(8,128)(2,1)S(1)}, bf16[2064,128]{1,0:T(8,128)(2,1)S(1)}, bf16[144,128]{1,0:T(8,128)(2,1)S(1)}) custom-call(s32[1,512]{1,0:T(1,128)} %ids_ref.1, bf16[16,1024]{1,0:T(8,128)(2,1)} %bitcast.8, bf16[512,1024]{1,0:T(8,128)(2,1)} %bitcast.7), custom_call_target="tpu_custom_call" | custom-call | tf_op jit(solution)/shard_map/near/pallas_call | solution.py:396
  8.4 1.9 %collective-permute-start = (bf16[144,128]{1,0:T(8,128)(2,1)S(1)}, bf16[144,128]{1,0:T(8,128)(2,1)S(1)}, u32[]{:S(2)}, u32[]{:S(2)}) collective-permute-start(bf16[144,128]{1,0:T(8,128)(2,1)S(1)} %get-tuple-element.21), channel_id=1, source_target_pairs={{9,16},{11,18},{13,20},{15,22},{16,9},{18,11},{20,13},{22,15},{0,8... | collective-permute-start | bytes 110600 | tf_op jit(solution)/shard_map/ppermute | solution.py:385
  10.3 3.9 %collective-permute-start.2 = (bf16[2064,128]{1,0:T(8,128)(2,1)S(1)}, bf16[2064,128]{1,0:T(8,128)(2,1)S(1)}, u32[]{:S(2)}, u32[]{:S(2)}) collective-permute-start(bf16[2064,128]{1,0:T(8,128)(2,1)S(1)} %get-tuple-element.24.rest_2_), channel_id=1, source_target_pairs={{0,4},{2,6},{4,0},{6,2},{8,12},{10,14},{12,8},{14,10},{17,21},{19,... | collective-permute-start | bytes 1585160 | tf_op jit(solution)/shard_map/ppermute | solution.py:385
  14.2 6.2 %collective-permute-done.extra = bf16[144,128]{1,0:T(8,128)(2,1)S(1)} collective-permute-done((bf16[144,128]{1,0:T(8,128)(2,1)S(1)}, bf16[144,128]{1,0:T(8,128)(2,1)S(1)}, u32[]{:S(2)}, u32[]{:S(2)}) %collective-permute-start) | collective-permute-done | bytes 36896 | tf_op jit(solution)/shard_map/ppermute | solution.py:385
  20.4 0.0 collective-permute-done.1.rows_ref
  20.4 1.6 %far.1 = (bf16[2064,128]{1,0:T(8,128)(2,1)S(1)}, bf16[2064,128]{1,0:T(8,128)(2,1)S(1)}, bf16[2064,128]{1,0:T(8,128)(2,1)S(1)}, bf16[2064,128]{1,0:T(8,128)(2,1)S(1)}) custom-call(bf16[144,128]{1,0:T(8,128)(2,1)S(1)} %collective-permute-done.extra, bf16[512,1024]{1,0:T(8,128)(2,1)S(1)} %collective-permute-done.1.rows_ref, ...), custom_call_target="tpu_custom_call" | custom-call | tf_op jit(solution)/shard_map/far/pallas_call | solution.py:419
  22.0 4.2 %collective-permute-start.3 = (bf16[2064,128]{1,0:T(8,128)(2,1)S(1)}, bf16[2064,128]{1,0:T(8,128)(2,1)S(1)}, u32[]{:S(2)}, u32[]{:S(2)}) collective-permute-start(bf16[2064,128]{1,0:T(8,128)(2,1)S(1)} %get-tuple-element.26), channel_id=1, source_target_pairs={{0,4},{2,6},{4,0},{6,2},{8,12},{10,14},{12,8},{14,10},{17,21},{19,... | collective-permute-start | bytes 1585160 | tf_op jit(solution)/shard_map/ppermute | solution.py:385
  26.2 0.0 collective-permute-done.2.rest_1_
  26.2 11.7 %collective-permute-done.3.rest_3_ = bf16[2064,128]{1,0:T(8,128)(2,1)S(1)} collective-permute-done((bf16[2064,128]{1,0:T(8,128)(2,1)S(1)}, bf16[2064,128]{1,0:T(8,128)(2,1)S(1)}, u32[]{:S(2)}, u32[]{:S(2)}) %collective-permute-start.3) | collective-permute-done | bytes 528416 | tf_op jit(solution)/shard_map/ppermute | solution.py:385
  37.9 1.6 %early.1 = bf16[1056,1024]{1,0:T(8,128)(2,1)S(1)} custom-call(bf16[2064,128]{1,0:T(8,128)(2,1)S(1)} %get-tuple-element.25.after.rest_2_.rest_0_, bf16[2192,128]{1,0:T(8,128)(2,1)S(1)} %get-tuple-element.23.rest_1_.rest_0_, bf16[2064,128]{1,0:T(8,128)(2,1)S(1)} %collective-permute-done.2.rest_1_, ...), custom_call_target="tpu_custom_call" | custom-call | tf_op jit(solution)/shard_map/early/pallas_call | solution.py:449
  39.5 1.4 %collective-permute-start.4 = (bf16[1056,1024]{1,0:T(8,128)(2,1)S(1)}, bf16[1056,1024]{1,0:T(8,128)(2,1)S(1)}, u32[]{:S(2)}, u32[]{:S(2)}) collective-permute-start(bf16[1056,1024]{1,0:T(8,128)(2,1)S(1)} %early.1), channel_id=1, source_target_pairs={{0,1},{2,3},{4,5},{6,7},{8,9},{10,11},{12,13},{14,15},{17,16},{19,... | collective-permute-start | bytes 6488072 | tf_op jit(solution)/shard_map/ppermute | solution.py:385
  41.0 0.7 %collective-permute-start.5 = (bf16[2192,128]{1,0:T(8,128)(2,1)S(1)}, bf16[2192,128]{1,0:T(8,128)(2,1)S(1)}, u32[]{:S(2)}, u32[]{:S(2)}) collective-permute-start(bf16[2192,128]{1,0:T(8,128)(2,1)S(1)} %get-tuple-element.28), channel_id=1, source_target_pairs={{1,24},{3,26},{5,28},{7,30},{24,1},{26,3},{28,5},{30,7}} | collective-permute-start | bytes 1683464 | tf_op jit(solution)/shard_map/ppermute | solution.py:385
  41.7 0.7 %collective-permute-start.6 = (bf16[2064,128]{1,0:T(8,128)(2,1)S(1)}, bf16[2064,128]{1,0:T(8,128)(2,1)S(1)}, u32[]{:S(2)}, u32[]{:S(2)}) collective-permute-start(bf16[2064,128]{1,0:T(8,128)(2,1)S(1)} %get-tuple-element.26), channel_id=1, source_target_pairs={{1,28},{3,30},{5,24},{7,26},{24,5},{26,7},{28,1},{30,3},{9,13},{11... | collective-permute-start | bytes 1585160 | tf_op jit(solution)/shard_map/ppermute | solution.py:385
  42.4 0.7 %collective-permute-start.7 = (bf16[2064,128]{1,0:T(8,128)(2,1)S(1)}, bf16[2064,128]{1,0:T(8,128)(2,1)S(1)}, u32[]{:S(2)}, u32[]{:S(2)}) collective-permute-start(bf16[2064,128]{1,0:T(8,128)(2,1)S(1)} %get-tuple-element.35), channel_id=1, source_target_pairs={{1,16},{3,18},{5,20},{7,22},{24,9},{26,11},{28,13},{30,15},{9,1},{... | collective-permute-start | bytes 1585160 | tf_op jit(solution)/shard_map/ppermute | solution.py:385
  43.1 0.7 %collective-permute-start.8 = (bf16[2064,128]{1,0:T(8,128)(2,1)S(1)}, bf16[2064,128]{1,0:T(8,128)(2,1)S(1)}, u32[]{:S(2)}, u32[]{:S(2)}) collective-permute-start(bf16[2064,128]{1,0:T(8,128)(2,1)S(1)} %get-tuple-element.36), channel_id=1, source_target_pairs={{1,20},{3,22},{5,16},{7,18},{24,13},{26,15},{28,9},{30,11},{9,5},{... | collective-permute-start | bytes 1585160 | tf_op jit(solution)/shard_map/ppermute | solution.py:385
  43.8 0.0 collective-permute-done.6.rest_2_
  43.8 0.0 collective-permute-done.5.rest_1_
  43.8 0.9 %collective-permute-done.4.group_a.units_a = bf16[1056,1024]{1,0:T(8,128)(2,1)S(1)} collective-permute-done((bf16[1056,1024]{1,0:T(8,128)(2,1)S(1)}, bf16[1056,1024]{1,0:T(8,128)(2,1)S(1)}, u32[]{:S(2)}, u32[]{:S(2)}) %collective-permute-start.4) | collective-permute-done | bytes 2162720 | tf_op jit(solution)/shard_map/ppermute | solution.py:385
  44.7 2.1 %mid.1 = (bf16[512,1024]{1,0:T(8,128)(2,1)S(1)}, f32[512,128]{1,0:T(8,128)S(1)}, f32[8,256]{1,0:T(8,128)S(1)}, f32[8,512]{1,0:T(8,128)S(1)}, f32[1024,128]{1,0:T(8,128)S(1)}, /*index=5*/bf16[32,1024]{1,0:T(8,128)(2,1)S(1)}) custom-call(bf16[1056,1024]{1,0:T(8,128)(2,1)S(1)} %collective-permute-done.4.group_a.units_a, ...), custom_call_target="tpu_custom_call" | custom-call | tf_op jit(solution)/shard_map/mid/pallas_call | solution.py:459
  46.8 0.0 collective-permute-done.7.rest_0_
  46.8 0.0 collective-permute-done.8.rest_1_
  46.8 0.0 copy-start
  46.8 1.7 %late.1 = f32[128,128]{1,0:T(8,128)S(1)} custom-call(bf16[1056,1024]{1,0:T(8,128)(2,1)S(1)} %collective-permute-done.4.group_a.units_a, f32[1024,128]{1,0:T(8,128)S(1)} %get-tuple-element.29.col_a, f32[8,512]{1,0:T(8,128)S(1)} %get-tuple-element.30.facts_a, bf16[512,1024]{1,0:T(8,128)(2,1)S(1)} %get-tuple-element.31.units_m, ...), custom_call_target="tpu_custom_call" | custom-call | tf_op jit(solution)/shard_map/late/pallas_call | solution.py:474
  48.5 10.9 %all_to_all.5 = f32[32,4,128]{2,1,0:T(4,128)S(1)} all-to-all(f32[32,4,128]{2,1,0:T(4,128)S(1)} %bitcast.4), channel_id=1, replica_groups=mesh['blk'=8,'grp'=4] {'blk','grp'}, dimensions={0} | all-to-all | bytes 131072 | tf_op jit(solution)/shard_map/all_to_all | solution.py:491
  59.4 0.0 copy-done
  59.4 0.8 %finish.1 = f32[1,512]{1,0:T(1,128)} custom-call(s32[1,512]{1,0:T(1,128)S(1)} %copy-done, f32[128,128]{1,0:T(8,128)S(1)} %bitcast.5), custom_call_target="tpu_custom_call" | custom-call | tf_op jit(solution)/shard_map/finish/pallas_call | solution.py:494
Async XLA Ops:
  0.0 20.4 %collective-permute-start.1 = (bf16[512,1024]{1,0:T(8,128)(2,1)}, bf16[512,1024]{1,0:T(8,128)(2,1)S(1)}, u32[]{:S(2)}, u32[]{:S(2)}) collective-permute-start(bf16[512,1024]{1,0:T(8,128)(2,1)} %bitcast.6), channel_id=1, source_target_pairs={{9,16},{11,18},{13,20},{15,22},{16,9},{18,11},{20,13},{22,15},{0,8... | collective-permute-start | bytes 3145736 | tf_op jit(solution)/shard_map/ppermute | solution.py:385
  8.4 12.0 %collective-permute-start = (bf16[144,128]{1,0:T(8,128)(2,1)S(1)}, bf16[144,128]{1,0:T(8,128)(2,1)S(1)}, u32[]{:S(2)}, u32[]{:S(2)}) collective-permute-start(bf16[144,128]{1,0:T(8,128)(2,1)S(1)} %get-tuple-element.21), channel_id=1, source_target_pairs={{9,16},{11,18},{13,20},{15,22},{16,9},{18,11},{20,13},{22,15},{0,8... | collective-permute-start | bytes 110600 | tf_op jit(solution)/shard_map/ppermute | solution.py:385
  10.3 15.8 %collective-permute-start.2 = (bf16[2064,128]{1,0:T(8,128)(2,1)S(1)}, bf16[2064,128]{1,0:T(8,128)(2,1)S(1)}, u32[]{:S(2)}, u32[]{:S(2)}) collective-permute-start(bf16[2064,128]{1,0:T(8,128)(2,1)S(1)} %get-tuple-element.24.rest_2_), channel_id=1, source_target_pairs={{0,4},{2,6},{4,0},{6,2},{8,12},{10,14},{12,8},{14,10},{17,21},{19,... | collective-permute-start | bytes 1585160 | tf_op jit(solution)/shard_map/ppermute | solution.py:385
  22.0 15.9 %collective-permute-start.3 = (bf16[2064,128]{1,0:T(8,128)(2,1)S(1)}, bf16[2064,128]{1,0:T(8,128)(2,1)S(1)}, u32[]{:S(2)}, u32[]{:S(2)}) collective-permute-start(bf16[2064,128]{1,0:T(8,128)(2,1)S(1)} %get-tuple-element.26), channel_id=1, source_target_pairs={{0,4},{2,6},{4,0},{6,2},{8,12},{10,14},{12,8},{14,10},{17,21},{19,... | collective-permute-start | bytes 1585160 | tf_op jit(solution)/shard_map/ppermute | solution.py:385
  39.5 5.2 %collective-permute-start.4 = (bf16[1056,1024]{1,0:T(8,128)(2,1)S(1)}, bf16[1056,1024]{1,0:T(8,128)(2,1)S(1)}, u32[]{:S(2)}, u32[]{:S(2)}) collective-permute-start(bf16[1056,1024]{1,0:T(8,128)(2,1)S(1)} %early.1), channel_id=1, source_target_pairs={{0,1},{2,3},{4,5},{6,7},{8,9},{10,11},{12,13},{14,15},{17,16},{19,... | collective-permute-start | bytes 6488072 | tf_op jit(solution)/shard_map/ppermute | solution.py:385
  41.0 2.8 %collective-permute-start.5 = (bf16[2192,128]{1,0:T(8,128)(2,1)S(1)}, bf16[2192,128]{1,0:T(8,128)(2,1)S(1)}, u32[]{:S(2)}, u32[]{:S(2)}) collective-permute-start(bf16[2192,128]{1,0:T(8,128)(2,1)S(1)} %get-tuple-element.28), channel_id=1, source_target_pairs={{1,24},{3,26},{5,28},{7,30},{24,1},{26,3},{28,5},{30,7}} | collective-permute-start | bytes 1683464 | tf_op jit(solution)/shard_map/ppermute | solution.py:385
  41.7 2.1 %collective-permute-start.6 = (bf16[2064,128]{1,0:T(8,128)(2,1)S(1)}, bf16[2064,128]{1,0:T(8,128)(2,1)S(1)}, u32[]{:S(2)}, u32[]{:S(2)}) collective-permute-start(bf16[2064,128]{1,0:T(8,128)(2,1)S(1)} %get-tuple-element.26), channel_id=1, source_target_pairs={{1,28},{3,30},{5,24},{7,26},{24,5},{26,7},{28,1},{30,3},{9,13},{11... | collective-permute-start | bytes 1585160 | tf_op jit(solution)/shard_map/ppermute | solution.py:385
  42.4 4.4 %collective-permute-start.7 = (bf16[2064,128]{1,0:T(8,128)(2,1)S(1)}, bf16[2064,128]{1,0:T(8,128)(2,1)S(1)}, u32[]{:S(2)}, u32[]{:S(2)}) collective-permute-start(bf16[2064,128]{1,0:T(8,128)(2,1)S(1)} %get-tuple-element.35), channel_id=1, source_target_pairs={{1,16},{3,18},{5,20},{7,22},{24,9},{26,11},{28,13},{30,15},{9,1},{... | collective-permute-start | bytes 1585160 | tf_op jit(solution)/shard_map/ppermute | solution.py:385
  43.1 3.7 %collective-permute-start.8 = (bf16[2064,128]{1,0:T(8,128)(2,1)S(1)}, bf16[2064,128]{1,0:T(8,128)(2,1)S(1)}, u32[]{:S(2)}, u32[]{:S(2)}) collective-permute-start(bf16[2064,128]{1,0:T(8,128)(2,1)S(1)} %get-tuple-element.36), channel_id=1, source_target_pairs={{1,20},{3,22},{5,16},{7,18},{24,13},{26,15},{28,9},{30,11},{9,5},{... | collective-permute-start | bytes 1585160 | tf_op jit(solution)/shard_map/ppermute | solution.py:385
  46.8 12.6 %copy-start = (s32[1,512]{1,0:T(1,128)S(1)}, s32[1,512]{1,0:T(1,128)}, u32[]{:S(2)}) copy-start(s32[1,512]{1,0:T(1,128)} %ids_ref.1) | copy-start | bytes 6148

commit v10 on v9

--- a/solution.py
+++ b/solution.py
@@ -238,62 +238,83 @@
     return [high, middle, value - high - middle]
 
 
-def early_kernel(chips, cap, strata_dev, after, *rest):
-    blocks, (held, id_col) = rest[:chips], rest[chips:]
-    in_a = lax.axis_index("grp") % 2 == lax.axis_index("blk") // chips
-
-    @pl.when(in_a)
+def in_a(chips):
+    return lax.axis_index("grp") % 2 == lax.axis_index("blk") // chips
+
+
+def first_kernel(chips, cap, strata_dev, after, *rest):
+    blocks, (held, id_col, facts) = rest[:-3], rest[-3:]
+
+    @pl.when(in_a(chips))
     def _():
         width = held.shape[1]
-        each = chips * cap
+        size = len(blocks) * cap
         depth = width // LANES * 2 * cap + TAIL
         ids = unpack(blocks, cap, strata_dev, held, id_col)
         for c in range(width // LANES):
             at = depth + c * strata_dev
-            held[2 * each : 2 * each + strata_dev, c * LANES : (c + 1) * LANES] = blocks[0][
-                at : at + strata_dev, :
-            ]
+            held[2 * size :, c * LANES : (c + 1) * LANES] = blocks[0][at : at + strata_dev, :]
         _, density, _ = join([], held, id_col, ids)
-        rows = [*parts_of(density[0]), *parts_of(density[1]), *ids]
-        tail = jnp.concatenate(rows + rows, axis=0).astype(jnp.bfloat16)
-        held[2 * each + strata_dev :, :each] = tail
-
-
-def mid_kernel(chips, cap, group_a, extra, *rest):
-    kept, blocks, (units, id_col, facts, facts_a, col_a, cents) = rest[0], rest[1:-6], rest[-6:]
+        for r, row in enumerate(ids):
+            facts[r : r + 1, :] = density[r]
+            facts[2 + r : 3 + r, :] = row
+
+
+def second_kernel(chips, cap, strata_dev, old_units, old_col, old_facts, *rest):
+    blocks, (held, id_col) = rest[:-2], rest[-2:]
+
+    @pl.when(in_a(chips))
+    def _():
+        size = len(blocks) * cap
+        ids = unpack(blocks, cap, strata_dev, held, id_col)
+        old = [old_facts[r : r + 1, :] for r in range(2)]
+        (earlier,), density, _ = join([(old_units, old_col, old)], held, id_col, ids)
+        rows = []
+        for r in range(2):
+            rows += parts_of(jnp.concatenate([earlier[r], density[r]], axis=1))
+        for r in range(2):
+            rows.append(jnp.concatenate([old_facts[2 + r : 3 + r, :], ids[r]], axis=1))
+        held[2 * size :, : chips * cap] = jnp.concatenate(rows + rows, axis=0).astype(jnp.bfloat16)
+
+
+def mid_kernel(chips, cap, first_a, second_a, extra, *rest):
+    kept, blocks, outs = rest[0], rest[1:-7], rest[-7:]
+    units, id_col, facts, facts_a, col_first, col_second, cents = outs
     inner = is_inner(chips)
     strata_dev, width = cents.shape[0] // 2, cents.shape[1]
     depth = width // LANES * 2 * cap + TAIL
-    each = chips * cap
+    each, size = chips * cap, chips // 2 * cap
 
     def place(block, base):
         for c in range(width // LANES):
             at = base + c * strata_dev
             cents[strata_dev:, c * LANES : (c + 1) * LANES] = block[at : at + strata_dev, :]
 
-    cents[:strata_dev, :] = group_a[2 * each : 2 * each + strata_dev, :]
+    cents[:strata_dev, :] = first_a[2 * size :, :]
     pl.when(inner)(lambda: place(extra, TAIL))
     pl.when(jnp.logical_not(inner))(lambda: place(blocks[0], depth))
-    tail = group_a[2 * each + strata_dev :, :each].astype(jnp.float32)
-    density_a = []
+    tail = second_a[2 * size :, :each].astype(jnp.float32)
+    groups = [(first_a, col_first, []), (second_a, col_second, [])]
     for r in range(2):
-        density_a.append(
-            tail[3 * r : 3 * r + 1, :] + tail[3 * r + 1 : 3 * r + 2, :] + tail[3 * r + 2 : 3 * r + 3, :]
-        )
-        row = tail[6 + r : 7 + r, :]
-        col_a[r * each : (r + 1) * each, :] = upright(row)
-        facts_a[2 + r : 3 + r, :] = row
+        density = tail[3 * r : 3 * r + 1, :] + tail[3 * r + 1 : 3 * r + 2, :]
+        density = density + tail[3 * r + 2 : 3 * r + 3, :]
+        facts_a[2 + r : 3 + r, :] = tail[6 + r : 7 + r, :]
         near = cents[r * strata_dev : (r + 1) * strata_dev, :]
-        facts_a[4 + r : 5 + r, :] = own_centroid(
-            across(near, group_a[r * each : (r + 1) * each, :]), row
-        )
+        at = slice(r * size, (r + 1) * size)
+        for i, (some, col, densities) in enumerate(groups):
+            lanes = slice(i * size, (i + 1) * size)
+            row = tail[6 + r : 7 + r, lanes]
+            col[at, :] = upright(row)
+            densities.append(density[:, lanes])
+            facts_a[4 + r : 5 + r, lanes] = own_centroid(across(near, some[at, :]), row)
     ids = unpack(blocks, cap, strata_dev, units, id_col, kept, inner)
-    (old,), density, picked = join([(group_a, col_a, density_a)], units, id_col, ids, cents)
+    old, density, picked = join(groups, units, id_col, ids, cents)
     for r, row in enumerate(ids):
         facts[r : r + 1, :] = density[r]
         facts[2 + r : 3 + r, :] = row
         facts[4 + r : 5 + r, :] = picked[r]
-        facts_a[r : r + 1, :] = old[r]
+        for i in range(2):
+            facts_a[r : r + 1, i * size : (i + 1) * size] = old[i][r]
 
 
 def upright(row):
@@ -306,24 +327,32 @@
     )
 
 
-def late_kernel(order, cap, groups, units_a, col_a, facts_a, units_m, col_m, facts_m, cents, *rest):
+def late_kernel(
+    order, cap, groups, first_a, second_a, col_first, col_second, facts_a, units_m, col_m, facts_m, cents, *rest
+):
     blocks, (out_ref, units, id_col) = rest[:-3], rest[-3:]
     strata_dev = cents.shape[0] // 2
     chips = len(order) // 2
     me, group = lax.axis_index("blk"), lax.axis_index("grp")
     at_work = (me // chips) != (group % 2)
     ids = unpack(blocks, cap, strata_dev, units, id_col)
+    size = chips // 2 * cap
     old = [
-        (some, col, [facts[r : r + 1, :] for r in range(2)])
-        for some, col, facts in ((units_a, col_a, facts_a), (units_m, col_m, facts_m))
+        (some, col, [facts_a[r : r + 1, i * size : (i + 1) * size] for r in range(2)])
+        for i, (some, col) in enumerate(((first_a, col_first), (second_a, col_second)))
     ]
+    old.append((units_m, col_m, [facts_m[r : r + 1, :] for r in range(2)]))
     earlier, density, picked_new = join(old, units, id_col, ids, cents)
     total = jnp.zeros((1, 1), jnp.float32)
     weights = []
     for r, row in enumerate(ids):
         states = [
-            (facts_a[2 + r : 3 + r, :], facts_a[4 + r : 5 + r, :], earlier[0][r]),
-            (facts_m[2 + r : 3 + r, :], facts_m[4 + r : 5 + r, :], earlier[1][r]),
+            (
+                facts_a[2 + r : 3 + r, :],
+                facts_a[4 + r : 5 + r, :],
+                jnp.concatenate([earlier[0][r], earlier[1][r]], axis=1),
+            ),
+            (facts_m[2 + r : 3 + r, :], facts_m[4 + r : 5 + r, :], earlier[2][r]),
             (row, picked_new[r], density[r]),
         ]
         row, picked, dense = [jnp.concatenate(parts, axis=1) for parts in zip(*states)]
@@ -435,42 +464,61 @@
                 + [((b, g), (b ^ e, g)) for b, g in inner],
             )
         )
-    last = [
-        send(
-            out[side + e],
-            [((b, g), (b ^ (chips + e), g ^ 1)) for b, g in outer]
-            + [((b, g), (b ^ (side + e), g)) for b, g in inner],
-        )
-        for e in range(side)
-    ]
     blocks_a.append(out[0])
     for e in range(1, side):
         blocks_a.append(send(out[e], [((b, g), (b ^ e, g)) for b, g in kind_a]))
-    group_a = pl.pallas_call(
-        functools.partial(early_kernel, chips, cap, strata_dev),
-        out_shape=shape(2 * each + strata_dev + TAIL, width),
-        in_specs=[ANY] + [VMEM] * chips,
+    size = side * cap
+    first_a, first_col, first_facts = pl.pallas_call(
+        functools.partial(first_kernel, chips, cap, strata_dev),
+        out_shape=[
+            shape(2 * size + strata_dev, width),
+            shape(2 * size, LANES, dtype=jnp.float32),
+            shape(8, size, dtype=jnp.float32),
+        ],
+        in_specs=[ANY] + [VMEM] * side,
+        out_specs=[VMEM] * 3,
+        compiler_params=params(20),
+        name="first",
+    )(out[0], *blocks_a[:side])
+    second_a = pl.pallas_call(
+        functools.partial(second_kernel, chips, cap, strata_dev),
+        out_shape=shape(2 * size + TAIL, width),
+        in_specs=[VMEM] * (3 + side),
         out_specs=VMEM,
-        scratch_shapes=[pltpu.VMEM((2 * each, LANES), jnp.float32)],
+        scratch_shapes=[pltpu.VMEM((2 * size, LANES), jnp.float32)],
         compiler_params=params(20),
-        name="early",
-    )(out[0], *blocks_a)
-    group_a = send(group_a, [((b, g), (b, g ^ 1)) for b, g in kind_a])
-    units_m, col_m, facts_m, facts_a, col_a, cents = pl.pallas_call(
+        name="second",
+    )(first_a, first_col, first_facts, *blocks_a[side:])
+    over = [((b, g), (b, g ^ 1)) for b, g in kind_a]
+    first_a, second_a = send(first_a, over), send(second_a, over)
+    last = []
+    for e in range(side):
+        block = out[side + e]
+        if e == side - 1:
+            block, _ = lax.optimization_barrier((block, first_a))
+        last.append(
+            send(
+                block,
+                [((b, g), (b ^ (chips + e), g ^ 1)) for b, g in outer]
+                + [((b, g), (b ^ (side + e), g)) for b, g in inner],
+            )
+        )
+    units_m, col_m, facts_m, facts_a, col_first, col_second, cents = pl.pallas_call(
         functools.partial(mid_kernel, chips, cap),
         out_shape=[
             shape(2 * side * cap, width),
             shape(2 * side * cap, LANES, dtype=jnp.float32),
             shape(8, side * cap, dtype=jnp.float32),
             shape(8, each, dtype=jnp.float32),
-            shape(2 * each, LANES, dtype=jnp.float32),
+            shape(2 * size, LANES, dtype=jnp.float32),
+            shape(2 * size, LANES, dtype=jnp.float32),
             shape(2 * strata_dev, width),
         ],
-        in_specs=[VMEM] * (side + 3),
-        out_specs=[VMEM] * 6,
+        in_specs=[VMEM] * (side + 4),
+        out_specs=[VMEM] * 7,
         compiler_params=params(20),
         name="mid",
-    )(group_a, extra, out[0], *first)
+    )(first_a, second_a, extra, out[0], *first)
     sent = pl.pallas_call(
         functools.partial(
             late_kernel,
@@ -479,7 +527,7 @@
             groups,
         ),
         out_shape=jax.ShapeDtypeStruct((shards * groups * 4, LANES), jnp.float32),
-        in_specs=[VMEM] * (7 + side),
+        in_specs=[VMEM] * (9 + side),
         out_specs=VMEM,
         scratch_shapes=[
             pltpu.VMEM((2 * side * cap, width), jnp.bfloat16),
@@ -487,7 +535,7 @@
         ],
         compiler_params=params(20),
         name="late",
-    )(group_a, col_a, facts_a, units_m, col_m, facts_m, cents, *last)
+    )(first_a, second_a, col_first, col_second, facts_a, units_m, col_m, facts_m, cents, *last)
     got = lax.all_to_all(
         sent.reshape(shards * groups, 4, LANES), AXES, 0, 0, tiled=True
     ).reshape(shards * groups * 4, LANES)

time: 60.6 us -> 60.2 us (level)
  waiting for transfers between devices: 18.8 us -> 15.7 us
  starting transfers between devices: 19.1 us -> 20.4 us
  blocking collectives: 10.9 us -> 12 us
    ppermute x9 -> x10, waiting for transfers between devices: 18.8 us -> 15.7 us  [send(): lax.ppermute(array, AXES, [(b * groups + g, to_b * groups + to_g) for (b,...]
    ppermute x9 -> x10, starting transfers between devices: 19.1 us -> 20.4 us  [send(): lax.ppermute(array, AXES, [(b * groups + g, to_b * groups + to_g) for (b,...]
    all_to_all x1, blocking collectives: 10.9 us -> 12 us  [body(): lax.all_to_all(sent.reshape(shards * groups, 4, LANES), AXES, 0, 0, tiled...]
    pallas_call x1 -> x2, Pallas kernels: 1.62 us -> 1.59 us  [the longest x1 0.99 us: body(): pl.pallas_call(functools.partial(second_kernel, chips, cap, strata_dev),...]
  transfers between devices with their start and end apart: 9 -> 10, of which waited for: 3 -> 2; matrix products, arithmetic and copies ran while one was open for 0% -> 0% of each run, Pallas kernels for 12% -> 15%
where the time goes in v10:
time: 60.2 us; the launch traced here: 59.8 us
  starting transfers between devices  20.4 us (34%)
  waiting for transfers between devices  15.7 us (26%)
  blocking collectives  12 us (20%)
  Pallas kernels  11.4 us (19%)
    ppermute x10, starting transfers between devices, send(): lax.ppermute(array, AXES, [(b * groups + g, to_b * groups + to_g) for (b,...  20.4 us
    ppermute x10, waiting for transfers between devices, send(): lax.ppermute(array, AXES, [(b * groups + g, to_b * groups + to_g) for (b,...  15.7 us
    all_to_all x1, blocking collectives, body(): lax.all_to_all(sent.reshape(shards * groups, 4, LANES), AXES, 0, 0, tiled...  12 us
    pallas_call x1, Pallas kernels, body(): pl.pallas_call(functools.partial(near_kernel, chips, cap), out_shape=[sha...  3.46 us
    pallas_call x1, Pallas kernels, body(): pl.pallas_call(functools.partial(mid_kernel, chips, cap), out_shape=[shap...  2.16 us
    pallas_call x1, Pallas kernels, body(): pl.pallas_call(functools.partial(late_kernel, [*range(chips), *(flip + e...  1.8 us
    pallas_call x1, Pallas kernels, body(): pl.pallas_call(functools.partial(far_kernel, chips, cap, strata_dev), out...  1.6 us
  transfers between devices with their start and end apart: 10, of which 2 were waited for; matrix products, arithmetic and copies ran while one was open for 0% of the time, Pallas kernels for 15%

profile of v10, /device:TPU:0, one launch (start us, length us, event | category | flops | bytes accessed | tf_op | source)
XLA Modules:
  0.0 59.8 jit_solution(11450070227537847251)
XLA Ops:
  0.0 4.9 %collective-permute-start.1 = (bf16[512,1024]{1,0:T(8,128)(2,1)}, bf16[512,1024]{1,0:T(8,128)(2,1)S(1)}, u32[]{:S(2)}, u32[]{:S(2)}) collective-permute-start(bf16[512,1024]{1,0:T(8,128)(2,1)} %bitcast.6), channel_id=1, source_target_pairs={{9,16},{11,18},{13,20},{15,22},{16,9},{18,11},{20,13},{22,15},{0,8... | collective-permute-start | bytes 3145736 | tf_op jit(solution)/shard_map/ppermute | solution.py:414
  4.9 3.5 %near.1 = (bf16[2192,128]{1,0:T(8,128)(2,1)S(1)}, bf16[2064,128]{1,0:T(8,128)(2,1)S(1)}, bf16[2192,128]{1,0:T(8,128)(2,1)S(1)}, bf16[2064,128]{1,0:T(8,128)(2,1)S(1)}, bf16[144,128]{1,0:T(8,128)(2,1)S(1)}) custom-call(s32[1,512]{1,0:T(1,128)} %ids_ref.1, bf16[16,1024]{1,0:T(8,128)(2,1)} %bitcast.8, bf16[512,1024]{1,0:T(8,128)(2,1)} %bitcast.7), custom_call_target="tpu_custom_call" | custom-call | tf_op jit(solution)/shard_map/near/pallas_call | solution.py:425
  8.4 3.4 %collective-permute-start.2 = (bf16[2064,128]{1,0:T(8,128)(2,1)S(1)}, bf16[2064,128]{1,0:T(8,128)(2,1)S(1)}, u32[]{:S(2)}, u32[]{:S(2)}) collective-permute-start(bf16[2064,128]{1,0:T(8,128)(2,1)S(1)} %get-tuple-element.29.rest_2_), channel_id=1, source_target_pairs={{0,4},{2,6},{4,0},{6,2},{8,12},{10,14},{12,8},{14,10},{17,21},{19,... | collective-permute-start | bytes 1585160 | tf_op jit(solution)/shard_map/ppermute | solution.py:414
  11.8 2.4 %collective-permute-start = (bf16[144,128]{1,0:T(8,128)(2,1)S(1)}, bf16[144,128]{1,0:T(8,128)(2,1)S(1)}, u32[]{:S(2)}, u32[]{:S(2)}) collective-permute-start(bf16[144,128]{1,0:T(8,128)(2,1)S(1)} %get-tuple-element.26), channel_id=1, source_target_pairs={{9,16},{11,18},{13,20},{15,22},{16,9},{18,11},{20,13},{22,15},{0,8... | collective-permute-start | bytes 110600 | tf_op jit(solution)/shard_map/ppermute | solution.py:414
  14.2 4.8 %collective-permute-done.extra = bf16[144,128]{1,0:T(8,128)(2,1)S(1)} collective-permute-done((bf16[144,128]{1,0:T(8,128)(2,1)S(1)}, bf16[144,128]{1,0:T(8,128)(2,1)S(1)}, u32[]{:S(2)}, u32[]{:S(2)}) %collective-permute-start) | collective-permute-done | bytes 36896 | tf_op jit(solution)/shard_map/ppermute | solution.py:414
  19.0 0.0 collective-permute-done.1.rows_ref
  19.0 1.6 %far.1 = (bf16[2064,128]{1,0:T(8,128)(2,1)S(1)}, bf16[2064,128]{1,0:T(8,128)(2,1)S(1)}, bf16[2064,128]{1,0:T(8,128)(2,1)S(1)}, bf16[2064,128]{1,0:T(8,128)(2,1)S(1)}) custom-call(bf16[144,128]{1,0:T(8,128)(2,1)S(1)} %collective-permute-done.extra, bf16[512,1024]{1,0:T(8,128)(2,1)S(1)} %collective-permute-done.1.rows_ref, ...), custom_call_target="tpu_custom_call" | custom-call | tf_op jit(solution)/shard_map/far/pallas_call | solution.py:448
  20.6 4.2 %collective-permute-start.4 = (bf16[2064,128]{1,0:T(8,128)(2,1)S(1)}, bf16[2064,128]{1,0:T(8,128)(2,1)S(1)}, u32[]{:S(2)}, u32[]{:S(2)}) collective-permute-start(bf16[2064,128]{1,0:T(8,128)(2,1)S(1)} %get-tuple-element.34), channel_id=1, source_target_pairs={{0,4},{2,6},{4,0},{6,2},{8,12},{10,14},{12,8},{14,10},{17,21},{19,... | collective-permute-start | bytes 1585160 | tf_op jit(solution)/shard_map/ppermute | solution.py:414
  24.8 0.0 collective-permute-done.2.rest_1_
  24.8 0.6 %first.1 = (bf16[528,1024]{1,0:T(8,128)(2,1)S(1)}, f32[512,128]{1,0:T(8,128)S(1)}, f32[8,256]{1,0:T(8,128)S(1)}) custom-call(bf16[2064,128]{1,0:T(8,128)(2,1)S(1)} %get-tuple-element.30.after.rest_0_, bf16[2192,128]{1,0:T(8,128)(2,1)S(1)} %get-tuple-element.28.rest_1_.rest_0_, bf16[2064,128]{1,0:T(8,128)(2,1)S(1)} %collective-permute-done.2.rest_1_), custom_call_target="tpu_custom_call" | custom-call | tf_op jit(solution)/shard_map/first/pallas_call | solution.py:471
  25.5 1.4 %collective-permute-start.3 = (bf16[528,1024]{1,0:T(8,128)(2,1)S(1)}, bf16[528,1024]{1,0:T(8,128)(2,1)S(1)}, u32[]{:S(2)}, u32[]{:S(2)}) collective-permute-start(bf16[528,1024]{1,0:T(8,128)(2,1)S(1)} %get-tuple-element.31.old_units), channel_id=1, source_target_pairs={{0,1},{2,3},{4,5},{6,7},{8,9},{10,11},{12,13},{14,15},{17,16},{19,... | collective-permute-start | bytes 3244040 | tf_op jit(solution)/shard_map/ppermute | solution.py:414
  26.8 10.9 %collective-permute-done.4.rest_1_ = bf16[2064,128]{1,0:T(8,128)(2,1)S(1)} collective-permute-done((bf16[2064,128]{1,0:T(8,128)(2,1)S(1)}, bf16[2064,128]{1,0:T(8,128)(2,1)S(1)}, u32[]{:S(2)}, u32[]{:S(2)}) %collective-permute-start.4) | collective-permute-done | bytes 528416 | tf_op jit(solution)/shard_map/ppermute | solution.py:414
  37.7 1.0 %second.1 = bf16[528,1024]{1,0:T(8,128)(2,1)S(1)} custom-call(bf16[528,1024]{1,0:T(8,128)(2,1)S(1)} %get-tuple-element.31.old_units, f32[512,128]{1,0:T(8,128)S(1)} %get-tuple-element.32.old_col, f32[8,256]{1,0:T(8,128)S(1)} %get-tuple-element.33.old_facts, bf16[2064,128]{1,0:T(8,128)(2,1)S(1)} %get-tuple-element.30.after.rest_0_, ...), custom_call_target="tpu_custom_call" | custom-call | tf_op jit(solution)/shard_map/second/pallas_call | solution.py:483
  38.7 1.4 %collective-permute-start.5 = (bf16[528,1024]{1,0:T(8,128)(2,1)S(1)}, bf16[528,1024]{1,0:T(8,128)(2,1)S(1)}, u32[]{:S(2)}, u32[]{:S(2)}) collective-permute-start(bf16[528,1024]{1,0:T(8,128)(2,1)S(1)} %second.1), channel_id=1, source_target_pairs={{0,1},{2,3},{4,5},{6,7},{8,9},{10,11},{12,13},{14,15},{17,16},{19,... | collective-permute-start | bytes 3244040 | tf_op jit(solution)/shard_map/ppermute | solution.py:414
  40.0 0.7 %collective-permute-start.6 = (bf16[2192,128]{1,0:T(8,128)(2,1)S(1)}, bf16[2192,128]{1,0:T(8,128)(2,1)S(1)}, u32[]{:S(2)}, u32[]{:S(2)}) collective-permute-start(bf16[2192,128]{1,0:T(8,128)(2,1)S(1)} %get-tuple-element.36), channel_id=1, source_target_pairs={{1,24},{3,26},{5,28},{7,30},{24,1},{26,3},{28,5},{30,7}} | collective-permute-start | bytes 1683464 | tf_op jit(solution)/shard_map/ppermute | solution.py:414
  40.7 0.7 %collective-permute-start.7 = (bf16[2064,128]{1,0:T(8,128)(2,1)S(1)}, bf16[2064,128]{1,0:T(8,128)(2,1)S(1)}, u32[]{:S(2)}, u32[]{:S(2)}) collective-permute-start(bf16[2064,128]{1,0:T(8,128)(2,1)S(1)} %get-tuple-element.34), channel_id=1, source_target_pairs={{1,28},{3,30},{5,24},{7,26},{24,5},{26,7},{28,1},{30,3},{9,13},{11... | collective-permute-start | bytes 1585160 | tf_op jit(solution)/shard_map/ppermute | solution.py:414
  41.4 0.7 %collective-permute-start.8 = (bf16[2064,128]{1,0:T(8,128)(2,1)S(1)}, bf16[2064,128]{1,0:T(8,128)(2,1)S(1)}, u32[]{:S(2)}, u32[]{:S(2)}) collective-permute-start(bf16[2064,128]{1,0:T(8,128)(2,1)S(1)} %get-tuple-element.44), channel_id=1, source_target_pairs={{1,16},{3,18},{5,20},{7,22},{24,9},{26,11},{28,13},{30,15},{9,1},{... | collective-permute-start | bytes 1585160 | tf_op jit(solution)/shard_map/ppermute | solution.py:414
  42.1 0.0 collective-permute-done.3.first_a
  42.2 0.7 %collective-permute-start.9 = (bf16[2064,128]{1,0:T(8,128)(2,1)S(1)}, bf16[2064,128]{1,0:T(8,128)(2,1)S(1)}, u32[]{:S(2)}, u32[]{:S(2)}) collective-permute-start(bf16[2064,128]{1,0:T(8,128)(2,1)S(1)} %get-tuple-element.46), channel_id=1, source_target_pairs={{1,20},{3,22},{5,16},{7,18},{24,13},{26,15},{28,9},{30,11},{9,5},{... | collective-permute-start | bytes 1585160 | tf_op jit(solution)/shard_map/ppermute | solution.py:414
  42.9 0.0 collective-permute-done.7.rest_2_
  42.9 0.0 collective-permute-done.6.rest_1_
  42.9 0.0 collective-permute-done.5.second_a
  42.9 2.2 %mid.1 = (bf16[512,1024]{1,0:T(8,128)(2,1)S(1)}, f32[512,128]{1,0:T(8,128)S(1)}, f32[8,256]{1,0:T(8,128)S(1)}, f32[8,512]{1,0:T(8,128)S(1)}, f32[512,128]{1,0:T(...) custom-call(bf16[528,1024]{1,0:T(8,128)(2,1)S(1)} %collective-permute-done.3.first_a, ...), custom_call_target="tpu_custom_call" | custom-call | tf_op jit(solution)/shard_map/mid/pallas_call | solution.py:506
  45.1 0.0 collective-permute-done.8.rest_0_
  45.1 0.0 collective-permute-done.9.rest_1_
  45.1 0.0 copy-start
  45.1 1.8 %late.1 = f32[128,128]{1,0:T(8,128)S(1)} custom-call(bf16[528,1024]{1,0:T(8,128)(2,1)S(1)} %collective-permute-done.3.first_a, bf16[528,1024]{1,0:T(8,128)(2,1)S(1)} %collective-permute-done.5.second_a, f32[512,128]{1,0:T(8,128)S(1)} %get-tuple-element.37.col_first, f32[512,128]{1,0:T(8,128)S(1)} %get-tuple-element.38.col_second, ...), custom_call_target="tpu_custom_call" | custom-call | tf_op jit(solution)/shard_map/late/pallas_call | solution.py:522
  46.9 12.0 %all_to_all.5 = f32[32,4,128]{2,1,0:T(4,128)S(1)} all-to-all(f32[32,4,128]{2,1,0:T(4,128)S(1)} %bitcast.4), channel_id=1, replica_groups=mesh['blk'=8,'grp'=4] {'blk','grp'}, dimensions={0} | all-to-all | bytes 131072 | tf_op jit(solution)/shard_map/all_to_all | solution.py:539
  58.9 0.0 copy-done
  58.9 0.8 %finish.1 = f32[1,512]{1,0:T(1,128)} custom-call(s32[1,512]{1,0:T(1,128)S(1)} %copy-done, f32[128,128]{1,0:T(8,128)S(1)} %bitcast.5), custom_call_target="tpu_custom_call" | custom-call | tf_op jit(solution)/shard_map/finish/pallas_call | solution.py:542
Async XLA Ops:
  0.0 19.0 %collective-permute-start.1 = (bf16[512,1024]{1,0:T(8,128)(2,1)}, bf16[512,1024]{1,0:T(8,128)(2,1)S(1)}, u32[]{:S(2)}, u32[]{:S(2)}) collective-permute-start(bf16[512,1024]{1,0:T(8,128)(2,1)} %bitcast.6), channel_id=1, source_target_pairs={{9,16},{11,18},{13,20},{15,22},{16,9},{18,11},{20,13},{22,15},{0,8... | collective-permute-start | bytes 3145736 | tf_op jit(solution)/shard_map/ppermute | solution.py:414
  8.4 16.4 %collective-permute-start.2 = (bf16[2064,128]{1,0:T(8,128)(2,1)S(1)}, bf16[2064,128]{1,0:T(8,128)(2,1)S(1)}, u32[]{:S(2)}, u32[]{:S(2)}) collective-permute-start(bf16[2064,128]{1,0:T(8,128)(2,1)S(1)} %get-tuple-element.29.rest_2_), channel_id=1, source_target_pairs={{0,4},{2,6},{4,0},{6,2},{8,12},{10,14},{12,8},{14,10},{17,21},{19,... | collective-permute-start | bytes 1585160 | tf_op jit(solution)/shard_map/ppermute | solution.py:414
  11.8 7.2 %collective-permute-start = (bf16[144,128]{1,0:T(8,128)(2,1)S(1)}, bf16[144,128]{1,0:T(8,128)(2,1)S(1)}, u32[]{:S(2)}, u32[]{:S(2)}) collective-permute-start(bf16[144,128]{1,0:T(8,128)(2,1)S(1)} %get-tuple-element.26), channel_id=1, source_target_pairs={{9,16},{11,18},{13,20},{15,22},{16,9},{18,11},{20,13},{22,15},{0,8... | collective-permute-start | bytes 110600 | tf_op jit(solution)/shard_map/ppermute | solution.py:414
  20.6 17.1 %collective-permute-start.4 = (bf16[2064,128]{1,0:T(8,128)(2,1)S(1)}, bf16[2064,128]{1,0:T(8,128)(2,1)S(1)}, u32[]{:S(2)}, u32[]{:S(2)}) collective-permute-start(bf16[2064,128]{1,0:T(8,128)(2,1)S(1)} %get-tuple-element.34), channel_id=1, source_target_pairs={{0,4},{2,6},{4,0},{6,2},{8,12},{10,14},{12,8},{14,10},{17,21},{19,... | collective-permute-start | bytes 1585160 | tf_op jit(solution)/shard_map/ppermute | solution.py:414
  25.5 16.7 %collective-permute-start.3 = (bf16[528,1024]{1,0:T(8,128)(2,1)S(1)}, bf16[528,1024]{1,0:T(8,128)(2,1)S(1)}, u32[]{:S(2)}, u32[]{:S(2)}) collective-permute-start(bf16[528,1024]{1,0:T(8,128)(2,1)S(1)} %get-tuple-element.31.old_units), channel_id=1, source_target_pairs={{0,1},{2,3},{4,5},{6,7},{8,9},{10,11},{12,13},{14,15},{17,16},{19,... | collective-permute-start | bytes 3244040 | tf_op jit(solution)/shard_map/ppermute | solution.py:414
  38.7 4.2 %collective-permute-start.5 = (bf16[528,1024]{1,0:T(8,128)(2,1)S(1)}, bf16[528,1024]{1,0:T(8,128)(2,1)S(1)}, u32[]{:S(2)}, u32[]{:S(2)}) collective-permute-start(bf16[528,1024]{1,0:T(8,128)(2,1)S(1)} %second.1), channel_id=1, source_target_pairs={{0,1},{2,3},{4,5},{6,7},{8,9},{10,11},{12,13},{14,15},{17,16},{19,... | collective-permute-start | bytes 3244040 | tf_op jit(solution)/shard_map/ppermute | solution.py:414
  40.0 2.8 %collective-permute-start.6 = (bf16[2192,128]{1,0:T(8,128)(2,1)S(1)}, bf16[2192,128]{1,0:T(8,128)(2,1)S(1)}, u32[]{:S(2)}, u32[]{:S(2)}) collective-permute-start(bf16[2192,128]{1,0:T(8,128)(2,1)S(1)} %get-tuple-element.36), channel_id=1, source_target_pairs={{1,24},{3,26},{5,28},{7,30},{24,1},{26,3},{28,5},{30,7}} | collective-permute-start | bytes 1683464 | tf_op jit(solution)/shard_map/ppermute | solution.py:414
  40.7 2.1 %collective-permute-start.7 = (bf16[2064,128]{1,0:T(8,128)(2,1)S(1)}, bf16[2064,128]{1,0:T(8,128)(2,1)S(1)}, u32[]{:S(2)}, u32[]{:S(2)}) collective-permute-start(bf16[2064,128]{1,0:T(8,128)(2,1)S(1)} %get-tuple-element.34), channel_id=1, source_target_pairs={{1,28},{3,30},{5,24},{7,26},{24,5},{26,7},{28,1},{30,3},{9,13},{11... | collective-permute-start | bytes 1585160 | tf_op jit(solution)/shard_map/ppermute | solution.py:414
  41.4 3.6 %collective-permute-start.8 = (bf16[2064,128]{1,0:T(8,128)(2,1)S(1)}, bf16[2064,128]{1,0:T(8,128)(2,1)S(1)}, u32[]{:S(2)}, u32[]{:S(2)}) collective-permute-start(bf16[2064,128]{1,0:T(8,128)(2,1)S(1)} %get-tuple-element.44), channel_id=1, source_target_pairs={{1,16},{3,18},{5,20},{7,22},{24,9},{26,11},{28,13},{30,15},{9,1},{... | collective-permute-start | bytes 1585160 | tf_op jit(solution)/shard_map/ppermute | solution.py:414
  42.2 2.9 %collective-permute-start.9 = (bf16[2064,128]{1,0:T(8,128)(2,1)S(1)}, bf16[2064,128]{1,0:T(8,128)(2,1)S(1)}, u32[]{:S(2)}, u32[]{:S(2)}) collective-permute-start(bf16[2064,128]{1,0:T(8,128)(2,1)S(1)} %get-tuple-element.46), channel_id=1, source_target_pairs={{1,20},{3,22},{5,16},{7,18},{24,13},{26,15},{28,9},{30,11},{9,5},{... | collective-permute-start | bytes 1585160 | tf_op jit(solution)/shard_map/ppermute | solution.py:414
  45.1 13.9 %copy-start = (s32[1,512]{1,0:T(1,128)S(1)}, s32[1,512]{1,0:T(1,128)}, u32[]{:S(2)}) copy-start(s32[1,512]{1,0:T(1,128)} %ids_ref.1) | copy-start | bytes 6148

commit v11 on v10

--- a/solution.py
+++ b/solution.py
@@ -327,8 +327,29 @@
     )
 
 
+def more_kernel(cap, first_a, second_a, col_first, col_second, facts_a, units_m, col_m, facts_m, cents, *rest):
+    blocks, (units, id_col, facts, facts_a_out, facts_m_out) = rest[:-5], rest[-5:]
+    size = first_a.shape[0] // 2 - cents.shape[0] // 4
+    old = [
+        (some, col, [facts_a[r : r + 1, i * size : (i + 1) * size] for r in range(2)])
+        for i, (some, col) in enumerate(((first_a, col_first), (second_a, col_second)))
+    ]
+    old.append((units_m, col_m, [facts_m[r : r + 1, :] for r in range(2)]))
+    ids = unpack(blocks, cap, cents.shape[0] // 2, units, id_col)
+    earlier, density, picked = join(old, units, id_col, ids, cents)
+    facts_a_out[...] = facts_a[...]
+    facts_m_out[...] = facts_m[...]
+    for r, row in enumerate(ids):
+        facts[r : r + 1, :] = density[r]
+        facts[2 + r : 3 + r, :] = row
+        facts[4 + r : 5 + r, :] = picked[r]
+        facts_a_out[r : r + 1, :size] = earlier[0][r]
+        facts_a_out[r : r + 1, size:] = earlier[1][r]
+        facts_m_out[r : r + 1, :] = earlier[2][r]
+
+
 def late_kernel(
-    order, cap, groups, first_a, second_a, col_first, col_second, facts_a, units_m, col_m, facts_m, cents, *rest
+    order, cap, groups, first_a, second_a, col_first, col_second, facts_a, units_m, col_m, facts_m, units_q, col_q, facts_q, cents, *rest
 ):
     blocks, (out_ref, units, id_col) = rest[:-3], rest[-3:]
     strata_dev = cents.shape[0] // 2
@@ -342,6 +363,7 @@
         for i, (some, col) in enumerate(((first_a, col_first), (second_a, col_second)))
     ]
     old.append((units_m, col_m, [facts_m[r : r + 1, :] for r in range(2)]))
+    old.append((units_q, col_q, [facts_q[r : r + 1, :] for r in range(2)]))
     earlier, density, picked_new = join(old, units, id_col, ids, cents)
     total = jnp.zeros((1, 1), jnp.float32)
     weights = []
@@ -353,6 +375,7 @@
                 jnp.concatenate([earlier[0][r], earlier[1][r]], axis=1),
             ),
             (facts_m[2 + r : 3 + r, :], facts_m[4 + r : 5 + r, :], earlier[2][r]),
+            (facts_q[2 + r : 3 + r, :], facts_q[4 + r : 5 + r, :], earlier[3][r]),
             (row, picked_new[r], density[r]),
         ]
         row, picked, dense = [jnp.concatenate(parts, axis=1) for parts in zip(*states)]
@@ -519,6 +542,23 @@
         compiler_params=params(20),
         name="mid",
     )(first_a, second_a, extra, out[0], *first)
+    final = LANES // cap
+    some = side - final
+    known = (first_a, second_a, col_first, col_second)
+    units_q, col_q, facts_q, facts_a, facts_m = pl.pallas_call(
+        functools.partial(more_kernel, cap),
+        out_shape=[
+            shape(2 * some * cap, width),
+            shape(2 * some * cap, LANES, dtype=jnp.float32),
+            shape(8, some * cap, dtype=jnp.float32),
+            shape(8, each, dtype=jnp.float32),
+            shape(8, size, dtype=jnp.float32),
+        ],
+        in_specs=[VMEM] * (9 + some),
+        out_specs=[VMEM] * 5,
+        compiler_params=params(20),
+        name="more",
+    )(*known, facts_a, units_m, col_m, facts_m, cents, *last[:some])
     sent = pl.pallas_call(
         functools.partial(
             late_kernel,
@@ -527,15 +567,15 @@
             groups,
         ),
         out_shape=jax.ShapeDtypeStruct((shards * groups * 4, LANES), jnp.float32),
-        in_specs=[VMEM] * (9 + side),
+        in_specs=[VMEM] * (12 + final),
         out_specs=VMEM,
         scratch_shapes=[
-            pltpu.VMEM((2 * side * cap, width), jnp.bfloat16),
-            pltpu.VMEM((2 * side * cap, LANES), jnp.float32),
+            pltpu.VMEM((2 * final * cap, width), jnp.bfloat16),
+            pltpu.VMEM((2 * final * cap, LANES), jnp.float32),
         ],
         compiler_params=params(20),
         name="late",
-    )(first_a, second_a, col_first, col_second, facts_a, units_m, col_m, facts_m, cents, *last)
+    )(*known, facts_a, units_m, col_m, facts_m, units_q, col_q, facts_q, cents, *last[some:])
     got = lax.all_to_all(
         sent.reshape(shards * groups, 4, LANES), AXES, 0, 0, tiled=True
     ).reshape(shards * groups * 4, LANES)

time: 60.2 us -> 59.9 us (level)
  blocking collectives: 12 us -> 10.8 us
  Pallas kernels: 11.4 us -> 12.4 us
    all_to_all x1, blocking collectives: 12 us -> 10.8 us  [body(): lax.all_to_all(sent.reshape(shards * groups, 4, LANES), AXES, 0, 0, tiled...]
    pallas_call x0 -> x1, Pallas kernels: none -> 1.29 us  [body(): pl.pallas_call(functools.partial(more_kernel, cap), out_shape=[shape(2 *...]
  transfers between devices with their start and end apart: 10 -> 10, of which waited for: 2 -> 2; matrix products, arithmetic and copies ran while one was open for 0% -> 0% of each run, Pallas kernels for 15% -> 17%
where the time goes in v11:
time: 59.9 us; the launch traced here: 59.5 us
  starting transfers between devices  20.4 us (34%)
  waiting for transfers between devices  15.7 us (26%)
  Pallas kernels  12.4 us (21%)
  blocking collectives  10.8 us (18%)
    ppermute x10, starting transfers between devices, send(): lax.ppermute(array, AXES, [(b * groups + g, to_b * groups + to_g) for (b,...  20.4 us
    ppermute x10, waiting for transfers between devices, send(): lax.ppermute(array, AXES, [(b * groups + g, to_b * groups + to_g) for (b,...  15.7 us
    all_to_all x1, blocking collectives, body(): lax.all_to_all(sent.reshape(shards * groups, 4, LANES), AXES, 0, 0, tiled...  10.8 us
    pallas_call x1, Pallas kernels, body(): pl.pallas_call(functools.partial(near_kernel, chips, cap), out_shape=[sha...  3.46 us
    pallas_call x1, Pallas kernels, body(): pl.pallas_call(functools.partial(mid_kernel, chips, cap), out_shape=[shap...  2.16 us
    pallas_call x1, Pallas kernels, body(): pl.pallas_call(functools.partial(far_kernel, chips, cap, strata_dev), out...  1.6 us
    pallas_call x1, Pallas kernels, body(): pl.pallas_call(functools.partial(late_kernel, [*range(chips), *(flip + e...  1.53 us
    pallas_call x1, Pallas kernels, body(): pl.pallas_call(functools.partial(more_kernel, cap), out_shape=[shape(2 *...  1.29 us
  transfers between devices with their start and end apart: 10, of which 2 were waited for; matrix products, arithmetic and copies ran while one was open for 0% of the time, Pallas kernels for 17%

profile of v11, /device:TPU:0, one launch (start us, length us, event | category | flops | bytes accessed | tf_op | source)
XLA Modules:
  0.0 59.5 jit_solution(4185620150717165358)
XLA Ops:
  0.0 4.9 %collective-permute-start.1 = (bf16[512,1024]{1,0:T(8,128)(2,1)}, bf16[512,1024]{1,0:T(8,128)(2,1)S(1)}, u32[]{:S(2)}, u32[]{:S(2)}) collective-permute-start(bf16[512,1024]{1,0:T(8,128)(2,1)} %bitcast.6), channel_id=1, source_target_pairs={{9,16},{11,18},{13,20},{15,22},{16,9},{18,11},{20,13},{22,15},{0,8... | collective-permute-start | bytes 3145736 | tf_op jit(solution)/shard_map/ppermute | solution.py:437
  4.9 3.5 %near.1 = (bf16[2192,128]{1,0:T(8,128)(2,1)S(1)}, bf16[2064,128]{1,0:T(8,128)(2,1)S(1)}, bf16[2192,128]{1,0:T(8,128)(2,1)S(1)}, bf16[2064,128]{1,0:T(8,128)(2,1)S(1)}, bf16[144,128]{1,0:T(8,128)(2,1)S(1)}) custom-call(s32[1,512]{1,0:T(1,128)} %ids_ref.1, bf16[16,1024]{1,0:T(8,128)(2,1)} %bitcast.8, bf16[512,1024]{1,0:T(8,128)(2,1)} %bitcast.7), custom_call_target="tpu_custom_call" | custom-call | tf_op jit(solution)/shard_map/near/pallas_call | solution.py:448
  8.4 3.4 %collective-permute-start.2 = (bf16[2064,128]{1,0:T(8,128)(2,1)S(1)}, bf16[2064,128]{1,0:T(8,128)(2,1)S(1)}, u32[]{:S(2)}, u32[]{:S(2)}) collective-permute-start(bf16[2064,128]{1,0:T(8,128)(2,1)S(1)} %get-tuple-element.34.rest_2_), channel_id=1, source_target_pairs={{0,4},{2,6},{4,0},{6,2},{8,12},{10,14},{12,8},{14,10},{17,21},{19,... | collective-permute-start | bytes 1585160 | tf_op jit(solution)/shard_map/ppermute | solution.py:437
  11.8 2.4 %collective-permute-start = (bf16[144,128]{1,0:T(8,128)(2,1)S(1)}, bf16[144,128]{1,0:T(8,128)(2,1)S(1)}, u32[]{:S(2)}, u32[]{:S(2)}) collective-permute-start(bf16[144,128]{1,0:T(8,128)(2,1)S(1)} %get-tuple-element.31), channel_id=1, source_target_pairs={{9,16},{11,18},{13,20},{15,22},{16,9},{18,11},{20,13},{22,15},{0,8... | collective-permute-start | bytes 110600 | tf_op jit(solution)/shard_map/ppermute | solution.py:437
  14.2 4.8 %collective-permute-done.extra = bf16[144,128]{1,0:T(8,128)(2,1)S(1)} collective-permute-done((bf16[144,128]{1,0:T(8,128)(2,1)S(1)}, bf16[144,128]{1,0:T(8,128)(2,1)S(1)}, u32[]{:S(2)}, u32[]{:S(2)}) %collective-permute-start) | collective-permute-done | bytes 36896 | tf_op jit(solution)/shard_map/ppermute | solution.py:437
  19.0 0.0 collective-permute-done.1.rows_ref
  19.0 1.6 %far.1 = (bf16[2064,128]{1,0:T(8,128)(2,1)S(1)}, bf16[2064,128]{1,0:T(8,128)(2,1)S(1)}, bf16[2064,128]{1,0:T(8,128)(2,1)S(1)}, bf16[2064,128]{1,0:T(8,128)(2,1)S(1)}) custom-call(bf16[144,128]{1,0:T(8,128)(2,1)S(1)} %collective-permute-done.extra, bf16[512,1024]{1,0:T(8,128)(2,1)S(1)} %collective-permute-done.1.rows_ref, ...), custom_call_target="tpu_custom_call" | custom-call | tf_op jit(solution)/shard_map/far/pallas_call | solution.py:471
  20.6 4.2 %collective-permute-start.4 = (bf16[2064,128]{1,0:T(8,128)(2,1)S(1)}, bf16[2064,128]{1,0:T(8,128)(2,1)S(1)}, u32[]{:S(2)}, u32[]{:S(2)}) collective-permute-start(bf16[2064,128]{1,0:T(8,128)(2,1)S(1)} %get-tuple-element.39), channel_id=1, source_target_pairs={{0,4},{2,6},{4,0},{6,2},{8,12},{10,14},{12,8},{14,10},{17,21},{19,... | collective-permute-start | bytes 1585160 | tf_op jit(solution)/shard_map/ppermute | solution.py:437
  24.8 0.0 collective-permute-done.2.rest_1_
  24.8 0.6 %first.1 = (bf16[528,1024]{1,0:T(8,128)(2,1)S(1)}, f32[512,128]{1,0:T(8,128)S(1)}, f32[8,256]{1,0:T(8,128)S(1)}) custom-call(bf16[2064,128]{1,0:T(8,128)(2,1)S(1)} %get-tuple-element.35.after.rest_0_, bf16[2192,128]{1,0:T(8,128)(2,1)S(1)} %get-tuple-element.33.rest_1_.rest_0_, bf16[2064,128]{1,0:T(8,128)(2,1)S(1)} %collective-permute-done.2.rest_1_), custom_call_target="tpu_custom_call" | custom-call | tf_op jit(solution)/shard_map/first/pallas_call | solution.py:494
  25.5 1.4 %collective-permute-start.3 = (bf16[528,1024]{1,0:T(8,128)(2,1)S(1)}, bf16[528,1024]{1,0:T(8,128)(2,1)S(1)}, u32[]{:S(2)}, u32[]{:S(2)}) collective-permute-start(bf16[528,1024]{1,0:T(8,128)(2,1)S(1)} %get-tuple-element.36.old_units), channel_id=1, source_target_pairs={{0,1},{2,3},{4,5},{6,7},{8,9},{10,11},{12,13},{14,15},{17,16},{19,... | collective-permute-start | bytes 3244040 | tf_op jit(solution)/shard_map/ppermute | solution.py:437
  26.8 10.9 %collective-permute-done.4.rest_1_ = bf16[2064,128]{1,0:T(8,128)(2,1)S(1)} collective-permute-done((bf16[2064,128]{1,0:T(8,128)(2,1)S(1)}, bf16[2064,128]{1,0:T(8,128)(2,1)S(1)}, u32[]{:S(2)}, u32[]{:S(2)}) %collective-permute-start.4) | collective-permute-done | bytes 528416 | tf_op jit(solution)/shard_map/ppermute | solution.py:437
  37.7 1.0 %second.1 = bf16[528,1024]{1,0:T(8,128)(2,1)S(1)} custom-call(bf16[528,1024]{1,0:T(8,128)(2,1)S(1)} %get-tuple-element.36.old_units, f32[512,128]{1,0:T(8,128)S(1)} %get-tuple-element.37.old_col, f32[8,256]{1,0:T(8,128)S(1)} %get-tuple-element.38.old_facts, bf16[2064,128]{1,0:T(8,128)(2,1)S(1)} %get-tuple-element.35.after.rest_0_, ...), custom_call_target="tpu_custom_call" | custom-call | tf_op jit(solution)/shard_map/second/pallas_call | solution.py:506
  38.7 1.4 %collective-permute-start.5 = (bf16[528,1024]{1,0:T(8,128)(2,1)S(1)}, bf16[528,1024]{1,0:T(8,128)(2,1)S(1)}, u32[]{:S(2)}, u32[]{:S(2)}) collective-permute-start(bf16[528,1024]{1,0:T(8,128)(2,1)S(1)} %second.1), channel_id=1, source_target_pairs={{0,1},{2,3},{4,5},{6,7},{8,9},{10,11},{12,13},{14,15},{17,16},{19,... | collective-permute-start | bytes 3244040 | tf_op jit(solution)/shard_map/ppermute | solution.py:437
  40.0 0.7 %collective-permute-start.6 = (bf16[2192,128]{1,0:T(8,128)(2,1)S(1)}, bf16[2192,128]{1,0:T(8,128)(2,1)S(1)}, u32[]{:S(2)}, u32[]{:S(2)}) collective-permute-start(bf16[2192,128]{1,0:T(8,128)(2,1)S(1)} %get-tuple-element.41), channel_id=1, source_target_pairs={{1,24},{3,26},{5,28},{7,30},{24,1},{26,3},{28,5},{30,7}} | collective-permute-start | bytes 1683464 | tf_op jit(solution)/shard_map/ppermute | solution.py:437
  40.7 0.7 %collective-permute-start.7 = (bf16[2064,128]{1,0:T(8,128)(2,1)S(1)}, bf16[2064,128]{1,0:T(8,128)(2,1)S(1)}, u32[]{:S(2)}, u32[]{:S(2)}) collective-permute-start(bf16[2064,128]{1,0:T(8,128)(2,1)S(1)} %get-tuple-element.39), channel_id=1, source_target_pairs={{1,28},{3,30},{5,24},{7,26},{24,5},{26,7},{28,1},{30,3},{9,13},{11... | collective-permute-start | bytes 1585160 | tf_op jit(solution)/shard_map/ppermute | solution.py:437
  41.4 0.7 %collective-permute-start.8 = (bf16[2064,128]{1,0:T(8,128)(2,1)S(1)}, bf16[2064,128]{1,0:T(8,128)(2,1)S(1)}, u32[]{:S(2)}, u32[]{:S(2)}) collective-permute-start(bf16[2064,128]{1,0:T(8,128)(2,1)S(1)} %get-tuple-element.49), channel_id=1, source_target_pairs={{1,16},{3,18},{5,20},{7,22},{24,9},{26,11},{28,13},{30,15},{9,1},{... | collective-permute-start | bytes 1585160 | tf_op jit(solution)/shard_map/ppermute | solution.py:437
  42.1 0.0 collective-permute-done.3.first_a
  42.2 0.7 %collective-permute-start.9 = (bf16[2064,128]{1,0:T(8,128)(2,1)S(1)}, bf16[2064,128]{1,0:T(8,128)(2,1)S(1)}, u32[]{:S(2)}, u32[]{:S(2)}) collective-permute-start(bf16[2064,128]{1,0:T(8,128)(2,1)S(1)} %get-tuple-element.56), channel_id=1, source_target_pairs={{1,20},{3,22},{5,16},{7,18},{24,13},{26,15},{28,9},{30,11},{9,5},{... | collective-permute-start | bytes 1585160 | tf_op jit(solution)/shard_map/ppermute | solution.py:437
  42.9 0.0 collective-permute-done.7.rest_2_
  42.9 0.0 collective-permute-done.6.rest_1_
  42.9 0.0 collective-permute-done.5.second_a
  42.9 2.2 %mid.1 = (bf16[512,1024]{1,0:T(8,128)(2,1)S(1)}, f32[512,128]{1,0:T(8,128)S(1)}, f32[8,256]{1,0:T(8,128)S(1)}, f32[8,512]{1,0:T(8,128)S(1)}, f32[512,128]{1,0:T(...) custom-call(bf16[528,1024]{1,0:T(8,128)(2,1)S(1)} %collective-permute-done.3.first_a, ...), custom_call_target="tpu_custom_call" | custom-call | tf_op jit(solution)/shard_map/mid/pallas_call | solution.py:529
  45.1 0.0 collective-permute-done.8.rest_0_
  45.1 1.3 %more.1 = (bf16[256,1024]{1,0:T(8,128)(2,1)S(1)}, f32[256,128]{1,0:T(8,128)S(1)}, f32[8,128]{1,0:T(8,128)S(1)}, f32[8,512]{1,0:T(8,128)S(1)}, f32[8,256]{1,0:T(8,128)S(1)}) custom-call(bf16[528,1024]{1,0:T(8,128)(2,1)S(1)} %collective-permute-done.3.first_a, bf16[528,1024]{1,0:T(8,128)(2,1)S(1)} %collective-permute-done.5.second_a, ...), custom_call_target="tpu_custom_call" | custom-call | tf_op jit(solution)/shard_map/more/pallas_call | solution.py:548
  46.4 0.0 collective-permute-done.9.rest_0_
  46.4 0.0 copy-start
  46.4 1.5 %late.1 = f32[128,128]{1,0:T(8,128)S(1)} custom-call(bf16[528,1024]{1,0:T(8,128)(2,1)S(1)} %collective-permute-done.3.first_a, bf16[528,1024]{1,0:T(8,128)(2,1)S(1)} %collective-permute-done.5.second_a, f32[512,128]{1,0:T(8,128)S(1)} %get-tuple-element.42.col_first, f32[512,128]{1,0:T(8,128)S(1)} %get-tuple-element.43.col_second, ...), custom_call_target="tpu_custom_call" | custom-call | tf_op jit(solution)/shard_map/late/pallas_call | solution.py:562
  47.9 10.8 %all_to_all.5 = f32[32,4,128]{2,1,0:T(4,128)S(1)} all-to-all(f32[32,4,128]{2,1,0:T(4,128)S(1)} %bitcast.5), channel_id=1, replica_groups=mesh['blk'=8,'grp'=4] {'blk','grp'}, dimensions={0} | all-to-all | bytes 131072 | tf_op jit(solution)/shard_map/all_to_all | solution.py:579
  58.7 0.0 copy-done
  58.7 0.8 %finish.1 = f32[1,512]{1,0:T(1,128)} custom-call(s32[1,512]{1,0:T(1,128)S(1)} %copy-done, f32[128,128]{1,0:T(8,128)S(1)} %bitcast.4), custom_call_target="tpu_custom_call" | custom-call | tf_op jit(solution)/shard_map/finish/pallas_call | solution.py:582
Async XLA Ops:
  0.0 19.0 %collective-permute-start.1 = (bf16[512,1024]{1,0:T(8,128)(2,1)}, bf16[512,1024]{1,0:T(8,128)(2,1)S(1)}, u32[]{:S(2)}, u32[]{:S(2)}) collective-permute-start(bf16[512,1024]{1,0:T(8,128)(2,1)} %bitcast.6), channel_id=1, source_target_pairs={{9,16},{11,18},{13,20},{15,22},{16,9},{18,11},{20,13},{22,15},{0,8... | collective-permute-start | bytes 3145736 | tf_op jit(solution)/shard_map/ppermute | solution.py:437
  8.4 16.4 %collective-permute-start.2 = (bf16[2064,128]{1,0:T(8,128)(2,1)S(1)}, bf16[2064,128]{1,0:T(8,128)(2,1)S(1)}, u32[]{:S(2)}, u32[]{:S(2)}) collective-permute-start(bf16[2064,128]{1,0:T(8,128)(2,1)S(1)} %get-tuple-element.34.rest_2_), channel_id=1, source_target_pairs={{0,4},{2,6},{4,0},{6,2},{8,12},{10,14},{12,8},{14,10},{17,21},{19,... | collective-permute-start | bytes 1585160 | tf_op jit(solution)/shard_map/ppermute | solution.py:437
  11.8 7.2 %collective-permute-start = (bf16[144,128]{1,0:T(8,128)(2,1)S(1)}, bf16[144,128]{1,0:T(8,128)(2,1)S(1)}, u32[]{:S(2)}, u32[]{:S(2)}) collective-permute-start(bf16[144,128]{1,0:T(8,128)(2,1)S(1)} %get-tuple-element.31), channel_id=1, source_target_pairs={{9,16},{11,18},{13,20},{15,22},{16,9},{18,11},{20,13},{22,15},{0,8... | collective-permute-start | bytes 110600 | tf_op jit(solution)/shard_map/ppermute | solution.py:437
  20.6 17.1 %collective-permute-start.4 = (bf16[2064,128]{1,0:T(8,128)(2,1)S(1)}, bf16[2064,128]{1,0:T(8,128)(2,1)S(1)}, u32[]{:S(2)}, u32[]{:S(2)}) collective-permute-start(bf16[2064,128]{1,0:T(8,128)(2,1)S(1)} %get-tuple-element.39), channel_id=1, source_target_pairs={{0,4},{2,6},{4,0},{6,2},{8,12},{10,14},{12,8},{14,10},{17,21},{19,... | collective-permute-start | bytes 1585160 | tf_op jit(solution)/shard_map/ppermute | solution.py:437
  25.5 16.7 %collective-permute-start.3 = (bf16[528,1024]{1,0:T(8,128)(2,1)S(1)}, bf16[528,1024]{1,0:T(8,128)(2,1)S(1)}, u32[]{:S(2)}, u32[]{:S(2)}) collective-permute-start(bf16[528,1024]{1,0:T(8,128)(2,1)S(1)} %get-tuple-element.36.old_units), channel_id=1, source_target_pairs={{0,1},{2,3},{4,5},{6,7},{8,9},{10,11},{12,13},{14,15},{17,16},{19,... | collective-permute-start | bytes 3244040 | tf_op jit(solution)/shard_map/ppermute | solution.py:437
  38.7 4.2 %collective-permute-start.5 = (bf16[528,1024]{1,0:T(8,128)(2,1)S(1)}, bf16[528,1024]{1,0:T(8,128)(2,1)S(1)}, u32[]{:S(2)}, u32[]{:S(2)}) collective-permute-start(bf16[528,1024]{1,0:T(8,128)(2,1)S(1)} %second.1), channel_id=1, source_target_pairs={{0,1},{2,3},{4,5},{6,7},{8,9},{10,11},{12,13},{14,15},{17,16},{19,... | collective-permute-start | bytes 3244040 | tf_op jit(solution)/shard_map/ppermute | solution.py:437
  40.0 2.8 %collective-permute-start.6 = (bf16[2192,128]{1,0:T(8,128)(2,1)S(1)}, bf16[2192,128]{1,0:T(8,128)(2,1)S(1)}, u32[]{:S(2)}, u32[]{:S(2)}) collective-permute-start(bf16[2192,128]{1,0:T(8,128)(2,1)S(1)} %get-tuple-element.41), channel_id=1, source_target_pairs={{1,24},{3,26},{5,28},{7,30},{24,1},{26,3},{28,5},{30,7}} | collective-permute-start | bytes 1683464 | tf_op jit(solution)/shard_map/ppermute | solution.py:437
  40.7 2.1 %collective-permute-start.7 = (bf16[2064,128]{1,0:T(8,128)(2,1)S(1)}, bf16[2064,128]{1,0:T(8,128)(2,1)S(1)}, u32[]{:S(2)}, u32[]{:S(2)}) collective-permute-start(bf16[2064,128]{1,0:T(8,128)(2,1)S(1)} %get-tuple-element.39), channel_id=1, source_target_pairs={{1,28},{3,30},{5,24},{7,26},{24,5},{26,7},{28,1},{30,3},{9,13},{11... | collective-permute-start | bytes 1585160 | tf_op jit(solution)/shard_map/ppermute | solution.py:437
  41.4 3.6 %collective-permute-start.8 = (bf16[2064,128]{1,0:T(8,128)(2,1)S(1)}, bf16[2064,128]{1,0:T(8,128)(2,1)S(1)}, u32[]{:S(2)}, u32[]{:S(2)}) collective-permute-start(bf16[2064,128]{1,0:T(8,128)(2,1)S(1)} %get-tuple-element.49), channel_id=1, source_target_pairs={{1,16},{3,18},{5,20},{7,22},{24,9},{26,11},{28,13},{30,15},{9,1},{... | collective-permute-start | bytes 1585160 | tf_op jit(solution)/shard_map/ppermute | solution.py:437
  42.2 4.2 %collective-permute-start.9 = (bf16[2064,128]{1,0:T(8,128)(2,1)S(1)}, bf16[2064,128]{1,0:T(8,128)(2,1)S(1)}, u32[]{:S(2)}, u32[]{:S(2)}) collective-permute-start(bf16[2064,128]{1,0:T(8,128)(2,1)S(1)} %get-tuple-element.56), channel_id=1, source_target_pairs={{1,20},{3,22},{5,16},{7,18},{24,13},{26,15},{28,9},{30,11},{9,5},{... | collective-permute-start | bytes 1585160 | tf_op jit(solution)/shard_map/ppermute | solution.py:437
  46.4 12.3 %copy-start = (s32[1,512]{1,0:T(1,128)S(1)}, s32[1,512]{1,0:T(1,128)}, u32[]{:S(2)}) copy-start(s32[1,512]{1,0:T(1,128)} %ids_ref.1) | copy-start | bytes 6148
